TPU v7x, 32 devices: a whole 2x2x4 slice. The times are simulated.
32 devices in a mesh: dp: 8 (over y, x, core), fsdp: 4 (over z).
Axes of the slice: x: 2, y: 2, z: 4, core: 2. Of those that a mesh axis runs over, the one named last changes fastest.
Arguments:
- inputs: bfloat16 [32, 512, 1024], P(('dp', 'fsdp')), may hold values from -6 to 6
- segment_ids: int32 [32, 512], P(('dp', 'fsdp')), may hold values from 0 to 6, as said below
- query_weight: bfloat16 [1024, 1024], P(('dp', 'fsdp')), may hold values from -0.1875 to 0.1875
- key_weight: bfloat16 [1024, 1024], P(('dp', 'fsdp')), may hold values from -0.1875 to 0.1875
- value_weight: bfloat16 [1024, 1024], P(('dp', 'fsdp')), may hold values from -0.1875 to 0.1875
- output_weight: bfloat16 [1024, 1024], P(('dp', 'fsdp')), may hold values from -1 to 1
- query_bias: bfloat16 [1024], P(('dp', 'fsdp')), may hold values from -3 to 3
- value_bias: bfloat16 [1024], P(('dp', 'fsdp')), may hold values from -3 to 3
- output_bias: bfloat16 [1024], P(('dp', 'fsdp')), may hold values from -3 to 3
- attn_gain: bfloat16 [1024], P(('dp', 'fsdp')), may hold values from 0.5 to 1.5
- attn_shift: bfloat16 [1024], P(('dp', 'fsdp')), may hold values from -2 to 2
- inner_weight: bfloat16 [1024, 4096], P(('dp', 'fsdp')), may hold values from -0.1875 to 0.1875
- inner_bias: bfloat16 [4096], P(('dp', 'fsdp')), may hold values from -3 to 3
- outer_weight: bfloat16 [4096, 1024], P(('dp', 'fsdp')), may hold values from -0.125 to 0.125
- outer_bias: bfloat16 [1024], P(('dp', 'fsdp')), may hold values from -3 to 3
- ffn_gain: bfloat16 [1024], P(('dp', 'fsdp')), may hold values from 0.5 to 1.5
- ffn_shift: bfloat16 [1024], P(('dp', 'fsdp')), may hold values from -2 to 2
- out_grad: bfloat16 [32, 512, 1024], P(('dp', 'fsdp')), may hold values from -6 to 6
Outputs:
- outputs: bfloat16 [32, 512, 1024], P(('dp', 'fsdp'))
- input_grad: float32 [32, 512, 1024], P(('dp', 'fsdp'))
- grad_query_weight: float32 [1024, 1024], P(('dp', 'fsdp'))
- grad_key_weight: float32 [1024, 1024], P(('dp', 'fsdp'))
- grad_value_weight: float32 [1024, 1024], P(('dp', 'fsdp'))
- grad_output_weight: float32 [1024, 1024], P(('dp', 'fsdp'))
- grad_query_bias: float32 [1024], P(('dp', 'fsdp'))
- grad_value_bias: float32 [1024], P(('dp', 'fsdp'))
- grad_output_bias: float32 [1024], P(('dp', 'fsdp'))
- grad_attn_gain: float32 [1024], P(('dp', 'fsdp'))
- grad_attn_shift: float32 [1024], P(('dp', 'fsdp'))
- grad_inner_weight: float32 [1024, 4096], P(('dp', 'fsdp'))
- grad_inner_bias: float32 [4096], P(('dp', 'fsdp'))
- grad_outer_weight: float32 [4096, 1024], P(('dp', 'fsdp'))
- grad_outer_bias: float32 [1024], P(('dp', 'fsdp'))
- grad_ffn_gain: float32 [1024], P(('dp', 'fsdp'))
- grad_ffn_shift: float32 [1024], P(('dp', 'fsdp'))
Inputs may be any that keep to these rules, and one draw needn't show every extreme that they name: `segment_ids`: in each row the document numbers start at 1, never fall and rise by one at each new document, up to 6 documents; padding (0) is a tail of at most 128 positions.
All inputs are finite; a program needn't handle non-finite values.
Results may differ from a plain program's by a relative error of at most 0.014.
Values may be sent and summed in bfloat16 or wider, within the bound.
No kernel may reach another device: no remote copies, remote signals or barrier semaphores. Data moves between devices by JAX's collectives and lax.ppermute only.
A program may use at most 256 MiB of HBM per device.

v0:
```python
import jax
import jax.numpy as jnp
from jax import lax
from jax.sharding import PartitionSpec as P

H = 16
HD = 64


EPSILON = 1e-05


def scaled_norm(rows_in, gain):
    row_mean = jnp.mean(rows_in, axis=-1, keepdims=True)
    centred = rows_in - row_mean
    spread = jnp.mean(centred * centred, axis=-1, keepdims=True)
    return centred * lax.rsqrt(spread + EPSILON) * gain


def gelu_exact(value_in):
    return jax.nn.gelu(value_in, approximate=False)


def to_groups(matrix, row_count, seq_len):
    groups = H // 4
    shaped = matrix.reshape(row_count, seq_len, groups, 4, HD).transpose(0, 2, 1, 3, 4)
    return shaped.reshape(row_count * groups, seq_len, 4, HD)


def from_groups(stacked, row_count, seq_len):
    groups = stacked.shape[0] // row_count
    shaped = stacked.reshape(row_count, groups, seq_len, 4, HD).transpose(0, 2, 1, 3, 4)
    return shaped.reshape(row_count * seq_len, groups * 4 * HD)


def masked_scores(query_block, key_block, seg_row):
    score_scale = HD ** (-0.5)
    scores = (
        jnp.einsum("qhd,khd->hqk", query_block, key_block, preferred_element_type=jnp.float32)
        * score_scale
    )
    same_doc = seg_row[:, None] == seg_row[None, :]
    return jnp.where(same_doc[None], scores, -1e30)


def attend_forward(item_set):
    query_block, key_block, value_block, seg_row = item_set
    scores = masked_scores(query_block, key_block, seg_row)
    row_max = jnp.max(scores, axis=-1, keepdims=True)
    raised = jnp.exp(scores - row_max)
    row_total = jnp.sum(raised, axis=-1, keepdims=True)
    prob_low = (raised / row_total).astype(jnp.bfloat16)
    mixed_block = jnp.einsum(
        "hqk,khd->qhd", prob_low, value_block, preferred_element_type=jnp.float32
    )
    return (mixed_block, (row_max + jnp.log(row_total))[..., 0])


def attend_backward(item_set):
    query_block, key_block, value_block, seg_row, mixed_grad, log_total = item_set
    score_scale = HD ** (-0.5)
    scores = masked_scores(query_block, key_block, seg_row)
    probabilities = jnp.exp(scores - log_total[..., None])
    prob_low = probabilities.astype(jnp.bfloat16)
    value_grad = jnp.einsum(
        "hqk,qhd->khd", prob_low, mixed_grad, preferred_element_type=jnp.float32
    )
    prob_grad = jnp.einsum(
        "qhd,khd->hqk", mixed_grad, value_block, preferred_element_type=jnp.float32
    )
    inner_sum = jnp.sum(probabilities * prob_grad, axis=-1, keepdims=True)
    score_grad = (probabilities * (prob_grad - inner_sum)).astype(jnp.bfloat16)
    query_grad = (
        jnp.einsum("hqk,khd->qhd", score_grad, key_block, preferred_element_type=jnp.float32)
        * score_scale
    )
    key_grad = (
        jnp.einsum("hqk,qhd->khd", score_grad, query_block, preferred_element_type=jnp.float32)
        * score_scale
    )
    return (query_grad, key_grad, value_grad)


def matmul(left, right):
    return jnp.dot(left, right, preferred_element_type=jnp.float32)


def column_sum(matrix):
    return jnp.sum(matrix.astype(jnp.float32), axis=0)


def shards(
    inputs,
    segment_ids,
    query_weight,
    key_weight,
    value_weight,
    output_weight,
    query_bias,
    value_bias,
    output_bias,
    attn_gain,
    attn_shift,
    inner_weight,
    inner_bias,
    outer_weight,
    outer_bias,
    ffn_gain,
    ffn_shift,
    out_grad,
):
    row_count, seq_len, model_width = inputs.shape
    tokens_here = row_count * seq_len
    flattened = inputs.reshape(tokens_here, model_width)
    (
        query_full,
        key_full,
        value_full,
        output_full,
        query_bias_full,
        value_bias_full,
        output_bias_full,
        attn_gain_full,
        attn_shift_full,
    ) = (
        lax.all_gather(query_weight, ("dp", "fsdp"), axis=0, tiled=True),
        lax.all_gather(key_weight, ("dp", "fsdp"), axis=0, tiled=True),
        lax.all_gather(value_weight, ("dp", "fsdp"), axis=0, tiled=True),
        lax.all_gather(output_weight, ("dp", "fsdp"), axis=0, tiled=True),
        lax.all_gather(query_bias, ("dp", "fsdp"), axis=0, tiled=True),
        lax.all_gather(value_bias, ("dp", "fsdp"), axis=0, tiled=True),
        lax.all_gather(output_bias, ("dp", "fsdp"), axis=0, tiled=True),
        lax.all_gather(attn_gain, ("dp", "fsdp"), axis=0, tiled=True),
        lax.all_gather(attn_shift, ("dp", "fsdp"), axis=0, tiled=True),
    )
    queries = (matmul(flattened, query_full) + query_bias_full.astype(jnp.float32)).astype(
        jnp.bfloat16
    )
    key_rows = matmul(flattened, key_full).astype(jnp.bfloat16)
    value_rows = (matmul(flattened, value_full) + value_bias_full.astype(jnp.float32)).astype(
        jnp.bfloat16
    )
    query_groups = to_groups(queries, row_count, seq_len)
    key_groups = to_groups(key_rows, row_count, seq_len)
    value_groups = to_groups(value_rows, row_count, seq_len)
    seg_repeat = jnp.repeat(segment_ids, H // 4, axis=0)
    group_mixed, log_totals = lax.map(
        attend_forward, (query_groups, key_groups, value_groups, seg_repeat)
    )
    mixed_low = from_groups(group_mixed, row_count, seq_len).astype(jnp.bfloat16)
    attn_branch = matmul(mixed_low, output_full) + output_bias_full.astype(jnp.float32)
    attn_sum = flattened.astype(jnp.float32) + attn_branch
    attn_normed = scaled_norm(
        attn_sum, attn_gain_full.astype(jnp.float32)
    ) + attn_shift_full.astype(jnp.float32)
    normed_low = attn_normed.astype(jnp.bfloat16)
    inner_full, inner_bias_full, outer_full, outer_bias_full, ffn_gain_full, ffn_shift_full = (
        lax.all_gather(inner_weight, ("dp", "fsdp"), axis=0, tiled=True),
        lax.all_gather(inner_bias, ("dp", "fsdp"), axis=0, tiled=True),
        lax.all_gather(outer_weight, ("dp", "fsdp"), axis=0, tiled=True),
        lax.all_gather(outer_bias, ("dp", "fsdp"), axis=0, tiled=True),
        lax.all_gather(ffn_gain, ("dp", "fsdp"), axis=0, tiled=True),
        lax.all_gather(ffn_shift, ("dp", "fsdp"), axis=0, tiled=True),
    )
    inner_pre = matmul(normed_low, inner_full) + inner_bias_full.astype(jnp.float32)
    act_low = gelu_exact(inner_pre).astype(jnp.bfloat16)
    ffn_branch = matmul(act_low, outer_full) + outer_bias_full.astype(jnp.float32)
    ffn_sum = attn_normed + ffn_branch
    outputs = (
        scaled_norm(ffn_sum, ffn_gain_full.astype(jnp.float32)) + ffn_shift_full.astype(jnp.float32)
    ).astype(jnp.bfloat16)
    inner_back, outer_back, ffn_gain_back = (
        lax.all_gather(inner_weight, ("dp", "fsdp"), axis=0, tiled=True),
        lax.all_gather(outer_weight, ("dp", "fsdp"), axis=0, tiled=True),
        lax.all_gather(ffn_gain, ("dp", "fsdp"), axis=0, tiled=True),
    )
    grad_out = out_grad.reshape(tokens_here, model_width).astype(jnp.float32)
    _, ffn_norm_pull = jax.vjp(scaled_norm, ffn_sum, ffn_gain_back.astype(jnp.float32))
    grad_ffn_sum, grad_ffn_gain = ffn_norm_pull(grad_out)
    grad_ffn_shift = jnp.sum(grad_out, axis=0)
    branch_grad = grad_ffn_sum.astype(jnp.bfloat16)
    grad_outer_bias = column_sum(branch_grad)
    grad_outer = jnp.einsum("nf,nd->fd", act_low, branch_grad, preferred_element_type=jnp.float32)
    grad_act = jnp.einsum("nd,fd->nf", branch_grad, outer_back, preferred_element_type=jnp.float32)
    _, gelu_pull = jax.vjp(gelu_exact, inner_pre)
    inner_grad = gelu_pull(grad_act)[0].astype(jnp.bfloat16)
    grad_inner_bias = column_sum(inner_grad)
    grad_inner = jnp.einsum("nd,nf->df", normed_low, inner_grad, preferred_element_type=jnp.float32)
    grad_normed = grad_ffn_sum + jnp.einsum(
        "nf,df->nd", inner_grad, inner_back, preferred_element_type=jnp.float32
    )
    ffn_terms = (
        grad_inner,
        grad_inner_bias,
        grad_outer,
        grad_outer_bias,
        grad_ffn_gain,
        grad_ffn_shift,
    )
    ffn_owned = (
        lax.psum_scatter(ffn_terms[0], ("dp", "fsdp"), scatter_dimension=0, tiled=True),
        lax.psum_scatter(ffn_terms[1], ("dp", "fsdp"), scatter_dimension=0, tiled=True),
        lax.psum_scatter(ffn_terms[2], ("dp", "fsdp"), scatter_dimension=0, tiled=True),
        lax.psum_scatter(ffn_terms[3], ("dp", "fsdp"), scatter_dimension=0, tiled=True),
        lax.psum_scatter(ffn_terms[4], ("dp", "fsdp"), scatter_dimension=0, tiled=True),
        lax.psum_scatter(ffn_terms[5], ("dp", "fsdp"), scatter_dimension=0, tiled=True),
    )
    (
        shard_inner,
        shard_inner_bias,
        shard_outer,
        shard_outer_bias,
        shard_ffn_gain,
        shard_ffn_shift,
    ) = ffn_owned
    query_back, key_back, value_back, output_back, attn_gain_back = (
        lax.all_gather(query_weight, ("dp", "fsdp"), axis=0, tiled=True),
        lax.all_gather(key_weight, ("dp", "fsdp"), axis=0, tiled=True),
        lax.all_gather(value_weight, ("dp", "fsdp"), axis=0, tiled=True),
        lax.all_gather(output_weight, ("dp", "fsdp"), axis=0, tiled=True),
        lax.all_gather(attn_gain, ("dp", "fsdp"), axis=0, tiled=True),
    )
    _, attn_norm_pull = jax.vjp(scaled_norm, attn_sum, attn_gain_back.astype(jnp.float32))
    grad_attn_sum, grad_attn_gain = attn_norm_pull(grad_normed)
    grad_attn_shift = jnp.sum(grad_normed, axis=0)
    attn_grad = grad_attn_sum.astype(jnp.bfloat16)
    grad_output_bias = column_sum(attn_grad)
    grad_output = jnp.einsum("nd,ne->de", mixed_low, attn_grad, preferred_element_type=jnp.float32)
    mixed_grad = jnp.einsum(
        "ne,de->nd", attn_grad, output_back, preferred_element_type=jnp.float32
    ).astype(jnp.bfloat16)
    group_qgrad, group_kgrad, group_vgrad = lax.map(
        attend_backward,
        (
            query_groups,
            key_groups,
            value_groups,
            seg_repeat,
            to_groups(mixed_grad, row_count, seq_len),
            log_totals,
        ),
    )
    query_grad = from_groups(group_qgrad, row_count, seq_len).astype(jnp.bfloat16)
    key_grad = from_groups(group_kgrad, row_count, seq_len).astype(jnp.bfloat16)
    value_grad = from_groups(group_vgrad, row_count, seq_len).astype(jnp.bfloat16)
    grad_query_bias = column_sum(query_grad)
    grad_value_bias = column_sum(value_grad)
    grad_query = jnp.einsum("nd,ne->de", flattened, query_grad, preferred_element_type=jnp.float32)
    grad_key = jnp.einsum("nd,ne->de", flattened, key_grad, preferred_element_type=jnp.float32)
    grad_value = jnp.einsum("nd,ne->de", flattened, value_grad, preferred_element_type=jnp.float32)
    input_grad = (
        grad_attn_sum
        + jnp.einsum("ne,de->nd", query_grad, query_back, preferred_element_type=jnp.float32)
        + jnp.einsum("ne,de->nd", key_grad, key_back, preferred_element_type=jnp.float32)
        + jnp.einsum("ne,de->nd", value_grad, value_back, preferred_element_type=jnp.float32)
    )
    attn_owned = (
        lax.psum_scatter(grad_query, ("dp", "fsdp"), scatter_dimension=0, tiled=True),
        lax.psum_scatter(grad_key, ("dp", "fsdp"), scatter_dimension=0, tiled=True),
        lax.psum_scatter(grad_value, ("dp", "fsdp"), scatter_dimension=0, tiled=True),
        lax.psum_scatter(grad_output, ("dp", "fsdp"), scatter_dimension=0, tiled=True),
        lax.psum_scatter(grad_query_bias, ("dp", "fsdp"), scatter_dimension=0, tiled=True),
        lax.psum_scatter(grad_value_bias, ("dp", "fsdp"), scatter_dimension=0, tiled=True),
        lax.psum_scatter(grad_output_bias, ("dp", "fsdp"), scatter_dimension=0, tiled=True),
        lax.psum_scatter(grad_attn_gain, ("dp", "fsdp"), scatter_dimension=0, tiled=True),
        lax.psum_scatter(grad_attn_shift, ("dp", "fsdp"), scatter_dimension=0, tiled=True),
    )
    (
        shard_query,
        shard_key,
        shard_value,
        shard_output,
        shard_query_bias,
        shard_value_bias,
        shard_output_bias,
        shard_attn_gain,
        shard_attn_shift,
    ) = attn_owned
    return (
        outputs.reshape(row_count, seq_len, model_width),
        input_grad.reshape(row_count, seq_len, model_width),
        shard_query,
        shard_key,
        shard_value,
        shard_output,
        shard_query_bias,
        shard_value_bias,
        shard_output_bias,
        shard_attn_gain,
        shard_attn_shift,
        shard_inner,
        shard_inner_bias,
        shard_outer,
        shard_outer_bias,
        shard_ffn_gain,
        shard_ffn_shift,
    )


def solution(mesh):
    placed = (
        P(("dp", "fsdp"), None, None),
        P(("dp", "fsdp"), None),
        P(("dp", "fsdp"), None),
        P(("dp", "fsdp"), None),
        P(("dp", "fsdp"), None),
        P(("dp", "fsdp"), None),
        P(("dp", "fsdp")),
        P(("dp", "fsdp")),
        P(("dp", "fsdp")),
        P(("dp", "fsdp")),
        P(("dp", "fsdp")),
        P(("dp", "fsdp"), None),
        P(("dp", "fsdp")),
        P(("dp", "fsdp"), None),
        P(("dp", "fsdp")),
        P(("dp", "fsdp")),
        P(("dp", "fsdp")),
        P(("dp", "fsdp"), None, None),
    )
    return jax.shard_map(
        shards,
        mesh=mesh,
        in_specs=placed,
        out_specs=(
            P(("dp", "fsdp"), None, None),
            P(("dp", "fsdp"), None, None),
            P(("dp", "fsdp"), None),
            P(("dp", "fsdp"), None),
            P(("dp", "fsdp"), None),
            P(("dp", "fsdp"), None),
            P(("dp", "fsdp")),
            P(("dp", "fsdp")),
            P(("dp", "fsdp")),
            P(("dp", "fsdp")),
            P(("dp", "fsdp")),
            P(("dp", "fsdp"), None),
            P(("dp", "fsdp")),
            P(("dp", "fsdp"), None),
            P(("dp", "fsdp")),
            P(("dp", "fsdp")),
            P(("dp", "fsdp")),
        ),
        check_vma=False,
    )
```

profile of v0, /device:TPU:0, one launch (start us, length us, event | category | flops | bytes accessed | tf_op | source)
XLA Modules:
  0.0 1826.3 jit_solution(2462448369746053519)
XLA Ops:
  17.9 42.3 %all-reduce.18 = (bf16[1024]{0:T(1024)(128)(2,1)S(1)}, bf16[1024]{0:T(1024)(128)(2,1)S(1)}, bf16[1024]{0:T(1024)(128)(2,1)S(1)}, bf16[1024]{0:T(1024)(128)(2,1)S...) all-reduce(bf16[1024]{0:T(1024)(128)(2,1)S(1)} %dynamic-update-slic, ...), channel_id=1, replica_groups=mesh['dp'=8,'fsdp'=4] {'dp','fsdp'}, use_global_device_ids=true, to_apply=%add | all-reduce | flops 8192 | bytes 32768
  60.3 65.7 %all-gather = bf16[32,1,128]{2,1,0:T(2,128)(2,1)S(1)} all-gather(bf16[1,1,128]{2,1,0:T(2,128)(2,1)} %bitcast.239), channel_id=1, replica_groups=mesh['dp'=8,'fsdp'=4] {'dp','fsdp'}, dimensions={0}, use_global_device_ids=true | all-gather | bytes 8448 | tf_op jit(solution)/shard_map/all_gather | solution.py:159
  126.0 3.2 add_convert_fusion.3
  129.8 3.2 add_convert_fusion.2
  133.6 53.3 %all-gather.12.cloned.1.call-done = bf16[1024,1024]{1,0:T(8,128)(2,1)} async-done(((bf16[32,1024]{1,0:T(8,128)(2,1)}), bf16[1024,1024]{1,0:T(8,128)(2,1)}) %all-gather.12.cloned.1.call-update) | async-done | bytes 2097168 | tf_op jit(solution)/shard_map/all_gather | solution.py:127
  186.9 4.1 convolution_convert_fusion.1
  193.7 16.7 while.26
  210.4 34.8 %all-gather.14.cloned.1.call-done = bf16[1024,1024]{1,0:T(8,128)(2,1)} async-done(((bf16[32,1024]{1,0:T(8,128)(2,1)}), bf16[1024,1024]{1,0:T(8,128)(2,1)}) %all-gather.14.cloned.1.call-update) | async-done | bytes 2097168 | tf_op jit(solution)/shard_map/all_gather | solution.py:129
  245.1 3.5 fusion.82
  250.3 73.9 %all-gather.16.cloned.1.call-done = bf16[1024,4096]{1,0:T(8,128)(2,1)} async-done(((bf16[32,4096]{1,0:T(8,128)(2,1)}), bf16[1024,4096]{1,0:T(8,128)(2,1)}) %all-gather.16.cloned.1.call-update) | async-done | bytes 8388624 | tf_op jit(solution)/shard_map/all_gather | solution.py:158
  324.2 28.4 %multiply_convert_fusion.1 = (bf16[512,4096]{1,0:T(8,128)(2,1)}, f32[512,4096]{1,0:T(8,128)}, f32[512,4096]{1,0:T(8,128)}) fusion(f32[4096]{0:T(1024)S(1)} %bitcast.236, bf16[1024,4096]{1,0:T(8,128)(2,1)} %all-gather.16.cloned.1.call-done, f32[512,1024]{1,0:T(8,128)} %copy-done, f32[1024]{0:T(1024)S(1)} %convert_element_type.165, ...), kind=kOutput, calls=%fused_computation.66 | convolution fusion | flops 4436000768 | bytes 31485952 | tf_op jit(solution)/shard_map/dot_general | solution.py:85
  352.6 50.4 %all-gather.18.cloned.1.call-done = bf16[4096,1024]{1,0:T(8,128)(2,1)} async-done(((bf16[128,1024]{1,0:T(8,128)(2,1)}), bf16[4096,1024]{1,0:T(8,128)(2,1)}) %all-gather.18.cloned.1.call-update) | async-done | bytes 8388624 | tf_op jit(solution)/shard_map/all_gather | solution.py:160
  403.0 10.0 fusion.83
  416.4 15.3 convert_reduce_fusion
  431.7 8.9 multiply_reduce_fusion.1
  448.8 34.3 %while.27 = (s32[]{:T(128)}, bf16[4,512,4,64]{1,3,2,0:T(8,128)(2,1)}, bf16[4,512,4,64]{1,3,2,0:T(8,128)(2,1)}, bf16[4,512,4,64]{1,3,2,0:T(8,128)(2,1)S(1)}, bf16...) while((s32[]{:T(128)}, ...), condition=%wide.region_14.15_spmd, body=%wide.region_12.14_spmd.sunk | while | flops 687339520 | bytes 56954112 | solution.py:232
  483.1 4.7 convolution_bitcast_fusion.2
  487.8 5.3 copy.72
  494.7 3.2 convolution_bitcast_fusion.1
  497.9 5.4 copy.74
  503.3 3.2 convolution_bitcast_fusion
  506.5 5.4 copy.76
  513.2 4.4 fusion.86
  519.2 10.7 fusion.75
  531.1 10.4 fusion.87
  543.6 40.6 %all-reduce.17 = (f32[1024]{0:T(1024)S(1)}, f32[1024]{0:T(1024)S(1)}, f32[1024]{0:T(1024)S(1)}, f32[1024]{0:T(1024)S(1)}, f32[1024]{0:T(1024)S(1)}, /*index=5*/f...) all-reduce(f32[1024]{0:T(1024)S(1)} %reduce_sum.191, ...), channel_id=6, replica_groups=mesh['dp'=8,'fsdp'=4] {'dp','fsdp'}, use_global_device_ids=true, to_apply=%region_20.21.clone | all-reduce | flops 12288 | bytes 98304
  597.7 42.3 %reduce-scatter.19.cloned.1.call-done = f32[32,1024]{1,0:T(8,128)} async-done(((f32[1024,1024]{1,0:T(8,128)}), f32[32,1024]{1,0:T(8,128)}) %reduce-scatter.19.cloned.1.call-update) | async-done | bytes 131088
  639.9 149.3 %reduce-scatter.21.cloned.1.call-done = f32[32,1024]{1,0:T(8,128)} async-done(((f32[1024,1024]{1,0:T(8,128)}), f32[32,1024]{1,0:T(8,128)}) %reduce-scatter.21.cloned.1.call-update) | async-done | bytes 131088
  789.3 150.1 %reduce-scatter.23.cloned.1.call-done = f32[32,1024]{1,0:T(8,128)} async-done(((f32[1024,1024]{1,0:T(8,128)}), f32[32,1024]{1,0:T(8,128)}) %reduce-scatter.23.cloned.1.call-update) | async-done | bytes 131088
  939.3 149.1 %reduce-scatter.13.cloned.1.call-done = f32[32,1024]{1,0:T(8,128)} async-done(((f32[1024,1024]{1,0:T(8,128)}), f32[32,1024]{1,0:T(8,128)}) %reduce-scatter.13.cloned.1.call-update) | async-done | bytes 131088 | tf_op jit(solution)/shard_map/reduce_scatter | solution.py:261
  1088.5 365.7 %reduce-scatter.15.cloned.1.call-done = f32[32,4096]{1,0:T(8,128)} async-done(((f32[1024,4096]{1,0:T(8,128)}), f32[32,4096]{1,0:T(8,128)}) %reduce-scatter.15.cloned.1.call-update) | async-done | bytes 524304 | tf_op jit(solution)/shard_map/reduce_scatter | solution.py:201
  1454.1 364.9 %reduce-scatter.17.cloned.1.call-done = f32[128,1024]{1,0:T(8,128)} async-done(((f32[4096,1024]{1,0:T(8,128)}), f32[128,1024]{1,0:T(8,128)}) %reduce-scatter.17.cloned.1.call-update) | async-done | bytes 524304 | tf_op jit(solution)/shard_map/reduce_scatter | solution.py:203
  (233 shorter events, 98.7 us)
Async XLA Ops:
  7.2 118.9 %all-gather.8.cloned.1.call-start = ((), (), s32[]{:S(2)}) async-start(), calls=%async_computation.6 | async-start | bytes 2162688 | tf_op jit(solution)/shard_map/all_gather | solution.py:128
  7.9 121.9 %all-gather.10.cloned.1.call-start = ((), (), s32[]{:S(2)}) async-start(), calls=%async_computation.7 | async-start | bytes 2162688 | tf_op jit(solution)/shard_map/all_gather | solution.py:126
  8.7 178.3 %all-gather.12.cloned.1.call-start = ((), (), s32[]{:S(2)}) async-start(), calls=%async_computation.8 | async-start | bytes 2162688 | tf_op jit(solution)/shard_map/all_gather | solution.py:127
  9.4 235.7 %all-gather.14.cloned.1.call-start = ((), (), s32[]{:S(2)}) async-start(), calls=%async_computation.9 | async-start | bytes 2162688 | tf_op jit(solution)/shard_map/all_gather | solution.py:129
  10.0 314.2 %all-gather.16.cloned.1.call-start = ((), (), s32[]{:S(2)}) async-start(), calls=%async_computation.10 | async-start | bytes 8650752 | tf_op jit(solution)/shard_map/all_gather | solution.py:158
  10.6 392.4 %all-gather.18.cloned.1.call-start = ((), (), s32[]{:S(2)}) async-start(), calls=%async_computation.11 | async-start | bytes 8650752 | tf_op jit(solution)/shard_map/all_gather | solution.py:160
  11.1 628.8 %reduce-scatter.19.cloned.1.call-start = ((), (), s32[]{:S(2)}) async-start(), calls=%async_computation.15 | async-start | bytes 4325376
  133.6 59.0 %copy-start.23 = (s32[1,512]{1,0:T(1,128)S(1)}, s32[1,512]{1,0:T(1,128)}, u32[]{:S(2)}) copy-start(s32[1,512]{1,0:T(1,128)} %param.23) | copy-start | bytes 6148
  210.4 40.0 %copy-start.7 = (bf16[4,512,4,64]{1,3,2,0:T(8,128)(2,1)}, bf16[4,512,4,64]{1,3,2,0:T(8,128)(2,1)S(1)}, u32[]{:S(2)}) copy-start(bf16[4,512,4,64]{1,3,2,0:T(8,128)(2,1)S(1)} %get-tuple-element.439) | copy-start | bytes 3145732
  403.0 10.3 copy-start.5
  416.3 15.4 copy-start.14
  416.4 15.3 copy-start.1
  440.6 3.2 copy-start.12
  452.7 2.1 copy-start.9
  461.3 2.1 copy-start.9
  463.3 1.5 copy-start.19
  469.8 2.1 copy-start.9
  471.8 1.5 copy-start.19
  478.3 2.1 copy-start.9
  480.3 1.5 copy-start.19
  493.2 1.5 copy-start.22
  493.2 296.1 %reduce-scatter.21.cloned.1.call-start = ((), (), s32[]{:S(2)}) async-start(), calls=%async_computation.16 | async-start | bytes 4325376
  503.3 436.1 %reduce-scatter.23.cloned.1.call-start = ((), (), s32[]{:S(2)}) async-start(), calls=%async_computation.17 | async-start | bytes 4325376
  512.0 576.5 %reduce-scatter.13.cloned.1.call-start = ((), (), s32[]{:S(2)}) async-start(), calls=%async_computation.12 | async-start | bytes 4325376 | tf_op jit(solution)/shard_map/reduce_scatter | solution.py:261
  517.6 1.6 copy-start.2
  517.6 936.5 %reduce-scatter.15.cloned.1.call-start = ((), (), s32[]{:S(2)}) async-start(), calls=%async_computation.13 | async-start | bytes 17301504 | tf_op jit(solution)/shard_map/reduce_scatter | solution.py:201
  529.9 1289.1 %reduce-scatter.17.cloned.1.call-start = ((), (), s32[]{:S(2)}) async-start(), calls=%async_computation.14 | async-start | bytes 17301504 | tf_op jit(solution)/shard_map/reduce_scatter | solution.py:203
  541.5 1.5 copy-start.11
  589.5 3.1 copy-start.21
  589.5 3.1 copy-start.24
  592.6 1.6 copy-start.4
  592.6 2.2 copy-start.13
  (20 other events, 24.2 us)
Sparse Core Ops, SparseCore 0:
  10.9 59.3 all-gather.7
  73.2 55.3 all-gather.9
  131.6 55.3 all-gather.11
  189.7 55.3 all-gather.13
  247.9 76.2 all-gather.15
  327.0 75.9 all-gather.17
  493.3 146.5 reduce-scatter.18
  642.8 146.4 reduce-scatter.20
  792.1 147.1 reduce-scatter.22
  942.0 146.3 reduce-scatter.12
  1091.3 362.7 reduce-scatter.14
  1456.9 362.1 reduce-scatter.16
where the time goes:
time: 1840 us; the launch traced here: 1830 us
  waiting for transfers between devices  1440 us (78%)
  matrix products  157 us (9%)
  blocking collectives  149 us (8%)
  local copies, waits for them, and re-layouts  51.7 us (3%)
    reduce_scatter x1, waiting for transfers between devices, shards(): lax.psum_scatter(ffn_terms[0], ('dp', 'fsdp'), scatter_dimension=0, tiled...  366 us
    reduce_scatter x1, waiting for transfers between devices, shards(): lax.psum_scatter(ffn_terms[2], ('dp', 'fsdp'), scatter_dimension=0, tiled...  365 us
    unnamed x15, waiting for transfers between devices  345 us
    reduce_scatter x1, waiting for transfers between devices, shards(): lax.psum_scatter(grad_output, ('dp', 'fsdp'), scatter_dimension=0, tiled=...  149 us
    unnamed x2, blocking collectives  83 us
    all_gather x1, waiting for transfers between devices, shards(): lax.all_gather(inner_weight, ('dp', 'fsdp'), axis=0, tiled=True)  73.9 us
    all_gather x1, blocking collectives, shards(): lax.all_gather(inner_bias, ('dp', 'fsdp'), axis=0, tiled=True)  65.7 us
    all_gather x1, waiting for transfers between devices, shards(): lax.all_gather(key_weight, ('dp', 'fsdp'), axis=0, tiled=True)  53.3 us
  transfers between devices with their start and end apart: 12, of which 10 were waited for; matrix products, arithmetic and copies ran while one was open for 7% of the time, Pallas kernels for 0%

commit v1 on v0

--- a/solution.py
+++ b/solution.py
@@ -1,6 +1,10 @@
+import functools
+
 import jax
 import jax.numpy as jnp
 from jax import lax
+from jax.experimental import pallas as pl
+from jax.experimental.pallas import tpu as pltpu
 from jax.sharding import PartitionSpec as P
 
 H = 16
@@ -89,7 +93,173 @@
     return jnp.sum(matrix.astype(jnp.float32), axis=0)
 
 
+AXES = ("dp", "fsdp")
+BF = jnp.bfloat16
+F32 = jnp.float32
+
+
+class Slice:
+    def __init__(self, dp, inner):
+        self.inner, self.chips, self.count = inner, dp // 2, dp * inner
+
+    def swap(self, value, mask):
+        pairs = [(i, i ^ mask) for i in range(self.count)]
+        return lax.ppermute(value, AXES, pairs)
+
+    def across_core(self, value):
+        return self.swap(value, self.inner)
+
+    def across_chip(self, value, hop):
+        return self.swap(value, hop * 2 * self.inner)
+
+    def place(self):
+        me = lax.axis_index(AXES)
+        z = me % self.inner
+        core = (me // self.inner) % 2
+        return me, jnp.stack([me // (2 * self.inner), core, z]).astype(jnp.int32)
+
+
+def gather_pieces(net, shard):
+    along_z = jnp.stack([shard] + [net.swap(shard, s) for s in range(1, net.inner)])
+    pieces = [(along_z, 0, 0, 0)]
+    if net.chips == 4:
+        half = net.inner // 2
+        first, second = net.across_chip(along_z, 1), net.across_chip(along_z, 2)
+        low = net.across_chip(first[:half], 2)
+        high = net.across_chip(second[half:], 1)
+        pieces += [(first, 1, 0, 0), (second, 2, 0, 0), (low, 3, 0, 0), (high, 3, 0, half)]
+    else:
+        pieces += [(net.across_chip(along_z, j), j, 0, 0) for j in range(1, net.chips)]
+    return pieces + [(net.across_core(p), j, 1, s) for p, j, _, s in pieces]
+
+
+def assemble(net, pieces, ids, me, parts, tile):
+    rows = pieces[0][0].shape[1]
+    total = net.count * rows
+    if rows % 16:
+        hops = []
+        for _, j, c, s in pieces:
+            hops.append((j * 2 + c) * net.inner + s)
+        order = {}
+        start = 0
+        for (p, j, c, s), hop in zip(pieces, hops):
+            for i in range(p.shape[0]):
+                order[hop + i] = start + i
+            start += p.shape[0]
+        stacked = jnp.concatenate([p for p, _, _, _ in pieces], axis=0)
+        stacked = jnp.stack([stacked[order[i]] for i in range(net.count)])
+        whole = jnp.take(stacked, jnp.arange(net.count) ^ me, axis=0)
+        whole = whole.reshape(total, -1)
+        return [whole[:, a : a + w] for a, w in parts]
+    first = [a // tile for a, _ in parts]
+    count = [w // tile for _, w in parts]
+    steps = sum(count)
+    base = [sum(count[:i]) for i in range(len(parts))]
+    start = first[0]
+    meta = [(p.shape[0], j, c, s) for p, j, c, s in pieces]
+
+    def body(ids_ref, *refs):
+        sources, sinks = refs[: len(meta)], refs[len(meta) :]
+        step = pl.program_id(0)
+        for sink, lo, n in zip(sinks, base, count):
+
+            @pl.when((step >= lo) & (step < lo + n))
+            def _():
+                for source, (depth, j, c, s) in zip(sources, meta):
+                    block = ((ids_ref[0] ^ j) * 2 + (ids_ref[1] ^ c)) * net.inner
+                    for i in range(depth):
+                        row = (block + (ids_ref[2] ^ (s + i))) * rows
+                        sink[pl.ds(pl.multiple_of(row, rows), rows), :] = source[i]
+
+    return pl.pallas_call(
+        body,
+        out_shape=[jax.ShapeDtypeStruct((total, w), BF) for _, w in parts],
+        grid_spec=pltpu.PrefetchScalarGridSpec(
+            num_scalar_prefetch=1,
+            grid=(steps,),
+            in_specs=[
+                pl.BlockSpec((depth, rows, tile), lambda n, ids: (0, 0, start + n))
+                for depth, _, _, _ in meta
+            ],
+            out_specs=[
+                pl.BlockSpec(
+                    (total, tile),
+                    lambda n, ids, lo=lo, c=c: (0, jnp.clip(n - lo, 0, c - 1)),
+                )
+                for lo, c in zip(base, count)
+            ],
+        ),
+        name="assemble",
+    )(ids, *[p for p, _, _, _ in pieces])
+
+
+def column_blocks(net, left, ids, order, core):
+    width = left.shape[1] // (net.chips * 2)
+    picked = []
+    for j in order:
+        at = ((ids[0] ^ j) * 2 + (ids[1] ^ core)) * width
+        picked.append(lax.dynamic_slice_in_dim(left, at, width, axis=1))
+    return picked[0] if len(picked) == 1 else jnp.concatenate(picked, axis=1)
+
+
+def outer_dot(left, right):
+    return jnp.einsum("tm,tn->mn", left, right, preferred_element_type=F32)
+
+
+def hop_orders(net, backwards):
+    bits = [1 << b for b in range(net.chips.bit_length() - 1)]
+    return bits[::-1] if backwards else bits
+
+
+def reduce_rows(net, left, right, ids, backwards):
+    bits = hop_orders(net, backwards)
+    held = list(range(net.chips))
+    order = [0]
+    for b in bits[::-1]:
+        order = order + [j ^ b for j in order]
+    width = left.shape[1] // (net.chips * 2)
+    sent = outer_dot(column_blocks(net, left, ids, order, 1), right).astype(BF)
+    got = net.across_core(sent)
+    half = len(order) // 2
+    if half == 0:
+        keep = outer_dot(column_blocks(net, left, ids, order, 0), right) + got.astype(F32)
+    else:
+        away = (
+            outer_dot(column_blocks(net, left, ids, order[half:], 0), right)
+            + got[half * width :].astype(F32)
+        ).astype(BF)
+        arrived = net.across_chip(away, bits[0])
+        keep = (
+            outer_dot(column_blocks(net, left, ids, order[:half], 0), right)
+            + got[: half * width].astype(F32)
+        ).astype(BF)
+        keep = keep.astype(F32) + arrived.astype(F32)
+        for b in bits[1:]:
+            half //= 2
+            away = keep[half * width :].astype(BF)
+            arrived = net.across_chip(away, b)
+            keep = keep[: half * width].astype(BF).astype(F32) + arrived.astype(F32)
+    blocks = keep.reshape(net.inner, width // net.inner, -1)
+    total = lax.dynamic_index_in_dim(blocks, ids[2], axis=0, keepdims=False)
+    for s in range(1, net.inner):
+        piece = lax.dynamic_index_in_dim(blocks, ids[2] ^ s, axis=0, keepdims=False)
+        total = total + net.swap(piece.astype(BF), s).astype(F32)
+    return total
+
+
+def reduce_vectors(net, vectors):
+    packed = jnp.concatenate([v.reshape(net.count, -1) for v in vectors], axis=1)
+    summed = jnp.sum(lax.all_to_all(packed, AXES, 0, 0, tiled=True), axis=0)
+    out, at = [], 0
+    for v in vectors:
+        n = v.shape[0] // net.count
+        out.append(summed[at : at + n])
+        at += n
+    return out
+
+
 def shards(
+    net,
     inputs,
     segment_ids,
     query_weight,
@@ -112,26 +282,46 @@
     row_count, seq_len, model_width = inputs.shape
     tokens_here = row_count * seq_len
     flattened = inputs.reshape(tokens_here, model_width)
+    me, ids = net.place()
+    own_rows = query_weight.shape[0]
+    small = [query_bias, value_bias, output_bias, attn_gain, attn_shift, outer_bias, ffn_gain, ffn_shift]
+    small = jnp.concatenate([jnp.stack(small, axis=1), inner_bias.reshape(own_rows, -1)], axis=1)
+    spare = 128 - small.shape[1]
+    small = jnp.pad(small, ((0, 0), (0, spare)))
+    first = gather_pieces(
+        net, jnp.concatenate([query_weight, key_weight, value_weight, small], axis=1)
+    )
+    second = gather_pieces(net, jnp.concatenate([output_weight, inner_weight], axis=1))
+    third = gather_pieces(net, outer_weight)
+    width = query_weight.shape[1]
+    wide = inner_weight.shape[1]
+    query_full, key_full, value_full = assemble(
+        net, first, ids, me, [(0, width), (width, width), (2 * width, width)], width
+    )
+    (small_full,) = assemble(net, first, ids, me, [(3 * width, 128)], 128)
+    lanes = small_full[:, :8].astype(jnp.float32).T
     (
-        query_full,
-        key_full,
-        value_full,
-        output_full,
         query_bias_full,
         value_bias_full,
         output_bias_full,
         attn_gain_full,
         attn_shift_full,
-    ) = (
-        lax.all_gather(query_weight, ("dp", "fsdp"), axis=0, tiled=True),
-        lax.all_gather(key_weight, ("dp", "fsdp"), axis=0, tiled=True),
-        lax.all_gather(value_weight, ("dp", "fsdp"), axis=0, tiled=True),
-        lax.all_gather(output_weight, ("dp", "fsdp"), axis=0, tiled=True),
-        lax.all_gather(query_bias, ("dp", "fsdp"), axis=0, tiled=True),
-        lax.all_gather(value_bias, ("dp", "fsdp"), axis=0, tiled=True),
-        lax.all_gather(output_bias, ("dp", "fsdp"), axis=0, tiled=True),
-        lax.all_gather(attn_gain, ("dp", "fsdp"), axis=0, tiled=True),
-        lax.all_gather(attn_shift, ("dp", "fsdp"), axis=0, tiled=True),
+        outer_bias_full,
+        ffn_gain_full,
+        ffn_shift_full,
+    ) = [lanes[i] for i in range(8)]
+    inner_bias_full = small_full[:, 8 : 8 + wide // width].astype(jnp.float32).reshape(-1)
+    output_full, inner_full = assemble(
+        net, second, ids, me, [(0, width), (width, wide)], width
+    )
+    (outer_full,) = assemble(net, third, ids, me, [(0, width)], min(width, 512))
+    inner_back, outer_back, ffn_gain_back = inner_full, outer_full, ffn_gain_full
+    query_back, key_back, value_back, output_back, attn_gain_back = (
+        query_full,
+        key_full,
+        value_full,
+        output_full,
+        attn_gain_full,
     )
     queries = (matmul(flattened, query_full) + query_bias_full.astype(jnp.float32)).astype(
         jnp.bfloat16
@@ -154,14 +344,6 @@
         attn_sum, attn_gain_full.astype(jnp.float32)
     ) + attn_shift_full.astype(jnp.float32)
     normed_low = attn_normed.astype(jnp.bfloat16)
-    inner_full, inner_bias_full, outer_full, outer_bias_full, ffn_gain_full, ffn_shift_full = (
-        lax.all_gather(inner_weight, ("dp", "fsdp"), axis=0, tiled=True),
-        lax.all_gather(inner_bias, ("dp", "fsdp"), axis=0, tiled=True),
-        lax.all_gather(outer_weight, ("dp", "fsdp"), axis=0, tiled=True),
-        lax.all_gather(outer_bias, ("dp", "fsdp"), axis=0, tiled=True),
-        lax.all_gather(ffn_gain, ("dp", "fsdp"), axis=0, tiled=True),
-        lax.all_gather(ffn_shift, ("dp", "fsdp"), axis=0, tiled=True),
-    )
     inner_pre = matmul(normed_low, inner_full) + inner_bias_full.astype(jnp.float32)
     act_low = gelu_exact(inner_pre).astype(jnp.bfloat16)
     ffn_branch = matmul(act_low, outer_full) + outer_bias_full.astype(jnp.float32)
@@ -169,63 +351,27 @@
     outputs = (
         scaled_norm(ffn_sum, ffn_gain_full.astype(jnp.float32)) + ffn_shift_full.astype(jnp.float32)
     ).astype(jnp.bfloat16)
-    inner_back, outer_back, ffn_gain_back = (
-        lax.all_gather(inner_weight, ("dp", "fsdp"), axis=0, tiled=True),
-        lax.all_gather(outer_weight, ("dp", "fsdp"), axis=0, tiled=True),
-        lax.all_gather(ffn_gain, ("dp", "fsdp"), axis=0, tiled=True),
-    )
     grad_out = out_grad.reshape(tokens_here, model_width).astype(jnp.float32)
     _, ffn_norm_pull = jax.vjp(scaled_norm, ffn_sum, ffn_gain_back.astype(jnp.float32))
     grad_ffn_sum, grad_ffn_gain = ffn_norm_pull(grad_out)
     grad_ffn_shift = jnp.sum(grad_out, axis=0)
     branch_grad = grad_ffn_sum.astype(jnp.bfloat16)
     grad_outer_bias = column_sum(branch_grad)
-    grad_outer = jnp.einsum("nf,nd->fd", act_low, branch_grad, preferred_element_type=jnp.float32)
+    shard_outer = reduce_rows(net, act_low, branch_grad, ids, False)
     grad_act = jnp.einsum("nd,fd->nf", branch_grad, outer_back, preferred_element_type=jnp.float32)
     _, gelu_pull = jax.vjp(gelu_exact, inner_pre)
     inner_grad = gelu_pull(grad_act)[0].astype(jnp.bfloat16)
     grad_inner_bias = column_sum(inner_grad)
-    grad_inner = jnp.einsum("nd,nf->df", normed_low, inner_grad, preferred_element_type=jnp.float32)
+    shard_inner = reduce_rows(net, normed_low, inner_grad, ids, True)
     grad_normed = grad_ffn_sum + jnp.einsum(
         "nf,df->nd", inner_grad, inner_back, preferred_element_type=jnp.float32
-    )
-    ffn_terms = (
-        grad_inner,
-        grad_inner_bias,
-        grad_outer,
-        grad_outer_bias,
-        grad_ffn_gain,
-        grad_ffn_shift,
-    )
-    ffn_owned = (
-        lax.psum_scatter(ffn_terms[0], ("dp", "fsdp"), scatter_dimension=0, tiled=True),
-        lax.psum_scatter(ffn_terms[1], ("dp", "fsdp"), scatter_dimension=0, tiled=True),
-        lax.psum_scatter(ffn_terms[2], ("dp", "fsdp"), scatter_dimension=0, tiled=True),
-        lax.psum_scatter(ffn_terms[3], ("dp", "fsdp"), scatter_dimension=0, tiled=True),
-        lax.psum_scatter(ffn_terms[4], ("dp", "fsdp"), scatter_dimension=0, tiled=True),
-        lax.psum_scatter(ffn_terms[5], ("dp", "fsdp"), scatter_dimension=0, tiled=True),
-    )
-    (
-        shard_inner,
-        shard_inner_bias,
-        shard_outer,
-        shard_outer_bias,
-        shard_ffn_gain,
-        shard_ffn_shift,
-    ) = ffn_owned
-    query_back, key_back, value_back, output_back, attn_gain_back = (
-        lax.all_gather(query_weight, ("dp", "fsdp"), axis=0, tiled=True),
-        lax.all_gather(key_weight, ("dp", "fsdp"), axis=0, tiled=True),
-        lax.all_gather(value_weight, ("dp", "fsdp"), axis=0, tiled=True),
-        lax.all_gather(output_weight, ("dp", "fsdp"), axis=0, tiled=True),
-        lax.all_gather(attn_gain, ("dp", "fsdp"), axis=0, tiled=True),
     )
     _, attn_norm_pull = jax.vjp(scaled_norm, attn_sum, attn_gain_back.astype(jnp.float32))
     grad_attn_sum, grad_attn_gain = attn_norm_pull(grad_normed)
     grad_attn_shift = jnp.sum(grad_normed, axis=0)
     attn_grad = grad_attn_sum.astype(jnp.bfloat16)
     grad_output_bias = column_sum(attn_grad)
-    grad_output = jnp.einsum("nd,ne->de", mixed_low, attn_grad, preferred_element_type=jnp.float32)
+    shard_output = reduce_rows(net, mixed_low, attn_grad, ids, False)
     mixed_grad = jnp.einsum(
         "ne,de->nd", attn_grad, output_back, preferred_element_type=jnp.float32
     ).astype(jnp.bfloat16)
@@ -245,37 +391,46 @@
     value_grad = from_groups(group_vgrad, row_count, seq_len).astype(jnp.bfloat16)
     grad_query_bias = column_sum(query_grad)
     grad_value_bias = column_sum(value_grad)
-    grad_query = jnp.einsum("nd,ne->de", flattened, query_grad, preferred_element_type=jnp.float32)
-    grad_key = jnp.einsum("nd,ne->de", flattened, key_grad, preferred_element_type=jnp.float32)
-    grad_value = jnp.einsum("nd,ne->de", flattened, value_grad, preferred_element_type=jnp.float32)
+    middle = key_grad.shape[1] // 2
+    shard_low = reduce_rows(
+        net, flattened, jnp.concatenate([query_grad, key_grad[:, :middle]], axis=1), ids, False
+    )
+    shard_high = reduce_rows(
+        net, flattened, jnp.concatenate([key_grad[:, middle:], value_grad], axis=1), ids, True
+    )
+    shard_query = shard_low[:, :model_width]
+    shard_key = jnp.concatenate([shard_low[:, model_width:], shard_high[:, :middle]], axis=1)
+    shard_value = shard_high[:, middle:]
     input_grad = (
         grad_attn_sum
         + jnp.einsum("ne,de->nd", query_grad, query_back, preferred_element_type=jnp.float32)
         + jnp.einsum("ne,de->nd", key_grad, key_back, preferred_element_type=jnp.float32)
         + jnp.einsum("ne,de->nd", value_grad, value_back, preferred_element_type=jnp.float32)
     )
-    attn_owned = (
-        lax.psum_scatter(grad_query, ("dp", "fsdp"), scatter_dimension=0, tiled=True),
-        lax.psum_scatter(grad_key, ("dp", "fsdp"), scatter_dimension=0, tiled=True),
-        lax.psum_scatter(grad_value, ("dp", "fsdp"), scatter_dimension=0, tiled=True),
-        lax.psum_scatter(grad_output, ("dp", "fsdp"), scatter_dimension=0, tiled=True),
-        lax.psum_scatter(grad_query_bias, ("dp", "fsdp"), scatter_dimension=0, tiled=True),
-        lax.psum_scatter(grad_value_bias, ("dp", "fsdp"), scatter_dimension=0, tiled=True),
-        lax.psum_scatter(grad_output_bias, ("dp", "fsdp"), scatter_dimension=0, tiled=True),
-        lax.psum_scatter(grad_attn_gain, ("dp", "fsdp"), scatter_dimension=0, tiled=True),
-        lax.psum_scatter(grad_attn_shift, ("dp", "fsdp"), scatter_dimension=0, tiled=True),
-    )
     (
-        shard_query,
-        shard_key,
-        shard_value,
-        shard_output,
         shard_query_bias,
         shard_value_bias,
         shard_output_bias,
         shard_attn_gain,
         shard_attn_shift,
-    ) = attn_owned
+        shard_inner_bias,
+        shard_outer_bias,
+        shard_ffn_gain,
+        shard_ffn_shift,
+    ) = reduce_vectors(
+        net,
+        [
+            grad_query_bias,
+            grad_value_bias,
+            grad_output_bias,
+            grad_attn_gain,
+            grad_attn_shift,
+            grad_inner_bias,
+            grad_outer_bias,
+            grad_ffn_gain,
+            grad_ffn_shift,
+        ],
+    )
     return (
         outputs.reshape(row_count, seq_len, model_width),
         input_grad.reshape(row_count, seq_len, model_width),
@@ -319,7 +474,7 @@
         P(("dp", "fsdp"), None, None),
     )
     return jax.shard_map(
-        shards,
+        functools.partial(shards, Slice(mesh.shape["dp"], mesh.shape["fsdp"])),
         mesh=mesh,
         in_specs=placed,
         out_specs=(

time: 1840 us -> 614 us (0.33)
  waiting for transfers between devices: 1440 us -> 211 us
  blocking collectives: 149 us -> 0 us
  starting transfers between devices: 0.47 us -> 108 us
  Pallas kernels: 0 us -> 25.3 us
  other arithmetic: 15.7 us -> 37.8 us
    reduce_scatter x3 -> x0, waiting for transfers between devices: 880 us -> none  [the longest x1 366 us: shards(): lax.psum_scatter(ffn_terms[0], ('dp', 'fsdp'), scatter_dimension=0, tiled...]
    unnamed x15 -> x0, waiting for transfers between devices: 345 us -> none
    all_gather x6 -> x0, waiting for transfers between devices: 212 us -> none  [the longest x1 73.9 us: shards(): lax.all_gather(inner_weight, ('dp', 'fsdp'), axis=0, tiled=True)]
    ppermute x0 -> x66, waiting for transfers between devices: none -> 211 us  [swap(): return lax.ppermute(value, AXES, pairs)]
    ppermute x0 -> x66, starting transfers between devices: none -> 104 us  [swap(): return lax.ppermute(value, AXES, pairs)]
    unnamed x2 -> x0, blocking collectives: 83 us -> none
    all_gather x1 -> x0, blocking collectives: 65.7 us -> none  [shards(): lax.all_gather(inner_bias, ('dp', 'fsdp'), axis=0, tiled=True)]
    unnamed x68 -> x157, local copies, waits for them, and re-layouts: 39.2 us -> 4.74 us
  transfers between devices with their start and end apart: 12 -> 67, of which waited for: 10 -> 24; matrix products, arithmetic and copies ran while one was open for 7% -> 20% of each run, Pallas kernels for 0% -> 3%
where the time goes in v1:
time: 614 us; the launch traced here: 608 us
  waiting for transfers between devices  211 us (34%)
  matrix products  161 us (26%)
  starting transfers between devices  108 us (18%)
  local copies, waits for them, and re-layouts  63 us (10%)
  other arithmetic  37.8 us (6%)
  Pallas kernels  25.3 us (4%)
    ppermute x66, waiting for transfers between devices, swap(): return lax.ppermute(value, AXES, pairs)  211 us
    ppermute x66, starting transfers between devices, swap(): return lax.ppermute(value, AXES, pairs)  104 us
    dot_general x15, matrix products, outer_dot(): return jnp.einsum('tm,tn->mn', left, right, preferred_element_type=F32)  40.2 us
    dot_general x6, matrix products, matmul(): return jnp.dot(left, right, preferred_element_type=jnp.float32)  37.3 us
    pallas_call x4, Pallas kernels, assemble(): pl.pallas_call(body, out_shape=[jax.ShapeDtypeStruct((total, w), BF) for...  25.3 us
    dot_general x1, matrix products, shards(): jnp.einsum('nd,fd->nf', branch_grad, outer_back, preferred_element_type=j...  14.4 us
  transfers between devices with their start and end apart: 67, of which 24 were waited for; matrix products, arithmetic and copies ran while one was open for 20% of the time, Pallas kernels for 3%

profile of v1, /device:TPU:0, one launch (start us, length us, event | category | flops | bytes accessed | tf_op | source)
XLA Modules:
  0.0 608.3 jit_solution(8450199089807997256)
XLA Ops:
  8.5 5.1 collective-permute-start.2
  20.9 8.7 %collective-permute-start.13 = (bf16[32,5120]{1,0:T(8,128)(2,1)S(1)}, bf16[32,5120]{1,0:T(8,128)(2,1)S(1)}, u32[]{:S(2)}, u32[]{:S(2)}) collective-permute-start(bf16[32,5120]{1,0:T(8,128)(2,1)S(1)} %constant_dynamic-update-slice_fusion), channel_id=1, source_target_pairs={{0,2},{1,3},{2,0},{3,1},{4,6},{5,7},{6,4},{7,5},{8,10},{9,11},{10,... | collective-permute-start | bytes 983048 | tf_op jit(solution)/shard_map/ppermute | solution.py:107
  29.6 22.0 %collective-permute-done.1 = bf16[32,3200]{1,0:T(8,128)(2,1)S(1)} collective-permute-done((bf16[32,3200]{1,0:T(8,128)(2,1)S(1)}, bf16[32,3200]{1,0:T(8,128)(2,1)S(1)}, u32[]{:S(2)}, u32[]{:S(2)}) %collective-permute-start.1) | collective-permute-done | bytes 204832 | tf_op jit(solution)/shard_map/ppermute | solution.py:107
  54.9 15.6 %collective-permute-start.24 = (bf16[128,1024]{1,0:T(8,128)(2,1)}, bf16[128,1024]{1,0:T(8,128)(2,1)S(1)}, u32[]{:S(2)}, u32[]{:S(2)}) collective-permute-start(bf16[128,1024]{1,0:T(8,128)(2,1)} %param.35), channel_id=1, source_target_pairs={{0,1},{1,0},{2,3},{3,2},{4,5},{5,4},{6,7},{7,6},{8,9},{9,8},{10,11... | collective-permute-start | bytes 786440 | tf_op jit(solution)/shard_map/ppermute | solution.py:107
  70.6 11.1 %collective-permute-done.25 = bf16[128,1024]{1,0:T(8,128)(2,1)S(1)} collective-permute-done((bf16[128,1024]{1,0:T(8,128)(2,1)}, bf16[128,1024]{1,0:T(8,128)(2,1)S(1)}, u32[]{:S(2)}, u32[]{:S(2)}) %collective-permute-start.25) | collective-permute-done | bytes 262176 | tf_op jit(solution)/shard_map/ppermute | solution.py:107
  83.2 3.9 collective-permute-done.24
  93.1 9.9 %collective-permute-done.3.refs_1_ = bf16[4,32,3200]{2,1,0:T(8,128)(2,1)} collective-permute-done((bf16[4,32,3200]{2,1,0:T(8,128)(2,1)S(1)}, bf16[4,32,3200]{2,1,0:T(8,128)(2,1)}, u32[]{:S(2)}, u32[]{:S(2)}) %collective-permute-start.3) | collective-permute-done | bytes 819232 | tf_op jit(solution)/shard_map/ppermute | solution.py:107
  104.5 3.9 collective-permute-done.4.refs_2_
  113.3 12.1 %collective-permute-done.27.refs_1_ = bf16[4,128,1024]{2,1,0:T(8,128)(2,1)} collective-permute-done((bf16[4,128,1024]{2,1,0:T(8,128)(2,1)}, bf16[4,128,1024]{2,1,0:T(8,128)(2,1)}, u32[]{:S(2)}, u32[]{:S(2)}) %collective-permute-start.27) | collective-permute-done | bytes 1048608 | tf_op jit(solution)/shard_map/ppermute | solution.py:107
  126.9 3.9 collective-permute-done.28.refs_2_
  130.8 35.8 %collective-permute-done.5.refs_3_ = bf16[2,32,3200]{2,1,0:T(8,128)(2,1)S(1)} collective-permute-done((bf16[2,32,3200]{2,1,0:T(8,128)(2,1)S(1)}, bf16[2,32,3200]{2,1,0:T(8,128)(2,1)S(1)}, u32[]{:S(2)}, u32[]{:S(2)}) %collective-permute-start.5) | collective-permute-done | bytes 409632 | tf_op jit(solution)/shard_map/ppermute | solution.py:107
  186.1 7.0 %assemble.4 = (bf16[1024,1024]{1,0:T(8,128)(2,1)}, bf16[1024,1024]{1,0:T(8,128)(2,1)}, bf16[1024,1024]{1,0:T(8,128)(2,1)}) custom-call(s32[3]{0:T(128)} %pad_add_fusion.ids_ref, bf16[4,32,3200]{2,1,0:T(8,128)(2,1)} %copy-done.7, bf16[4,32,3200]{2,1,0:T(8,128)(2,1)} %collective-permute-done.3.refs_1_, bf16[4,32,3200]{2,1,0:T(8,128)(2,1)} %collective-permute-done.4.refs_2_, ...), custom_call_target="tpu_custom_call" | custom-call | tf_op jit(solution)/shard_map/assemble/pallas_call | solution.py:174
  198.5 9.0 %collective-permute-done.17.refs_3_ = bf16[2,32,5120]{2,1,0:T(8,128)(2,1)} collective-permute-done((bf16[2,32,5120]{2,1,0:T(8,128)(2,1)}, bf16[2,32,5120]{2,1,0:T(8,128)(2,1)}, u32[]{:S(2)}, u32[]{:S(2)}) %collective-permute-start.17) | collective-permute-done | bytes 655392 | tf_op jit(solution)/shard_map/ppermute | solution.py:107
  210.4 4.6 collective-permute-done.18.refs_4_
  217.2 20.5 %while.26 = (s32[]{:T(128)}, bf16[4,512,4,64]{1,3,2,0:T(8,128)(2,1)}, f32[4,4,512]{2,1,0:T(4,128)S(1)}, bf16[4,512,4,64]{1,3,2,0:T(8,128)(2,1)}, s32[4,512]{1,0:...) while((s32[]{:T(128)}, ...), condition=%wide.region_3.4_spmd, body=%wide.region_0.3_spmd.sunk | while | flops 281278464 | bytes 15016037 | solution.py:337
  242.5 6.6 %assemble.7 = bf16[4096,1024]{1,0:T(8,128)(2,1)} custom-call(s32[3]{0:T(128)} %pad_add_fusion.ids_ref, bf16[4,128,1024]{2,1,0:T(8,128)(2,1)} %pad_maximum_fusion.3.refs_0_, bf16[4,128,1024]{2,1,0:T(8,128)(2,1)} %collective-permute-done.27.refs_1_, bf16[4,128,1024]{2,1,0:T(8,128)(2,1)} %collective-permute-done.28.refs_2_, ...), custom_call_target="tpu_custom_call" | custom-call | tf_op jit(solution)/shard_map/assemble/pallas_call | solution.py:174
  249.2 9.3 %assemble.6 = (bf16[1024,1024]{1,0:T(8,128)(2,1)}, bf16[1024,4096]{1,0:T(8,128)(2,1)}) custom-call(s32[3]{0:T(128)} %pad_add_fusion.ids_ref, bf16[4,32,5120]{2,1,0:T(8,128)(2,1)} %pad_maximum_fusion.2.refs_0_, bf16[4,32,5120]{2,1,0:T(8,128)(2,1)} %collective-permute-done.15.refs_1_, bf16[4,32,5120]{2,1,0:T(8,128)(2,1)} %collective-permute-done.16.refs_2_, ...), custom_call_target="tpu_custom_call" | custom-call | tf_op jit(solution)/shard_map/assemble/pallas_call | solution.py:174
  262.9 24.1 %multiply_convert_fusion.1 = (bf16[512,4096]{1,0:T(8,128)(2,1)S(1)}, f32[512,4096]{1,0:T(8,128)}, f32[512,4096]{1,0:T(8,128)}) fusion(f32[4096]{0:T(1024)S(1)} %reshape.339, bf16[512,1024]{1,0:T(8,128)(2,1)S(1)} %fusion.72, bf16[1024,4096]{1,0:T(8,128)(2,1)S(1)} %copy-done.79), kind=kOutput, calls=%fused_computation.66 | convolution fusion | flops 4433379328 | bytes 30425088 | tf_op jit(solution)/shard_map/dot_general | solution.py:89
  287.0 4.8 fusion.187
  296.3 14.4 %convert_reduce_fusion = (f32[4096]{0:T(1024)}, bf16[512,4096]{1,0:T(8,128)(2,1)S(1)}) fusion(f32[512,4096]{1,0:T(8,128)} %get-tuple-element.182, f32[512,4096]{1,0:T(8,128)} %get-tuple-element.247, f32[4096]{0:T(1024)S(1)} %reshape.339, bf16[512,1024]{1,0:T(8,128)(2,1)S(1)} %get-tuple-element.172, bf16[4096,1024]{1,0:T(8,128)(2,1)} %assemble.7), kind=kOutput, calls=%fused_computation.64 | convolution fusion | flops 4330614784 | bytes 30441472 | tf_op jit(solution)/shard_map/nd,fd->nf/dot_general | solution.py:361
  310.7 9.7 %multiply_reduce_fusion.1 = (f32[1024]{0:T(1024)}, f32[512]{0:T(512)S(1)}, f32[1024]{0:T(1024)}, f32[512,1024]{1,0:T(8,128)S(1)}) fusion(f32[512,1024]{1,0:T(8,128)S(1)} %get-tuple-element.246, f32[512]{0:T(512)S(1)} %fusion.164, f32[512]{0:T(512)S(1)} %broadcast_multiply_fusion.1, f32[1024]{0:T(1024)S(1)} %get-tuple-element.133, ...), kind=kOutput, calls=%fused_computation.110 | convolution fusion | flops 4300207616 | bytes 18894848 | tf_op jit(solution)/shard_map/nf,df->nd/dot_general | solution.py:366
  330.8 44.2 %while.27 = (s32[]{:T(128)}, bf16[4,512,4,64]{1,3,2,0:T(8,128)(2,1)}, bf16[4,512,4,64]{1,3,2,0:T(8,128)(2,1)}, bf16[4,512,4,64]{1,3,2,0:T(8,128)(2,1)}, bf16[4,5...) while((s32[]{:T(128)}, ...), condition=%wide.region_14.15_spmd, body=%wide.region_12.14_spmd.sunk | while | flops 687339520 | bytes 65342784 | solution.py:378
  375.0 4.6 fusion.189
  408.9 7.0 %convolution_convert_fusion = bf16[512,4096]{1,0:T(8,128)(2,1)} fusion(bf16[512,4096]{1,0:T(8,128)(2,1)} %copy-done, bf16[512,128]{1,0:T(8,128)(2,1)} %get-tuple-element.205, bf16[512,128]{1,0:T(8,128)(2,1)} %get-tuple-element.206, bf16[512,128]{1,0:T(8,128)(2,1)} %get-tuple-element.207, bf16[512,128]{1,0:T(8,128)(2,1)} %get-tuple-element.208), kind=kOutput, calls=%fused_computation.80 | convolution fusion | flops 2151677952 | bytes 8912896 | tf_op jit(solution)/shard_map/tm,tn->mn/dot_general | solution.py:206
  417.6 4.4 convolution_convert_fusion.1
  437.9 7.7 %collective-permute-done.49 = bf16[256,1024]{1,0:T(8,128)(2,1)} collective-permute-done((bf16[256,1024]{1,0:T(8,128)(2,1)}, bf16[256,1024]{1,0:T(8,128)(2,1)}, u32[]{:S(2)}, u32[]{:S(2)}) %collective-permute-start.49) | collective-permute-done | bytes 524320 | tf_op jit(solution)/shard_map/ppermute | solution.py:107
  471.4 13.7 %collective-permute-done.43 = bf16[256,1536]{1,0:T(8,128)(2,1)S(1)} collective-permute-done((bf16[256,1536]{1,0:T(8,128)(2,1)S(1)}, bf16[256,1536]{1,0:T(8,128)(2,1)S(1)}, u32[]{:S(2)}, u32[]{:S(2)}) %collective-permute-start.43) | collective-permute-done | bytes 786464 | tf_op jit(solution)/shard_map/ppermute | solution.py:107
  509.1 25.8 %collective-permute-done.55 = bf16[256,4096]{1,0:T(8,128)(2,1)S(1)} collective-permute-done((bf16[256,4096]{1,0:T(8,128)(2,1)S(1)}, bf16[256,4096]{1,0:T(8,128)(2,1)S(1)}, u32[]{:S(2)}, u32[]{:S(2)}) %collective-permute-start.55) | collective-permute-done | bytes 2097184 | tf_op jit(solution)/shard_map/ppermute | solution.py:107
  549.0 14.3 %collective-permute-done.56 = bf16[128,4096]{1,0:T(8,128)(2,1)S(1)} collective-permute-done((bf16[128,4096]{1,0:T(8,128)(2,1)S(1)}, bf16[128,4096]{1,0:T(8,128)(2,1)S(1)}, u32[]{:S(2)}, u32[]{:S(2)}) %collective-permute-start.56) | collective-permute-done | bytes 1048608 | tf_op jit(solution)/shard_map/ppermute | solution.py:107
  574.8 14.0 %collective-permute-start.63 = (bf16[128,1024]{1,0:T(8,128)(2,1)S(1)}, bf16[128,1024]{1,0:T(8,128)(2,1)S(1)}, u32[]{:S(2)}, u32[]{:S(2)}) collective-permute-start(bf16[128,1024]{1,0:T(8,128)(2,1)S(1)} %get-tuple-element.196), channel_id=1, source_target_pairs={{0,1},{1,0},{2,3},{3,2},{4,5},{5,4},{6,7},{7,6},{8,9},{9,8},{10,11... | collective-permute-start | bytes 786440 | tf_op jit(solution)/shard_map/ppermute | solution.py:107
  588.8 9.6 %collective-permute-done.58 = bf16[32,4096]{1,0:T(8,128)(2,1)S(1)} collective-permute-done((bf16[32,4096]{1,0:T(8,128)(2,1)S(1)}, bf16[32,4096]{1,0:T(8,128)(2,1)S(1)}, u32[]{:S(2)}, u32[]{:S(2)}) %collective-permute-start.58) | collective-permute-done | bytes 262176 | tf_op jit(solution)/shard_map/ppermute | solution.py:107
  599.3 7.6 %collective-permute-done.64 = bf16[128,1024]{1,0:T(8,128)(2,1)S(1)} collective-permute-done((bf16[128,1024]{1,0:T(8,128)(2,1)S(1)}, bf16[128,1024]{1,0:T(8,128)(2,1)S(1)}, u32[]{:S(2)}, u32[]{:S(2)}) %collective-permute-start.64) | collective-permute-done | bytes 262176 | tf_op jit(solution)/shard_map/ppermute | solution.py:107
  (508 shorter events, 275.0 us)
Async XLA Ops:
  13.6 38.0 %collective-permute-start.1 = (bf16[32,3200]{1,0:T(8,128)(2,1)S(1)}, bf16[32,3200]{1,0:T(8,128)(2,1)S(1)}, u32[]{:S(2)}, u32[]{:S(2)}) collective-permute-start(bf16[32,3200]{1,0:T(8,128)(2,1)S(1)} %fusion.148), channel_id=1, source_target_pairs={{0,2},{1,3},{2,0},{3,1},{4,6},{5,7},{6,4},{7,5},{8,10},{9,11},{10,... | collective-permute-start | bytes 614408 | tf_op jit(solution)/shard_map/ppermute | solution.py:107
  13.6 38.0 %collective-permute-start = (bf16[32,3200]{1,0:T(8,128)(2,1)S(1)}, bf16[32,3200]{1,0:T(8,128)(2,1)S(1)}, u32[]{:S(2)}, u32[]{:S(2)}) collective-permute-start(bf16[32,3200]{1,0:T(8,128)(2,1)S(1)} %fusion.148), channel_id=1, source_target_pairs={{0,1},{1,0},{2,3},{3,2},{4,5},{5,4},{6,7},{7,6},{8,9},{9,8},{10,11... | collective-permute-start | bytes 614408 | tf_op jit(solution)/shard_map/ppermute | solution.py:107
  16.1 73.7 %collective-permute-start.14 = (bf16[32,5120]{1,0:T(8,128)(2,1)S(1)}, bf16[32,5120]{1,0:T(8,128)(2,1)S(1)}, u32[]{:S(2)}, u32[]{:S(2)}) collective-permute-start(bf16[32,5120]{1,0:T(8,128)(2,1)S(1)} %constant_dynamic-update-slice_fusion), channel_id=1, source_target_pairs={{0,3},{1,2},{2,1},{3,0},{4,7},{5,6},{6,5},{7,4},{8,11},{9,10},{10,... | collective-permute-start | bytes 983048 | tf_op jit(solution)/shard_map/ppermute | solution.py:107
  19.9 35.0 %collective-permute-start.26 = (bf16[128,1024]{1,0:T(8,128)(2,1)}, bf16[128,1024]{1,0:T(8,128)(2,1)S(1)}, u32[]{:S(2)}, u32[]{:S(2)}) collective-permute-start(bf16[128,1024]{1,0:T(8,128)(2,1)} %param.35), channel_id=1, source_target_pairs={{0,3},{1,2},{2,1},{3,0},{4,7},{5,6},{6,5},{7,4},{8,11},{9,10},{10,... | collective-permute-start | bytes 786440 | tf_op jit(solution)/shard_map/ppermute | solution.py:107
  20.9 68.9 %collective-permute-start.13 = (bf16[32,5120]{1,0:T(8,128)(2,1)S(1)}, bf16[32,5120]{1,0:T(8,128)(2,1)S(1)}, u32[]{:S(2)}, u32[]{:S(2)}) collective-permute-start(bf16[32,5120]{1,0:T(8,128)(2,1)S(1)} %constant_dynamic-update-slice_fusion), channel_id=1, source_target_pairs={{0,2},{1,3},{2,0},{3,1},{4,6},{5,7},{6,4},{7,5},{8,10},{9,11},{10,... | collective-permute-start | bytes 983048 | tf_op jit(solution)/shard_map/ppermute | solution.py:107
  51.7 39.7 %collective-permute-start.12 = (bf16[32,5120]{1,0:T(8,128)(2,1)S(1)}, bf16[32,5120]{1,0:T(8,128)(2,1)S(1)}, u32[]{:S(2)}, u32[]{:S(2)}) collective-permute-start(bf16[32,5120]{1,0:T(8,128)(2,1)S(1)} %constant_dynamic-update-slice_fusion), channel_id=1, source_target_pairs={{0,1},{1,0},{2,3},{3,2},{4,5},{5,4},{6,7},{7,6},{8,9},{9,8},{10,11... | collective-permute-start | bytes 983048 | tf_op jit(solution)/shard_map/ppermute | solution.py:107
  89.8 35.7 %collective-permute-start.27 = (bf16[4,128,1024]{2,1,0:T(8,128)(2,1)}, bf16[4,128,1024]{2,1,0:T(8,128)(2,1)}, u32[]{:S(2)}, u32[]{:S(2)}) collective-permute-start(bf16[4,128,1024]{2,1,0:T(8,128)(2,1)} %pad_maximum_fusion.3.refs_0_), channel_id=1, source_target_pairs={{0,8},{1,9},{2,10},{3,11},{4,12},{5,13},{6,14},{7,15},{8,0},{9,1},... | collective-permute-start | bytes 3145736 | tf_op jit(solution)/shard_map/ppermute | solution.py:107
  91.3 39.5 %collective-permute-start.28 = (bf16[4,128,1024]{2,1,0:T(8,128)(2,1)}, bf16[4,128,1024]{2,1,0:T(8,128)(2,1)}, u32[]{:S(2)}, u32[]{:S(2)}) collective-permute-start(bf16[4,128,1024]{2,1,0:T(8,128)(2,1)} %pad_maximum_fusion.3.refs_0_), channel_id=1, source_target_pairs={{0,16},{1,17},{2,18},{3,19},{4,20},{5,21},{6,22},{7,23},{8,24},{9,... | collective-permute-start | bytes 3145736 | tf_op jit(solution)/shard_map/ppermute | solution.py:107
  103.0 64.2 %collective-permute-start.15 = (bf16[4,32,5120]{2,1,0:T(8,128)(2,1)}, bf16[4,32,5120]{2,1,0:T(8,128)(2,1)}, u32[]{:S(2)}, u32[]{:S(2)}) collective-permute-start(bf16[4,32,5120]{2,1,0:T(8,128)(2,1)} %pad_maximum_fusion.2.refs_0_), channel_id=1, source_target_pairs={{0,8},{1,9},{2,10},{3,11},{4,12},{5,13},{6,14},{7,15},{8,0},{9,1},... | collective-permute-start | bytes 3932168 | tf_op jit(solution)/shard_map/ppermute | solution.py:107
  108.3 59.1 %collective-permute-start.16 = (bf16[4,32,5120]{2,1,0:T(8,128)(2,1)}, bf16[4,32,5120]{2,1,0:T(8,128)(2,1)}, u32[]{:S(2)}, u32[]{:S(2)}) collective-permute-start(bf16[4,32,5120]{2,1,0:T(8,128)(2,1)} %pad_maximum_fusion.2.refs_0_), channel_id=1, source_target_pairs={{0,16},{1,17},{2,18},{3,19},{4,20},{5,21},{6,22},{7,23},{8,24},{9,... | collective-permute-start | bytes 3932168 | tf_op jit(solution)/shard_map/ppermute | solution.py:107
  111.8 54.8 %collective-permute-start.5 = (bf16[2,32,3200]{2,1,0:T(8,128)(2,1)S(1)}, bf16[2,32,3200]{2,1,0:T(8,128)(2,1)S(1)}, u32[]{:S(2)}, u32[]{:S(2)}) collective-permute-start(bf16[2,32,3200]{2,1,0:T(8,128)(2,1)S(1)} %slice.214), channel_id=1, source_target_pairs={{0,16},{1,17},{2,18},{3,19},{4,20},{5,21},{6,22},{7,23},{8,24},{9,... | collective-permute-start | bytes 1228808 | tf_op jit(solution)/shard_map/ppermute | solution.py:107
  125.5 41.2 %collective-permute-start.6 = (bf16[2,32,3200]{2,1,0:T(8,128)(2,1)S(1)}, bf16[2,32,3200]{2,1,0:T(8,128)(2,1)S(1)}, u32[]{:S(2)}, u32[]{:S(2)}) collective-permute-start(bf16[2,32,3200]{2,1,0:T(8,128)(2,1)S(1)} %slice.215), channel_id=1, source_target_pairs={{0,8},{1,9},{2,10},{3,11},{4,12},{5,13},{6,14},{7,15},{8,0},{9,1},... | collective-permute-start | bytes 1228808 | tf_op jit(solution)/shard_map/ppermute | solution.py:107
  130.8 48.3 %collective-permute-start.8 = (bf16[4,32,3200]{2,1,0:T(8,128)(2,1)}, bf16[4,32,3200]{2,1,0:T(8,128)(2,1)S(1)}, u32[]{:S(2)}, u32[]{:S(2)}) collective-permute-start(bf16[4,32,3200]{2,1,0:T(8,128)(2,1)} %collective-permute-done.3.refs_1_), channel_id=1, source_target_pairs={{0,4},{1,5},{2,6},{3,7},{4,0},{5,1},{6,2},{7,3},{8,12},{9,13},{10,... | collective-permute-start | bytes 2457608 | tf_op jit(solution)/shard_map/ppermute | solution.py:107
  182.1 32.9 %collective-permute-start.32 = (bf16[4,128,1024]{2,1,0:T(8,128)(2,1)}, bf16[4,128,1024]{2,1,0:T(8,128)(2,1)}, u32[]{:S(2)}, u32[]{:S(2)}) collective-permute-start(bf16[4,128,1024]{2,1,0:T(8,128)(2,1)} %collective-permute-done.27.refs_1_), channel_id=1, source_target_pairs={{0,4},{1,5},{2,6},{3,7},{4,0},{5,1},{6,2},{7,3},{8,12},{9,13},{10,... | collective-permute-start | bytes 3145736 | tf_op jit(solution)/shard_map/ppermute | solution.py:107
  215.0 34.1 %collective-permute-start.19 = (bf16[4,32,5120]{2,1,0:T(8,128)(2,1)}, bf16[4,32,5120]{2,1,0:T(8,128)(2,1)}, u32[]{:S(2)}, u32[]{:S(2)}) collective-permute-start(bf16[4,32,5120]{2,1,0:T(8,128)(2,1)} %pad_maximum_fusion.2.refs_0_), channel_id=1, source_target_pairs={{0,4},{1,5},{2,6},{3,7},{4,0},{5,1},{6,2},{7,3},{8,12},{9,13},{10,... | collective-permute-start | bytes 3932168 | tf_op jit(solution)/shard_map/ppermute | solution.py:107
  215.0 34.2 %collective-permute-start.20 = (bf16[4,32,5120]{2,1,0:T(8,128)(2,1)}, bf16[4,32,5120]{2,1,0:T(8,128)(2,1)}, u32[]{:S(2)}, u32[]{:S(2)}) collective-permute-start(bf16[4,32,5120]{2,1,0:T(8,128)(2,1)} %collective-permute-done.15.refs_1_), channel_id=1, source_target_pairs={{0,4},{1,5},{2,6},{3,7},{4,0},{5,1},{6,2},{7,3},{8,12},{9,13},{10,... | collective-permute-start | bytes 3932168 | tf_op jit(solution)/shard_map/ppermute | solution.py:107
  215.5 33.7 %collective-permute-start.21 = (bf16[4,32,5120]{2,1,0:T(8,128)(2,1)}, bf16[4,32,5120]{2,1,0:T(8,128)(2,1)}, u32[]{:S(2)}, u32[]{:S(2)}) collective-permute-start(bf16[4,32,5120]{2,1,0:T(8,128)(2,1)} %collective-permute-done.16.refs_2_), channel_id=1, source_target_pairs={{0,4},{1,5},{2,6},{3,7},{4,0},{5,1},{6,2},{7,3},{8,12},{9,13},{10,... | collective-permute-start | bytes 3932168 | tf_op jit(solution)/shard_map/ppermute | solution.py:107
  215.6 33.5 %collective-permute-start.22 = (bf16[2,32,5120]{2,1,0:T(8,128)(2,1)}, bf16[2,32,5120]{2,1,0:T(8,128)(2,1)}, u32[]{:S(2)}, u32[]{:S(2)}) collective-permute-start(bf16[2,32,5120]{2,1,0:T(8,128)(2,1)} %collective-permute-done.17.refs_3_), channel_id=1, source_target_pairs={{0,4},{1,5},{2,6},{3,7},{4,0},{5,1},{6,2},{7,3},{8,12},{9,13},{10,... | collective-permute-start | bytes 1966088 | tf_op jit(solution)/shard_map/ppermute | solution.py:107
  216.0 33.1 %collective-permute-start.23 = (bf16[2,32,5120]{2,1,0:T(8,128)(2,1)}, bf16[2,32,5120]{2,1,0:T(8,128)(2,1)}, u32[]{:S(2)}, u32[]{:S(2)}) collective-permute-start(bf16[2,32,5120]{2,1,0:T(8,128)(2,1)} %collective-permute-done.18.refs_4_), channel_id=1, source_target_pairs={{0,4},{1,5},{2,6},{3,7},{4,0},{5,1},{6,2},{7,3},{8,12},{9,13},{10,... | collective-permute-start | bytes 1966088 | tf_op jit(solution)/shard_map/ppermute | solution.py:107
  387.0 61.8 %collective-permute-start.36 = (bf16[512,1536]{1,0:T(8,128)(2,1)}, bf16[512,1536]{1,0:T(8,128)(2,1)}, u32[]{:S(2)}, u32[]{:S(2)}) collective-permute-start(bf16[512,1536]{1,0:T(8,128)(2,1)} %convolution_convert_fusion.3), channel_id=1, source_target_pairs={{0,4},{1,5},{2,6},{3,7},{4,0},{5,1},{6,2},{7,3},{8,12},{9,13},{10,... | collective-permute-start | bytes 4718600 | tf_op jit(solution)/shard_map/ppermute | solution.py:107
  390.6 68.9 %collective-permute-start.42 = (bf16[512,1536]{1,0:T(8,128)(2,1)}, bf16[512,1536]{1,0:T(8,128)(2,1)}, u32[]{:S(2)}, u32[]{:S(2)}) collective-permute-start(bf16[512,1536]{1,0:T(8,128)(2,1)} %convolution_convert_fusion.2), channel_id=1, source_target_pairs={{0,4},{1,5},{2,6},{3,7},{4,0},{5,1},{6,2},{7,3},{8,12},{9,13},{10,... | collective-permute-start | bytes 4718600 | tf_op jit(solution)/shard_map/ppermute | solution.py:107
  392.4 36.3 %collective-permute-start.48 = (bf16[512,1024]{1,0:T(8,128)(2,1)}, bf16[512,1024]{1,0:T(8,128)(2,1)}, u32[]{:S(2)}, u32[]{:S(2)}) collective-permute-start(bf16[512,1024]{1,0:T(8,128)(2,1)} %convolution_convert_fusion.6), channel_id=1, source_target_pairs={{0,4},{1,5},{2,6},{3,7},{4,0},{5,1},{6,2},{7,3},{8,12},{9,13},{10,... | collective-permute-start | bytes 3145736 | tf_op jit(solution)/shard_map/ppermute | solution.py:107
  416.0 72.2 %collective-permute-start.54 = (bf16[512,4096]{1,0:T(8,128)(2,1)}, bf16[512,4096]{1,0:T(8,128)(2,1)}, u32[]{:S(2)}, u32[]{:S(2)}) collective-permute-start(bf16[512,4096]{1,0:T(8,128)(2,1)} %convolution_convert_fusion), channel_id=1, source_target_pairs={{0,4},{1,5},{2,6},{3,7},{4,0},{5,1},{6,2},{7,3},{8,12},{9,13},{10,... | collective-permute-start | bytes 12582920 | tf_op jit(solution)/shard_map/ppermute | solution.py:107
  422.1 74.0 %collective-permute-start.60 = (bf16[2048,1024]{1,0:T(8,128)(2,1)}, bf16[2048,1024]{1,0:T(8,128)(2,1)}, u32[]{:S(2)}, u32[]{:S(2)}) collective-permute-start(bf16[2048,1024]{1,0:T(8,128)(2,1)} %convolution_convert_fusion.1), channel_id=1, source_target_pairs={{0,4},{1,5},{2,6},{3,7},{4,0},{5,1},{6,2},{7,3},{8,12},{9,13},{10,... | collective-permute-start | bytes 12582920 | tf_op jit(solution)/shard_map/ppermute | solution.py:107
  491.1 43.8 %collective-permute-start.55 = (bf16[256,4096]{1,0:T(8,128)(2,1)S(1)}, bf16[256,4096]{1,0:T(8,128)(2,1)S(1)}, u32[]{:S(2)}, u32[]{:S(2)}) collective-permute-start(bf16[256,4096]{1,0:T(8,128)(2,1)S(1)} %add_convert_fusion.5), channel_id=1, source_target_pairs={{0,16},{1,17},{2,18},{3,19},{4,20},{5,21},{6,22},{7,23},{8,24},{9,... | collective-permute-start | bytes 6291464 | tf_op jit(solution)/shard_map/ppermute | solution.py:107
  501.0 43.6 %collective-permute-start.61 = (bf16[1024,1024]{1,0:T(8,128)(2,1)S(1)}, bf16[1024,1024]{1,0:T(8,128)(2,1)S(1)}, u32[]{:S(2)}, u32[]{:S(2)}) collective-permute-start(bf16[1024,1024]{1,0:T(8,128)(2,1)S(1)} %add_convert_fusion.2), channel_id=1, source_target_pairs={{0,8},{1,9},{2,10},{3,11},{4,12},{5,13},{6,14},{7,15},{8,0},{9,1},... | collective-permute-start | bytes 6291464 | tf_op jit(solution)/shard_map/ppermute | solution.py:107
  502.8 37.1 %collective-permute-start.47 = (bf16[32,1536]{1,0:T(8,128)(2,1)S(1)}, bf16[32,1536]{1,0:T(8,128)(2,1)S(1)}, u32[]{:S(2)}, u32[]{:S(2)}) collective-permute-start(bf16[32,1536]{1,0:T(8,128)(2,1)S(1)} %get-tuple-element.229), channel_id=1, source_target_pairs={{0,3},{1,2},{2,1},{3,0},{4,7},{5,6},{6,5},{7,4},{8,11},{9,10},{10,... | collective-permute-start | bytes 294920 | tf_op jit(solution)/shard_map/ppermute | solution.py:107
  505.5 34.4 %collective-permute-start.46 = (bf16[32,1536]{1,0:T(8,128)(2,1)S(1)}, bf16[32,1536]{1,0:T(8,128)(2,1)S(1)}, u32[]{:S(2)}, u32[]{:S(2)}) collective-permute-start(bf16[32,1536]{1,0:T(8,128)(2,1)S(1)} %get-tuple-element.230), channel_id=1, source_target_pairs={{0,2},{1,3},{2,0},{3,1},{4,6},{5,7},{6,4},{7,5},{8,10},{9,11},{10,... | collective-permute-start | bytes 294920 | tf_op jit(solution)/shard_map/ppermute | solution.py:107
  505.5 34.4 %collective-permute-start.45 = (bf16[32,1536]{1,0:T(8,128)(2,1)S(1)}, bf16[32,1536]{1,0:T(8,128)(2,1)S(1)}, u32[]{:S(2)}, u32[]{:S(2)}) collective-permute-start(bf16[32,1536]{1,0:T(8,128)(2,1)S(1)} %get-tuple-element.228), channel_id=1, source_target_pairs={{0,1},{1,0},{2,3},{3,2},{4,5},{5,4},{6,7},{7,6},{8,9},{9,8},{10,11... | collective-permute-start | bytes 294920 | tf_op jit(solution)/shard_map/ppermute | solution.py:107
  566.1 32.3 %collective-permute-start.58 = (bf16[32,4096]{1,0:T(8,128)(2,1)S(1)}, bf16[32,4096]{1,0:T(8,128)(2,1)S(1)}, u32[]{:S(2)}, u32[]{:S(2)}) collective-permute-start(bf16[32,4096]{1,0:T(8,128)(2,1)S(1)} %get-tuple-element.201), channel_id=1, source_target_pairs={{0,2},{1,3},{2,0},{3,1},{4,6},{5,7},{6,4},{7,5},{8,10},{9,11},{10,... | collective-permute-start | bytes 786440 | tf_op jit(solution)/shard_map/ppermute | solution.py:107
  566.1 32.3 %collective-permute-start.57 = (bf16[32,4096]{1,0:T(8,128)(2,1)S(1)}, bf16[32,4096]{1,0:T(8,128)(2,1)S(1)}, u32[]{:S(2)}, u32[]{:S(2)}) collective-permute-start(bf16[32,4096]{1,0:T(8,128)(2,1)S(1)} %get-tuple-element.199), channel_id=1, source_target_pairs={{0,1},{1,0},{2,3},{3,2},{4,5},{5,4},{6,7},{7,6},{8,9},{9,8},{10,11... | collective-permute-start | bytes 786440 | tf_op jit(solution)/shard_map/ppermute | solution.py:107
  571.1 35.9 %collective-permute-start.64 = (bf16[128,1024]{1,0:T(8,128)(2,1)S(1)}, bf16[128,1024]{1,0:T(8,128)(2,1)S(1)}, u32[]{:S(2)}, u32[]{:S(2)}) collective-permute-start(bf16[128,1024]{1,0:T(8,128)(2,1)S(1)} %get-tuple-element.198), channel_id=1, source_target_pairs={{0,2},{1,3},{2,0},{3,1},{4,6},{5,7},{6,4},{7,5},{8,10},{9,11},{10,... | collective-permute-start | bytes 786440 | tf_op jit(solution)/shard_map/ppermute | solution.py:107
  (141 other events, 1357.2 us)

commit v2 on v0

v2 whole, which is shorter than its diff:
```python
import functools

import jax
import jax.numpy as jnp
from jax import lax
from jax.experimental import pallas as pl
from jax.experimental.pallas import tpu as pltpu
from jax.sharding import PartitionSpec as P

H = 16
HD = 64
AXES = ("dp", "fsdp")
BF = jnp.bfloat16
F32 = jnp.float32
EPSILON = 1e-05
NT = (((1,), (1,)), ((), ()))
TN = (((0,), (0,)), ((), ()))
MASKED = -1e30
LIGHT = pl.CostEstimate(flops=1, bytes_accessed=1, transcendentals=0)
ANY = pl.BlockSpec(memory_space=pl.ANY)


def whole(shape):
    return pl.BlockSpec(shape, lambda *_: (0,) * len(shape))


def struct(shape, dtype):
    return jax.ShapeDtypeStruct(shape, dtype)


def dot(left, right):
    return jnp.dot(left, right, preferred_element_type=F32)


def dot_tn(left, right):
    return lax.dot_general(left, right, TN, preferred_element_type=F32)


def dot_nt(left, right):
    return lax.dot_general(left, right, NT, preferred_element_type=F32)


def tie(value, *after):
    return lax.optimization_barrier((value, *after))[0]


def normalise(rows):
    centred = rows - jnp.mean(rows, axis=-1, keepdims=True)
    spread = jnp.mean(centred * centred, axis=-1, keepdims=True)
    inverse = lax.rsqrt(spread + EPSILON)
    return centred * inverse, inverse


def normalise_back(cotangent, normed, inverse):
    slope = jnp.mean(cotangent * normed, axis=-1, keepdims=True)
    return inverse * (cotangent - jnp.mean(cotangent, axis=-1, keepdims=True) - normed * slope)


def total_rows(matrix):
    return jnp.sum(matrix, axis=0, keepdims=True)


def lane_half(block, which):
    lane = lax.broadcasted_iota(jnp.int32, block.shape, 1)
    return jnp.where((lane >= HD) == (which == 1), block, jnp.zeros_like(block))


def set_mask(seg_ref, mask_ref):
    seg_row = seg_ref[...].astype(F32)
    seg_col = jnp.broadcast_to(seg_row, (128, seg_row.shape[1])).T
    for at in range(0, seg_row.shape[1], 128):
        same = seg_col == seg_row[:, at : at + 128]
        mask_ref[:, at : at + 128] = jnp.where(same, 0.0, MASKED)


def attend_forward_body(seg_ref, q_ref, k_ref, v_ref, mixed_ref, total_ref, mask_ref):
    @pl.when(pl.program_id(1) == 0)
    def _():
        set_mask(seg_ref, mask_ref)

    query = q_ref[...] * jnp.bfloat16(HD**-0.5)
    key = k_ref[...]
    value_t = v_ref[...].T
    halves = []
    for h in range(2):
        scores = lax.dot_general(lane_half(key, h), query, NT, preferred_element_type=F32)
        scores = scores + mask_ref[...]
        high = jnp.max(scores, axis=0, keepdims=True)
        raised = jnp.exp(scores - high)
        total = jnp.sum(raised, axis=0, keepdims=True)
        low = (raised * (1.0 / total)).astype(BF)
        rows = value_t[h * HD : (h + 1) * HD]
        halves.append(jnp.dot(rows, low, preferred_element_type=F32))
        total_ref[0, h : h + 1, :] = high + jnp.log(total)
    mixed_ref[...] = jnp.concatenate(halves, axis=0).T.astype(BF)


def attend_backward_body(
    seg_ref, q_ref, k_ref, v_ref, g_ref, total_ref, *rest
):
    dq_ref, dk_ref, dv_ref, dq_sum_ref, dv_sum_ref, mask_ref = rest[-6:]

    @pl.when(pl.program_id(1) == 0)
    def _():
        set_mask(seg_ref, mask_ref)

    scale = HD**-0.5
    query = q_ref[...] * jnp.bfloat16(scale)
    key, value, grad = k_ref[...], v_ref[...], g_ref[...]
    key_t = key.T
    lane = lax.broadcasted_iota(jnp.int32, key.shape, 1)
    dq_t, dk, dv = [], None, None
    for h in range(2):
        scores = lax.dot_general(lane_half(key, h), query, NT, preferred_element_type=F32)
        probs = jnp.exp(scores + mask_ref[...] - total_ref[0, h : h + 1, :])
        prob_grad = lax.dot_general(lane_half(value, h), grad, NT, preferred_element_type=F32)
        inner_sum = jnp.sum(probs * prob_grad, axis=0, keepdims=True)
        score_grad = (probs * (prob_grad - inner_sum)).astype(BF)
        dv_h = jnp.dot(probs.astype(BF), grad, preferred_element_type=F32)
        dk_h = jnp.dot(score_grad, query, preferred_element_type=F32)
        dv = dv_h if h == 0 else jnp.where(lane < HD, dv, dv_h)
        dk = dk_h if h == 0 else jnp.where(lane < HD, dk, dk_h)
        rows = key_t[h * HD : (h + 1) * HD]
        dq_t.append(jnp.dot(rows, score_grad, preferred_element_type=F32))
    dq = (jnp.concatenate(dq_t, axis=0).T * scale).astype(BF)
    dv = dv.astype(BF)
    dq_ref[...] = dq
    dk_ref[...] = dk.astype(BF)
    dv_ref[...] = dv
    wide = (8, dq.shape[1])
    dq_sum_ref[0] = jnp.broadcast_to(jnp.sum(dq.astype(F32), axis=0, keepdims=True), wide)
    dv_sum_ref[0] = jnp.broadcast_to(jnp.sum(dv.astype(F32), axis=0, keepdims=True), wide)


def attention_specs(seq_len, deps):
    block = pl.BlockSpec((seq_len, 2 * HD), lambda r, n: (r, n))
    seg = pl.BlockSpec((None, 1, seq_len), lambda r, n: (r, 0, 0))
    total = pl.BlockSpec((None, 1, 8, seq_len), lambda r, n: (r, n, 0, 0))
    sums = pl.BlockSpec((1, 8, 2 * HD), lambda r, n: (r, 0, n))
    return block, seg, total, sums, [pl.BlockSpec(memory_space=pl.ANY)] * deps


def attend_forward(seg, queries, keys, values):
    rows, seq_len = seg.shape
    block, seg_spec, total, _, _ = attention_specs(seq_len, 0)
    tokens, width = queries.shape
    pairs = width // (2 * HD)
    return pl.pallas_call(
        attend_forward_body,
        out_shape=[
            jax.ShapeDtypeStruct((tokens, width), BF),
            jax.ShapeDtypeStruct((rows, pairs, 8, seq_len), F32),
        ],
        grid=(rows, pairs),
        in_specs=[seg_spec, block, block, block],
        out_specs=[block, total],
        scratch_shapes=[pltpu.VMEM((seq_len, seq_len), F32)],
        name="attend_forward",
        cost_estimate=LIGHT,
    )(seg.reshape(rows, 1, seq_len), queries, keys, values)


def attend_backward(seg, queries, keys, values, mixed_grad, totals, deps):
    rows, seq_len = seg.shape
    block, seg_spec, total, sums, extra = attention_specs(seq_len, len(deps))
    tokens, width = queries.shape
    pairs = width // (2 * HD)
    outs = pl.pallas_call(
        attend_backward_body,
        out_shape=[jax.ShapeDtypeStruct((tokens, width), BF)] * 3
        + [jax.ShapeDtypeStruct((rows, 8, width), F32)] * 2,
        grid=(rows, pairs),
        in_specs=[seg_spec, block, block, block, block, total] + extra,
        out_specs=[block, block, block, sums, sums],
        scratch_shapes=[pltpu.VMEM((seq_len, seq_len), F32)],
        name="attend_backward",
        cost_estimate=LIGHT,
    )(seg.reshape(rows, 1, seq_len), queries, keys, values, mixed_grad, totals, *deps)
    dq, dk, dv, dq_sum, dv_sum = outs
    return dq, dk, dv, jnp.sum(dq_sum[:, 0], axis=0), jnp.sum(dv_sum[:, 0], axis=0)


class Slice:
    def __init__(self, dp, inner):
        self.inner, self.chips, self.count = inner, dp // 2, dp * inner

    def swap(self, value, mask):
        pairs = [(i, i ^ mask) for i in range(self.count)]
        return lax.ppermute(value, AXES, pairs)

    def across_core(self, value):
        return self.swap(value, self.inner)

    def across_chip(self, value, hop):
        return self.swap(value, hop * 2 * self.inner)

    def place(self):
        me = lax.axis_index(AXES)
        z = me % self.inner
        core = (me // self.inner) % 2
        return me, jnp.stack([me // (2 * self.inner), core, z]).astype(jnp.int32)


def first_shard(matrices, vectors):
    rows = matrices[0].shape[0]
    columns = sum(p.shape[1] for p in matrices)

    def body(*refs):
        out_ref, turn_ref = refs[-2:]
        at = 0
        for ref in refs[: len(matrices)]:
            out_ref[:, at : at + ref.shape[1]] = ref[...]
            at += ref.shape[1]
        turn_ref[...] = jnp.zeros_like(turn_ref)
        row = 0
        for ref in refs[len(matrices) : -2]:
            for start in range(0, ref.shape[1], rows):
                turn_ref[row : row + 1, 0:rows] = ref[:, start : start + rows].astype(F32)
                row += 1
        out_ref[:, at:] = turn_ref[...].T[0:rows].astype(BF)

    return pl.pallas_call(
        body,
        out_shape=struct((rows, columns + 128), BF),
        scratch_shapes=[pltpu.VMEM((128, 128), F32)],
        name="first_shard",
        cost_estimate=LIGHT,
    )(*matrices, *[v.reshape(1, -1) for v in vectors])


def in_z_order(net, parts, ids):
    rows, columns = parts[0].shape
    if rows % 16:
        stacked = jnp.stack(parts)
        return jnp.take(stacked, jnp.arange(net.inner) ^ ids[2], axis=0).reshape(-1, columns)
    tile = next(columns // n for n in (2, 3, 1) if columns % (n * 128) == 0)

    def body(ids_ref, *refs):
        for s, part in enumerate(refs[:-1]):
            row = (ids_ref[2] ^ s) * rows
            refs[-1][pl.ds(pl.multiple_of(row, rows), rows), :] = part[...]

    return pl.pallas_call(
        body,
        out_shape=struct((net.inner * rows, columns), BF),
        grid_spec=pltpu.PrefetchScalarGridSpec(
            num_scalar_prefetch=1,
            grid=(columns // tile,),
            in_specs=[pl.BlockSpec((rows, tile), lambda n, ids: (0, n))] * net.inner,
            out_specs=pl.BlockSpec((net.inner * rows, tile), lambda n, ids: (0, n)),
        ),
        name="in_z_order",
        cost_estimate=LIGHT,
    )(ids, *parts)


class Gather:
    def __init__(self, net, shard, ids, relay, *late):
        self.net, self.ids = net, ids
        self.relayed = relay and net.chips == 4
        self.along = [shard]
        reach = net.inner // 2
        while reach:
            if late and len(self.along) > 1:
                self.along[1:] = [tie(part, *late) for part in self.along[1:]]
            self.along = [
                part
                for near in self.along
                for part in (near, net.swap(near, reach))
            ]
            reach //= 2
        order = [0]
        reach = net.inner // 2
        while reach:
            order = [s ^ far for s in order for far in (0, reach)]
            reach //= 2
        self.along = [self.along[order.index(s)] for s in range(net.inner)]

    def ordered(self, *after):
        parts = list(lax.optimization_barrier((*self.along, *after))[: self.net.inner])
        self.block = in_z_order(self.net, parts, self.ids)
        self.rows = self.block.shape[0]
        return self.block

    def plane(self, *after):
        net = self.net
        self.pieces = [(self.block, 0, 0, 0)]
        hops = range(1, 3 if self.relayed else net.chips)
        sent = tie(self.block, *after)
        self.pieces += [(net.across_chip(sent, j), j, 0, 0) for j in hops]

    def relay(self, *after):
        net = self.net
        if self.relayed:
            half = self.rows // 2
            first, second = self.pieces[1][0], self.pieces[2][0]
            low = net.across_chip(tie(first, second, *after)[:half], 2)
            high = net.across_chip(tie(second, first, *after)[half:], 1)
            self.pieces += [(low, 3, 0, 0), (high, 3, 0, half)]
        return [p for p, _, _, _ in self.pieces]

    def cores(self, *after):
        across = [(self.net.across_core(tie(p, *after)), j, 1, s) for p, j, _, s in self.pieces]
        return Rows(self.net, self.rows, self.pieces + across)


class Rows:
    def __init__(self, net, block, pieces):
        self.block = block
        self.count = net.chips * 2
        self.arrays = [p for p, _, _, _ in pieces]
        self.meta = [(p.shape[0], j, c, s) for p, j, c, s in pieces]

    def after(self, *others):
        again = Rows.__new__(Rows)
        again.block, again.count, again.meta = self.block, self.count, self.meta
        tied = lax.optimization_barrier((*self.arrays, *others))
        again.arrays = list(tied[: len(self.arrays)])
        return again

    def start(self, ids_ref, refs, column, target, at, width, sems):
        for ref, (rows, j, c, s) in zip(refs, self.meta):
            block = (ids_ref[0] ^ j) * 2 + (ids_ref[1] ^ c)
            row = pl.multiple_of(block * self.block + s, 16)
            pltpu.make_async_copy(
                ref.at[:, pl.ds(column, width)],
                target.at[pl.ds(row, rows), pl.ds(at, width)],
                sems.at[block],
            ).start()

    def wait(self, block, target, at, width, sems):
        row = block * self.block
        if not isinstance(row, int):
            row = pl.multiple_of(row, 16)
        there = target.at[pl.ds(row, self.block), pl.ds(at, width)]
        pltpu.make_async_copy(there, there, sems.at[block]).wait()

    def wait_all(self, target, at, width, sems):
        for block in range(self.count):
            self.wait(block, target, at, width, sems)


def kernel(body, name, ids, grid, operands, outs, scratch):
    return pl.pallas_call(
        body,
        out_shape=[o for o, _ in outs],
        grid_spec=pltpu.PrefetchScalarGridSpec(
            num_scalar_prefetch=1,
            grid=grid,
            in_specs=[s for _, s in operands],
            out_specs=[s for _, s in outs],
            scratch_shapes=scratch,
        ),
        name=name,
        cost_estimate=LIGHT,
    )(ids, *[o for o, _ in operands])


def project(ids, tokens, weights):
    count, width = tokens.shape
    tile = 512
    per = width // tile
    n_pieces = len(weights.arrays)

    def body(ids_ref, x_ref, *refs):
        pieces = refs[:n_pieces]
        outs = refs[n_pieces : n_pieces + 3]
        vec_ref, w_ref, s_ref, sems = refs[n_pieces + 3 :]
        step = pl.program_id(0)

        @pl.when(step == 0)
        def _():
            weights.start(ids_ref, pieces, 4 * width, s_ref, 0, 128, sems.at[3])
            for i in range(3):
                weights.start(ids_ref, pieces, i * width, w_ref, i * width, width, sems.at[i])
            weights.wait_all(s_ref, 0, 128, sems.at[3])
            vec_ref[...] = s_ref[...].astype(F32).T[0 : vec_ref.shape[0]]

        for i, row in enumerate((0, None, 1)):

            @pl.when(step == i * per)
            def _():
                weights.wait_all(w_ref, i * width, width, sems.at[i])

            @pl.when((step >= i * per) & (step < (i + 1) * per))
            def _():
                columns = pl.ds(pl.multiple_of(step * tile, tile), tile)
                out = dot(x_ref[...], w_ref[:, columns])
                if row is not None:
                    inside = pl.ds(pl.multiple_of((step - i * per) * tile, tile), tile)
                    out = out + vec_ref[row : row + 1, inside]
                outs[i][...] = out.astype(BF)

    def out_spec(i):
        return pl.BlockSpec((count, tile), lambda n, ids: (0, jnp.clip(n - i * per, 0, per - 1)))

    return kernel(
        body,
        "project",
        ids,
        (3 * per,),
        [(tokens, whole(tokens.shape))] + [(p, ANY) for p in weights.arrays],
        [(struct(tokens.shape, BF), out_spec(i)) for i in range(3)]
        + [(struct((16, width), F32), whole((16, width)))],
        [
            pltpu.VMEM((width, 3 * width), BF),
            pltpu.VMEM((width, 128), BF),
            pltpu.SemaphoreType.DMA((4, weights.count)),
        ],
    )


def close_attention(ids, mixed, tokens, weights, vectors):
    count, width = tokens.shape
    rows = 256
    n_pieces = len(weights.arrays)

    def body(ids_ref, m_ref, x_ref, vec_ref, *refs):
        pieces = refs[:n_pieces]
        normed_ref, inverse_ref, low_ref, w_ref, sems = refs[n_pieces:]

        @pl.when(pl.program_id(0) == 0)
        def _():
            weights.start(ids_ref, pieces, 3 * width, w_ref, 0, width, sems)
            weights.wait_all(w_ref, 0, width, sems)

        total = x_ref[...].astype(F32) + (dot(m_ref[...], w_ref[...]) + vec_ref[2:3])
        normed, inverse = normalise(total)
        normed_ref[...] = normed
        inverse_ref[...] = jnp.broadcast_to(inverse, inverse_ref.shape)
        low_ref[...] = (normed * vec_ref[3:4] + vec_ref[4:5]).astype(BF)

    block = pl.BlockSpec((rows, width), lambda n, ids: (n, 0))
    return kernel(
        body,
        "close_attention",
        ids,
        (count // rows,),
        [(mixed, block), (tokens, block), (vectors, whole(vectors.shape))]
        + [(p, ANY) for p in weights.arrays],
        [
            (struct((count, width), F32), block),
            (struct((count, 128), F32), pl.BlockSpec((rows, 128), lambda n, ids: (n, 0))),
            (struct((count, width), BF), block),
        ],
        [pltpu.VMEM((width, width), BF), pltpu.SemaphoreType.DMA((weights.count,))],
    )


def ffn_in(ids, low, weights, bias):
    count, width = low.shape
    wide = bias.shape[1]
    tile = 1024
    n_pieces = len(weights.arrays)

    def body(ids_ref, x_ref, bias_ref, *refs):
        pieces = refs[:n_pieces]
        act_ref, slope_ref, w_ref, sems = refs[n_pieces:]
        step = pl.program_id(0)

        @pl.when(step == 0)
        def _():
            for g in range(wide // tile):
                weights.start(ids_ref, pieces, g * tile, w_ref.at[g], 0, tile, sems.at[g])

        weights.wait_all(w_ref.at[step], 0, tile, sems.at[step])
        for at in range(0, tile, 512):
            columns = slice(at, at + 512)
            pre = dot(x_ref[...], w_ref[step, :, columns]) + bias_ref[:, columns]
            below = 0.5 + 0.5 * lax.erf(pre * (0.5**0.5))
            density = jnp.exp(pre * pre * -0.5) * 0.3989422804014327
            act_ref[:, columns] = (pre * below).astype(BF)
            slope_ref[:, columns] = below + pre * density

    block = pl.BlockSpec((count, tile), lambda n, ids: (0, n))
    return kernel(
        body,
        "ffn_in",
        ids,
        (wide // tile,),
        [(low, whole(low.shape)), (bias, pl.BlockSpec((1, tile), lambda n, ids: (0, n)))]
        + [(p, ANY) for p in weights.arrays],
        [(struct((count, wide), BF), block), (struct((count, wide), F32), block)],
        [
            pltpu.VMEM((wide // tile, width, tile), BF),
            pltpu.SemaphoreType.DMA((wide // tile, weights.count)),
        ],
    )


def ffn_out(ids, act, normed, out_grad, weights, vectors):
    count, wide = act.shape
    width = normed.shape[1]
    n_pieces = len(weights.arrays)

    def body(ids_ref, act_ref, n_ref, g_ref, vec_ref, *refs):
        pieces = refs[:n_pieces]
        out_ref, sum_ref, low_ref, sums_ref, acc_ref, w_ref, sems = refs[n_pieces:]
        tile = 256
        for i in range(width // tile):
            weights.start(ids_ref, pieces, i * tile, w_ref, i * tile, tile, sems.at[i])
        for i in range(width // tile):
            part = slice(i * tile, (i + 1) * tile)
            start = n_ref[:, part] * vec_ref[3:4, part] + vec_ref[4:5, part] + vec_ref[5:6, part]
            weights.wait_all(w_ref, i * tile, tile, sems.at[i])
            acc_ref[:, part] = start + dot(act_ref[...], w_ref[:, part])
        n2, inverse = normalise(acc_ref[...])
        out_ref[...] = (n2 * vec_ref[6:7] + vec_ref[7:8]).astype(BF)
        grad = g_ref[...].astype(F32)
        back = normalise_back(grad * vec_ref[6:7], n2, inverse)
        low = back.astype(BF)
        sum_ref[...] = back
        low_ref[...] = low
        sums_ref[0:1, :] = total_rows(grad * n2)
        sums_ref[1:2, :] = total_rows(grad)
        sums_ref[2:3, :] = total_rows(low.astype(F32))

    size = (count, width)
    return kernel(
        body,
        "ffn_out",
        ids,
        (1,),
        [
            (act, whole(act.shape)),
            (normed, whole(size)),
            (out_grad, whole(size)),
            (vectors, whole(vectors.shape)),
        ]
        + [(p, ANY) for p in weights.arrays],
        [
            (struct(size, BF), whole(size)),
            (struct(size, F32), whole(size)),
            (struct(size, BF), whole(size)),
            (struct((8, width), F32), whole((8, width))),
        ],
        [
            pltpu.VMEM(size, F32),
            pltpu.VMEM((wide, width), BF),
            pltpu.SemaphoreType.DMA((width // 256, weights.count)),
        ],
    )


def ffn_back(ids, grad, slope, weights, deps):
    count, wide = slope.shape
    width = grad.shape[1]
    block = min(wide, 1024)
    per = block // weights.block
    n_pieces = len(weights.arrays)

    def body(ids_ref, grad_ref, slope_ref, *refs):
        pieces = refs[:n_pieces]
        out_ref, sums_ref, w_ref, sems = refs[-4:]
        step = pl.program_id(0)

        @pl.when(step == 0)
        def _():
            weights.start(ids_ref, pieces, 0, w_ref, 0, width, sems)

        for i in range(per):
            weights.wait(step * per + i, w_ref, 0, width, sems)
        rows = pl.ds(pl.multiple_of(step * block, 16), block)
        back = (dot_nt(grad_ref[...], w_ref[rows, :]) * slope_ref[...]).astype(BF)
        out_ref[...] = back
        sums_ref[...] = jnp.broadcast_to(total_rows(back.astype(F32)), sums_ref.shape)

    tile = pl.BlockSpec((count, block), lambda n, ids: (0, n))
    return kernel(
        body,
        "ffn_back",
        ids,
        (wide // block,),
        [(grad, whole(grad.shape)), (slope, tile)]
        + [(p, ANY) for p in weights.arrays]
        + [(d, ANY) for d in deps],
        [
            (struct((count, wide), BF), tile),
            (struct((8, wide), F32), pl.BlockSpec((8, block), lambda n, ids: (0, n))),
        ],
        [pltpu.VMEM((wide, width), BF), pltpu.SemaphoreType.DMA((weights.count,))],
    )


def attention_norm_back(ids, inner_grad, ffn_grad, normed, inverse, inner, weights, vectors, deps):
    count, wide = inner_grad.shape
    width = normed.shape[1]
    tile = 256
    steps = width // tile
    per = tile // inner.block
    n_pieces = len(weights.arrays)

    def body(ids_ref, grad_ref, ffn_ref, n_ref, inverse_ref, vec_ref, *refs):
        pieces = refs[:n_pieces]
        inner_pieces = refs[n_pieces : 2 * n_pieces]
        low_ref, sum_ref, mixed_ref, sums_ref, acc_ref, w_ref, w_sems, o_ref, o_sems = refs[-9:]
        step = pl.program_id(0)

        @pl.when(step == 0)
        def _():
            inner.start(ids_ref, inner_pieces, 0, w_ref, 0, wide, w_sems)
            weights.start(ids_ref, pieces, 3 * width, o_ref, 0, width, o_sems)

        for i in range(per):
            inner.wait(step * per + i, w_ref, 0, wide, w_sems)
        place = pl.ds(pl.multiple_of(step * tile, tile), tile)
        acc_ref[:, place] = ffn_ref[...] + dot_nt(grad_ref[...], w_ref[place, :])

        @pl.when(step == steps - 1)
        def _():
            grad = acc_ref[...]
            normed_rows = n_ref[...]
            back = normalise_back(grad * vec_ref[3:4], normed_rows, inverse_ref[:, 0:1])
            low = back.astype(BF)
            low_ref[...] = low
            sum_ref[...] = back
            sums_ref[0:1, :] = total_rows(grad * normed_rows)
            sums_ref[1:2, :] = total_rows(grad)
            sums_ref[2:3, :] = total_rows(low.astype(F32))
            weights.wait_all(o_ref, 0, width, o_sems)
            mixed_ref[...] = dot_nt(low, o_ref[...]).astype(BF)

    size = (count, width)
    return kernel(
        body,
        "attention_norm_back",
        ids,
        (steps,),
        [
            (inner_grad, whole(inner_grad.shape)),
            (ffn_grad, pl.BlockSpec((count, tile), lambda n, ids: (0, n))),
            (normed, whole(size)),
            (inverse, whole(inverse.shape)),
            (vectors, whole(vectors.shape)),
        ]
        + [(p, ANY) for p in weights.arrays + inner.arrays]
        + [(d, ANY) for d in deps],
        [
            (struct(size, BF), whole(size)),
            (struct(size, F32), whole(size)),
            (struct(size, BF), whole(size)),
            (struct((8, width), F32), whole((8, width))),
        ],
        [
            pltpu.VMEM(size, F32),
            pltpu.VMEM((width, wide), BF),
            pltpu.SemaphoreType.DMA((weights.count,)),
            pltpu.VMEM((width, width), BF),
            pltpu.SemaphoreType.DMA((weights.count,)),
        ],
    )


def inputs_back(ids, base, grads, weights, deps):
    count, width = base.shape
    tile = 256
    per = tile // weights.block
    n_pieces = len(weights.arrays)

    def body(ids_ref, base_ref, q_ref, k_ref, v_ref, *refs):
        pieces = refs[:n_pieces]
        out_ref, w_ref, sems = refs[-3:]
        step = pl.program_id(0)

        @pl.when(step == 0)
        def _():
            weights.start(ids_ref, pieces, 0, w_ref, 0, 3 * width, sems)

        for i in range(per):
            weights.wait(step * per + i, w_ref, 0, 3 * width, sems)
        place = pl.ds(pl.multiple_of(step * tile, tile), tile)
        out = base_ref[...]
        for i, ref in enumerate((q_ref, k_ref, v_ref)):
            out = out + dot_nt(ref[...], w_ref[place, i * width : (i + 1) * width])
        out_ref[...] = out

    block = pl.BlockSpec((count, tile), lambda n, ids: (0, n))
    return kernel(
        body,
        "inputs_back",
        ids,
        (width // tile,),
        [(base, block)]
        + [(g, whole(g.shape)) for g in grads]
        + [(p, ANY) for p in weights.arrays]
        + [(d, ANY) for d in deps],
        [(struct(base.shape, F32), block)],
        [pltpu.VMEM((width, 3 * width), BF), pltpu.SemaphoreType.DMA((weights.count,))],
    )[0]


def split_hops(kept, bit):
    stay = [j for j in kept if not j & bit]
    return stay, [j | bit for j in stay]


class RowSum:
    def __init__(self, net, pairs, ids, tile):
        self.net, self.ids, self.tile = net, ids, tile
        self.rights = [right for _, right in pairs]
        self.left = []
        for left, _ in pairs:
            if not any(left is known for known in self.left):
                self.left.append(left)
        self.uses = [[left is known for known in self.left].index(True) for left, _ in pairs]
        self.width = self.left[0].shape[1] // (net.chips * 2)
        self.columns = sum(r.shape[1] for r in self.rights)
        bits = [1 << b for b in range(net.chips.bit_length() - 1)]
        self.bits = (bits, bits[::-1])
        self.kept = [list(range(net.chips))] * 2

    def lefts(self, core):
        net, width = self.net, self.width
        if width % 128 == 0:
            spec = [
                pl.BlockSpec(
                    (self.left[0].shape[0], width),
                    lambda n, ids, j=j: (0, (ids[0] ^ j) * 2 + (ids[1] ^ core)),
                )
                for j in range(net.chips)
            ]
            return [left for left in self.left for _ in spec], spec * len(self.left)
        chosen = []
        for left in self.left:
            picked = []
            for j in range(net.chips):
                at = ((self.ids[0] ^ j) * 2 + (self.ids[1] ^ core)) * width
                picked.append(lax.dynamic_slice_in_dim(left, at, width, axis=1))
            chosen.append(jnp.concatenate(picked, axis=1))
        return chosen, [whole(picked.shape) for picked in chosen]

    def right_specs(self):
        specs, lo = [], 0
        for right in self.rights:
            count = right.shape[1] // self.tile
            specs.append(
                pl.BlockSpec(
                    (right.shape[0], self.tile),
                    lambda n, ids, lo=lo, c=count: (0, jnp.clip(n - lo, 0, c - 1)),
                )
            )
            lo += count
        return specs

    def product(self, left_refs, right_refs, step, then):
        each = len(left_refs) // len(self.left)
        lo = 0
        for ref, right, use in zip(right_refs, self.rights, self.uses):
            count = right.shape[1] // self.tile

            @pl.when((step >= lo) & (step < lo + count))
            def _():
                left = [part[...] for part in left_refs[use * each : (use + 1) * each]]
                if each > 1 and self.width < 512:
                    left = [jnp.concatenate(left, axis=1)]
                for i, part in enumerate(left):
                    then(i * part.shape[1], dot_tn(part, ref[...]))

            lo += count

    def other_core(self, *deps):
        lefts, left_specs = self.lefts(1)
        rows = self.net.chips * self.width

        def body(ids_ref, *refs):
            out_ref = refs[-1]

            def store(at, value):
                out_ref[at : at + value.shape[0], :] = value.astype(BF)

            self.product(
                refs[: len(lefts)],
                refs[len(lefts) : len(lefts) + len(self.rights)],
                pl.program_id(0),
                store,
            )

        (self.sent,) = kernel(
            body,
            "rows_of_other_core",
            self.ids,
            (self.columns // self.tile,),
            list(zip(lefts + self.rights, left_specs + self.right_specs()))
            + [(d, ANY) for d in deps],
            [
                (
                    struct((rows, self.columns), BF),
                    pl.BlockSpec((rows, self.tile), lambda n, ids: (0, n)),
                )
            ],
            [],
        )
        self.got = self.net.across_core(self.sent)
        return self.sent

    def own_core(self, *deps):
        lefts, left_specs = self.lefts(0)
        rows, tile = self.net.chips * self.width, self.tile
        steps = self.columns // tile
        half = steps // 2
        sides = [split_hops(self.kept[s], self.bits[s][0]) for s in range(2)]

        def body(ids_ref, *refs):
            got_ref = refs[len(lefts) + len(self.rights)]
            out_refs = refs[-4:]
            step = pl.program_id(0)

            def store(at, value):
                value = (value + got_ref[at : at + value.shape[0], :].astype(F32)).astype(BF)
                for side in range(2):

                    @pl.when((step >= side * half) & (step < (side + 1) * half))
                    def _():
                        for which, hops in enumerate(sides[side]):
                            for i, j in enumerate(hops):
                                row = j * self.width - at
                                if 0 <= row < value.shape[0]:
                                    out_refs[side * 2 + which][
                                        i * self.width : (i + 1) * self.width, :
                                    ] = value[row : row + self.width]

            self.product(
                refs[: len(lefts)],
                refs[len(lefts) : len(lefts) + len(self.rights)],
                step,
                store,
            )

        outs = []
        for side in range(2):
            spec = pl.BlockSpec(
                (rows // 2, tile),
                lambda n, ids, side=side: (0, jnp.clip(n - side * half, 0, half - 1)),
            )
            outs += [(struct((rows // 2, self.columns // 2), BF), spec)] * 2
        out = kernel(
            body,
            "rows_of_own_core",
            self.ids,
            (steps,),
            list(zip(lefts + self.rights, left_specs + self.right_specs()))
            + [(self.got, pl.BlockSpec((rows, tile), lambda n, ids: (0, n)))]
            + [(d, ANY) for d in deps],
            outs,
            [],
        )
        self.held = [out[0], out[2]]
        self.away = [out[1], out[3]]
        self.send()
        return out[0]

    def send(self):
        for s in range(2):
            self.kept[s] = split_hops(self.kept[s], self.bits[s][0])[0]
        self.arrived = [self.net.across_chip(self.away[s], self.bits[s][0]) for s in range(2)]
        self.bits = (self.bits[0][1:], self.bits[1][1:])

    def fold(self, *deps):
        rows, columns = self.held[0].shape
        tile = columns // 2
        sides = [split_hops(self.kept[s], self.bits[s][0]) for s in range(2)]

        def body(ids_ref, *refs):
            out_refs = refs[-4:]
            for s in range(2):
                for which, hops in enumerate(sides[s]):
                    for i, j in enumerate(hops):
                        at = self.kept[s].index(j) * self.width
                        part = slice(at, at + self.width)
                        value = refs[2 * s][part, :].astype(F32) + refs[2 * s + 1][part, :].astype(F32)
                        out_refs[2 * s + which][i * self.width : (i + 1) * self.width, :] = (
                            value.astype(BF)
                        )

        block = pl.BlockSpec((rows, tile), lambda n, ids: (0, n))
        half = pl.BlockSpec((rows // 2, tile), lambda n, ids: (0, n))
        out = kernel(
            body,
            "fold",
            self.ids,
            (columns // tile,),
            [(a, block) for s in range(2) for a in (self.held[s], self.arrived[s])]
            + [(d, ANY) for d in deps],
            [(struct((rows // 2, columns), BF), half)] * 4,
            [],
        )
        self.held = [out[0], out[2]]
        self.away = [out[1], out[3]]
        self.send()
        return self.fold() if self.bits[0] else out[0]

    def fold_z(self, *deps):
        net, count = self.net, self.net.inner
        columns = self.held[0].shape[1]
        rows = self.width // count
        stay, leave = split_hops(list(range(count)), 1)
        size = (rows * len(stay), 2 * columns)
        if rows % 16:
            held = tie(jnp.concatenate(self.held, axis=1), *deps).astype(F32)
            held = held + jnp.concatenate(self.arrived, axis=1).astype(F32)
            held = held.reshape(count, rows, -1).astype(BF)
            keep, away = (
                jnp.take(held, jnp.array(hops) ^ self.ids[2], axis=0).reshape(size)
                for hops in (stay, leave)
            )
        else:

            def body(ids_ref, *refs):
                for out_ref, hops in zip(refs[-2:], (stay, leave)):
                    for i, s in enumerate(hops):
                        at = pl.ds(pl.multiple_of((ids_ref[2] ^ s) * rows, 16), rows)
                        for side in range(2):
                            value = refs[2 * side][at, :].astype(F32)
                            value = value + refs[2 * side + 1][at, :].astype(F32)
                            place = slice(side * columns, (side + 1) * columns)
                            out_ref[i * rows : (i + 1) * rows, place] = value.astype(BF)

            keep, away = kernel(
                body,
                "fold_z",
                self.ids,
                (1,),
                [
                    (a, whole(a.shape))
                    for s in range(2)
                    for a in (self.held[s], self.arrived[s])
                ]
                + [(d, ANY) for d in deps],
                [(struct(size, BF), whole(size))] * 2,
                [],
            )
        self.total, self.came, self.reach = keep, net.swap(away, 1), 1
        return keep

    def fold_far(self, *deps):
        while self.reach * 2 < self.net.inner:
            self.reach *= 2
            total = tie(self.total, *deps).astype(F32) + self.came.astype(F32)
            rows = self.width // self.net.inner
            count = total.shape[0] // rows
            stay = [i for i in range(count) if not i & 1]
            blocks = total.reshape(count, rows, -1)
            away = jnp.concatenate([blocks[i + 1] for i in stay], axis=0).astype(BF)
            self.total = jnp.concatenate([blocks[i] for i in stay], axis=0)
            self.came = self.net.swap(away, self.reach)
        return self.came

    def finish(self, *deps):
        return tie(self.total, *deps).astype(F32) + self.came.astype(F32)


def shards(
    net,
    inputs,
    segment_ids,
    query_weight,
    key_weight,
    value_weight,
    output_weight,
    query_bias,
    value_bias,
    output_bias,
    attn_gain,
    attn_shift,
    inner_weight,
    inner_bias,
    outer_weight,
    outer_bias,
    ffn_gain,
    ffn_shift,
    out_grad,
):
    row_count, seq_len, width = inputs.shape
    tokens = inputs.reshape(row_count * seq_len, width)
    _, ids = net.place()
    small = [
        query_bias,
        value_bias,
        output_bias,
        attn_gain,
        attn_shift,
        outer_bias,
        ffn_gain,
        ffn_shift,
        inner_bias,
    ]
    mine = query_bias.shape[0]
    shard = first_shard([query_weight, key_weight, value_weight, output_weight], small)
    gather_a = Gather(net, shard, ids, True)
    gather_a.ordered()
    gather_a.plane()
    gather_b = Gather(net, tie(inner_weight, gather_a.block), ids, True)
    arrived = gather_a.relay(*gather_b.along)
    weights_a = gather_a.cores()
    gather_b.ordered(*arrived)
    gather_b.plane(*weights_a.arrays)
    queries, keys, values, vectors = project(ids, tokens, weights_a)
    gather_c = Gather(
        net, tie(outer_weight, gather_b.block, *weights_a.arrays), ids, True, queries
    )
    spread = inner_bias.shape[0] // mine
    inner_bias_full = vectors[8 : 8 + spread].reshape(spread, net.count, mine)
    inner_bias_full = inner_bias_full.swapaxes(0, 1).reshape(1, -1)
    mixed, totals = attend_forward(segment_ids, queries, keys, values)
    arrived = gather_b.relay(mixed, *gather_c.along)
    weights_b = gather_b.cores()
    gather_c.ordered(*arrived)
    gather_c.plane()
    normed, inverse, normed_low = close_attention(ids, mixed, tokens, weights_a, vectors)
    act, slope = ffn_in(ids, normed_low, weights_b, inner_bias_full)
    gather_c.relay(act)
    weights_c = gather_c.cores()
    grad_out = out_grad.reshape(tokens.shape)
    outputs, ffn_grad, branch_grad, ffn_sums = ffn_out(
        ids, act, normed, grad_out, weights_c, vectors
    )
    outer_sum = RowSum(net, [(act, branch_grad)], ids, 512)
    last = outer_sum.other_core()
    inner_grad, inner_sums = ffn_back(ids, branch_grad, slope, weights_c, [last])
    last = outer_sum.own_core(inner_grad)
    inner_sum = RowSum(net, [(normed_low, inner_grad)], ids, 1024)
    last = inner_sum.other_core(last)
    attn_grad, attn_sum_grad, mixed_grad, attn_sums = attention_norm_back(
        ids, inner_grad, ffn_grad, normed, inverse, weights_b, weights_a, vectors, [last]
    )
    last = outer_sum.fold(attn_grad)
    last = inner_sum.own_core(last)
    query_grad, key_grad, value_grad, grad_query_bias, grad_value_bias = attend_backward(
        segment_ids, queries, keys, values, mixed_grad, totals, [last]
    )
    inputs_sum = RowSum(
        net,
        [(mixed, attn_grad)] + [(tokens, g) for g in (query_grad, key_grad, value_grad)],
        ids,
        1024,
    )
    last = inputs_sum.other_core(*outer_sum.arrived, *inner_sum.arrived)
    last = inner_sum.fold(last)
    last = outer_sum.fold_z(last)
    last = inputs_sum.own_core(last)
    outer_sum.fold_far(last)
    last = inner_sum.fold_z(last)
    input_grad = inputs_back(
        ids, attn_sum_grad, (query_grad, key_grad, value_grad), weights_a, [last, outer_sum.came]
    )
    shard_outer = outer_sum.finish(input_grad)
    last = inputs_sum.fold(input_grad)
    inner_sum.fold_far(last)
    last = inputs_sum.fold_z(inner_sum.came)
    shard_inner = inner_sum.finish(last)
    inputs_sum.fold_far(last)
    shard_inputs = inputs_sum.finish()
    shard_output, shard_query, shard_key, shard_value = (
        shard_inputs[:, i * width : (i + 1) * width] for i in range(4)
    )
    rows = jnp.concatenate(
        [grad_query_bias[None], grad_value_bias[None], attn_sums[:3], ffn_sums[:3]], axis=0
    )
    rows = rows.reshape(8, net.count, mine).swapaxes(0, 1).reshape(net.count, 8 * mine)
    packed = jnp.concatenate([rows, inner_sums[0].reshape(net.count, -1)], axis=1)
    packed = tie(packed, last)
    summed = jnp.sum(lax.all_to_all(packed, AXES, 0, 0, tiled=True), axis=0)
    vector = [summed[i * mine : (i + 1) * mine] for i in range(8)]
    return (
        outputs.reshape(inputs.shape),
        input_grad.reshape(inputs.shape),
        shard_query,
        shard_key,
        shard_value,
        shard_output,
        vector[0],
        vector[1],
        vector[4],
        vector[2],
        vector[3],
        shard_inner,
        summed[8 * mine :],
        shard_outer,
        vector[7],
        vector[5],
        vector[6],
    )


def solution(mesh):
    placed = (
        P(("dp", "fsdp"), None, None),
        P(("dp", "fsdp"), None),
        P(("dp", "fsdp"), None),
        P(("dp", "fsdp"), None),
        P(("dp", "fsdp"), None),
        P(("dp", "fsdp"), None),
        P(("dp", "fsdp")),
        P(("dp", "fsdp")),
        P(("dp", "fsdp")),
        P(("dp", "fsdp")),
        P(("dp", "fsdp")),
        P(("dp", "fsdp"), None),
        P(("dp", "fsdp")),
        P(("dp", "fsdp"), None),
        P(("dp", "fsdp")),
        P(("dp", "fsdp")),
        P(("dp", "fsdp")),
        P(("dp", "fsdp"), None, None),
    )
    return jax.shard_map(
        functools.partial(shards, Slice(mesh.shape["dp"], mesh.shape["fsdp"])),
        mesh=mesh,
        in_specs=placed,
        out_specs=(
            P(("dp", "fsdp"), None, None),
            P(("dp", "fsdp"), None, None),
            P(("dp", "fsdp"), None),
            P(("dp", "fsdp"), None),
            P(("dp", "fsdp"), None),
            P(("dp", "fsdp"), None),
            P(("dp", "fsdp")),
            P(("dp", "fsdp")),
            P(("dp", "fsdp")),
            P(("dp", "fsdp")),
            P(("dp", "fsdp")),
            P(("dp", "fsdp"), None),
            P(("dp", "fsdp")),
            P(("dp", "fsdp"), None),
            P(("dp", "fsdp")),
            P(("dp", "fsdp")),
            P(("dp", "fsdp")),
        ),
        check_vma=False,
    )
```

time: 1840 us -> 430 us (0.23)
  waiting for transfers between devices: 1440 us -> 129 us
  Pallas kernels: 0 us -> 200 us
  matrix products: 157 us -> 0 us
  blocking collectives: 149 us -> 0 us
  starting transfers between devices: 0.47 us -> 63.2 us
  local copies, waits for them, and re-layouts: 51.7 us -> 22.5 us
    reduce_scatter x3 -> x0, waiting for transfers between devices: 880 us -> none  [the longest x1 366 us: shards(): lax.psum_scatter(ffn_terms[0], ('dp', 'fsdp'), scatter_dimension=0, tiled...]
    unnamed x15 -> x0, waiting for transfers between devices: 345 us -> none
    all_gather x6 -> x0, waiting for transfers between devices: 212 us -> none  [the longest x1 73.9 us: shards(): lax.all_gather(inner_weight, ('dp', 'fsdp'), axis=0, tiled=True)]
    pallas_call x0 -> x25, Pallas kernels: none -> 200 us  [the longest x19 158 us: kernel(): pl.pallas_call(body, out_shape=[o for o, _ in outs], grid_spec=pltpu.Pref...]
    dot_general x46 -> x0, matrix products: 157 us -> none  [the longest x6 52.4 us: matmul(): return jnp.dot(left, right, preferred_element_type=jnp.float32)]
    ppermute x0 -> x57, waiting for transfers between devices: none -> 128 us  [swap(): return lax.ppermute(value, AXES, pairs)]
    unnamed x2 -> x0, blocking collectives: 83 us -> none
    all_gather x1 -> x0, blocking collectives: 65.7 us -> none  [shards(): lax.all_gather(inner_bias, ('dp', 'fsdp'), axis=0, tiled=True)]
  transfers between devices with their start and end apart: 12 -> 58, of which waited for: 10 -> 24; matrix products, arithmetic and copies ran while one was open for 7% -> 4% of each run, Pallas kernels for 0% -> 32%
where the time goes in v2:
time: 430 us; the launch traced here: 422 us
  Pallas kernels  200 us (47%)
  waiting for transfers between devices  129 us (30%)
  starting transfers between devices  63.2 us (15%)
  local copies, waits for them, and re-layouts  22.5 us (5%)
  other arithmetic  5.56 us (1%)
    pallas_call x19, Pallas kernels, kernel(): pl.pallas_call(body, out_shape=[o for o, _ in outs], grid_spec=pltpu.Pref...  158 us
    ppermute x57, waiting for transfers between devices, swap(): return lax.ppermute(value, AXES, pairs)  128 us
    ppermute x57, starting transfers between devices, swap(): return lax.ppermute(value, AXES, pairs)  59.1 us
    pallas_call x1, Pallas kernels, attend_backward(): pl.pallas_call(attend_backward_body, out_shape=[jax.ShapeDtypeStruct((tok...  17 us
    pallas_call x1, Pallas kernels, attend_forward(): pl.pallas_call(attend_forward_body, out_shape=[jax.ShapeDtypeStruct((toke...  12.8 us
    unnamed x88, local copies, waits for them, and re-layouts  10.6 us
    pallas_call x3, Pallas kernels, in_z_order(): pl.pallas_call(body, out_shape=struct((net.inner * rows, columns), BF), g...  9.53 us
  transfers between devices with their start and end apart: 58, of which 24 were waited for; matrix products, arithmetic and copies ran while one was open for 4% of the time, Pallas kernels for 32%

profile of v2, /device:TPU:0, one launch (start us, length us, event | category | flops | bytes accessed | tf_op | source)
XLA Modules:
  0.0 421.7 jit_solution(16270019329550743532)
XLA Ops:
  2.6 4.0 collective-permute-start.1
  8.2 11.0 %collective-permute-done.1.refs_2_ = bf16[32,4224]{1,0:T(8,128)(2,1)S(1)} collective-permute-done((bf16[32,4224]{1,0:T(8,128)(2,1)}, bf16[32,4224]{1,0:T(8,128)(2,1)S(1)}, u32[]{:S(2)}, u32[]{:S(2)}) %collective-permute-start.1) | collective-permute-done | bytes 270368 | tf_op jit(solution)/shard_map/ppermute | solution.py:189
  20.5 6.3 %collective-permute-done.2.refs_3_ = bf16[32,4224]{1,0:T(8,128)(2,1)S(1)} collective-permute-done((bf16[32,4224]{1,0:T(8,128)(2,1)S(1)}, bf16[32,4224]{1,0:T(8,128)(2,1)S(1)}, u32[]{:S(2)}, u32[]{:S(2)}) %collective-permute-start.2) | collective-permute-done | bytes 270368 | tf_op jit(solution)/shard_map/ppermute | solution.py:189
  39.2 9.4 %collective-permute-done.6.refs_2_ = bf16[32,4096]{1,0:T(8,128)(2,1)S(1)} collective-permute-done((bf16[32,4096]{1,0:T(8,128)(2,1)S(1)}, bf16[32,4096]{1,0:T(8,128)(2,1)S(1)}, u32[]{:S(2)}, u32[]{:S(2)}) %collective-permute-start.6) | collective-permute-done | bytes 262176 | tf_op jit(solution)/shard_map/ppermute | solution.py:189
  49.1 6.6 %collective-permute-done.7.refs_3_ = bf16[32,4096]{1,0:T(8,128)(2,1)S(1)} collective-permute-done((bf16[32,4096]{1,0:T(8,128)(2,1)S(1)}, bf16[32,4096]{1,0:T(8,128)(2,1)S(1)}, u32[]{:S(2)}, u32[]{:S(2)}) %collective-permute-start.7) | collective-permute-done | bytes 262176 | tf_op jit(solution)/shard_map/ppermute | solution.py:189
  59.5 9.5 %collective-permute-done.9.refs_4_ = bf16[64,4224]{1,0:T(8,128)(2,1)} collective-permute-done((bf16[64,4224]{1,0:T(8,128)(2,1)S(1)}, bf16[64,4224]{1,0:T(8,128)(2,1)}, u32[]{:S(2)}, u32[]{:S(2)}) %collective-permute-start.9) | collective-permute-done | bytes 540704 | tf_op jit(solution)/shard_map/ppermute | solution.py:189
  78.4 4.3 %collective-permute-start.18 = (bf16[128,1024]{1,0:T(8,128)(2,1)}, bf16[128,1024]{1,0:T(8,128)(2,1)S(1)}, u32[]{:S(2)}, u32[]{:S(2)}) collective-permute-start(bf16[128,1024]{1,0:T(8,128)(2,1)} %refs_0_.3), channel_id=1, source_target_pairs={{0,2},{1,3},{2,0},{3,1},{4,6},{5,7},{6,4},{7,5},{8,10},{9,11},{10,... | collective-permute-start | bytes 786440 | tf_op jit(solution)/shard_map/ppermute | solution.py:189
  84.1 10.0 %project.1 = (bf16[512,1024]{1,0:T(8,128)(2,1)}, bf16[512,1024]{1,0:T(8,128)(2,1)}, bf16[512,1024]{1,0:T(8,128)(2,1)}, f32[16,1024]{1,0:T(8,128)}) custom-call(s32[3]{0:T(128)} %pad_add_fusion.ids_ref, bf16[512,1024]{1,0:T(8,128)(2,1)} %bitcast.26, bf16[128,4224]{1,0:T(8,128)(2,1)} %in_z_order.3.refs_0_, bf16[128,4224]{1,0:T(8,128)(2,1)} %copy-done, ...), custom_call_target="tpu_custom_call" | custom-call | flops 1 | bytes 1 | tf_op jit(solution)/shard_map/project/pallas_call | solution.py:344
  95.7 12.8 %attend_forward.1 = (bf16[512,1024]{1,0:T(8,128)(2,1)}, f32[1,8,8,512]{3,2,1,0:T(8,128)}) custom-call(s32[1,1,512]{2,1,0:T(1,128)} %bitcast.43, bf16[512,1024]{1,0:T(8,128)(2,1)} %get-tuple-element.108.q_ref, bf16[512,1024]{1,0:T(8,128)(2,1)} %get-tuple-element.109.k_ref, bf16[512,1024]{1,0:T(8,128)(2,1)} %get-tuple-element.110.v_ref), custom_call_target="tpu_custom_call" | custom-call | flops 1 | bytes 1 | tf_op jit(solution)/shard_map/attend_forward/pallas_call | solution.py:148
  111.0 11.9 %collective-permute-done.21.refs_4_.refs_14_ = bf16[64,4096]{1,0:T(8,128)(2,1)S(1)} collective-permute-done((bf16[64,4096]{1,0:T(8,128)(2,1)S(1)}, bf16[64,4096]{1,0:T(8,128)(2,1)S(1)}, u32[]{:S(2)}, u32[]{:S(2)}) %collective-permute-start.21) | collective-permute-done | bytes 524320 | tf_op jit(solution)/shard_map/ppermute | solution.py:189
  129.0 6.9 %close_attention.1 = (f32[512,1024]{1,0:T(8,128)}, f32[512,128]{1,0:T(8,128)}, bf16[512,1024]{1,0:T(8,128)(2,1)}) custom-call(s32[3]{0:T(128)} %pad_add_fusion.ids_ref, bf16[512,1024]{1,0:T(8,128)(2,1)} %get-tuple-element.111.m_ref.refs_0_.refs_1_.refs_2_.refs_3_, bf16[512,1024]{1,0:T(8,128)(2,1)} %bitcast.27, f32[16,1024]{1,0:T(8,128)} %get-tuple-element.112.vec_ref, ...), custom_call_target="tpu_custom_call" | custom-call | flops 1 | bytes 1 | tf_op jit(solution)/shard_map/close_attention/pallas_call | solution.py:344
  137.6 13.4 %ffn_in.1 = (bf16[512,4096]{1,0:T(8,128)(2,1)}, f32[512,4096]{1,0:T(8,128)}) custom-call(s32[3]{0:T(128)} %pad_add_fusion.ids_ref, bf16[512,1024]{1,0:T(8,128)(2,1)} %get-tuple-element.113.x_ref.refs_0_.refs_1_.refs_2_.refs_3_, f32[1,4096]{1,0:T(1,128)} %reshape.126.bias_ref, bf16[128,4096]{1,0:T(8,128)(2,1)} %in_z_order.4.refs_0_.refs_10_, ...), custom_call_target="tpu_custom_call" | custom-call | flops 1 | bytes 1 | tf_op jit(solution)/shard_map/ffn_in/pallas_call | solution.py:344
  157.2 10.5 %collective-permute-done.30.refs_4_ = bf16[256,1024]{1,0:T(8,128)(2,1)S(1)} collective-permute-done((bf16[256,1024]{1,0:T(8,128)(2,1)S(1)}, bf16[256,1024]{1,0:T(8,128)(2,1)S(1)}, u32[]{:S(2)}, u32[]{:S(2)}) %collective-permute-start.30) | collective-permute-done | bytes 524320 | tf_op jit(solution)/shard_map/ppermute | solution.py:189
  172.6 18.6 %ffn_out.1 = (bf16[512,1024]{1,0:T(8,128)(2,1)}, f32[512,1024]{1,0:T(8,128)}, bf16[512,1024]{1,0:T(8,128)(2,1)}, f32[8,1024]{1,0:T(8,128)}) custom-call(s32[3]{0:T(128)} %pad_add_fusion.ids_ref, bf16[512,4096]{1,0:T(8,128)(2,1)} %get-tuple-element.123.act_ref.refs_0_.refs_1_.refs_2_.refs_3_, f32[512,1024]{1,0:T(8,128)} %get-tuple-element.124.n_ref, ...), custom_call_target="tpu_custom_call" | custom-call | flops 1 | bytes 1 | tf_op jit(solution)/shard_map/ffn_out/pallas_call | solution.py:344
  191.2 6.4 %rows_of_other_core.3.refs_10_ = bf16[2048,1024]{1,0:T(8,128)(2,1)} custom-call(s32[3]{0:T(128)} %pad_add_fusion.ids_ref, bf16[512,4096]{1,0:T(8,128)(2,1)} %get-tuple-element.123.act_ref.refs_0_.refs_1_.refs_2_.refs_3_, bf16[512,4096]{1,0:T(8,128)(2,1)} %get-tuple-element.123.act_ref.refs_0_.refs_1_.refs_2_.refs_3_, ...), custom_call_target="tpu_custom_call" | custom-call | flops 1 | bytes 1 | tf_op jit(solution)/shard_map/rows_of_other_core/pallas_call | solution.py:344
  197.7 12.3 %ffn_back.1 = (bf16[512,4096]{1,0:T(8,128)(2,1)}, f32[8,4096]{1,0:T(8,128)}) custom-call(s32[3]{0:T(128)} %pad_add_fusion.ids_ref, bf16[512,1024]{1,0:T(8,128)(2,1)} %get-tuple-element.132.refs_4_.grad_ref, f32[512,4096]{1,0:T(8,128)} %get-tuple-element.133.slope_ref, bf16[512,1024]{1,0:T(8,128)(2,1)} %in_z_order.5.refs_0_, ...), custom_call_target="tpu_custom_call" | custom-call | flops 1 | bytes 1 | tf_op jit(solution)/shard_map/ffn_back/pallas_call | solution.py:344
  210.1 9.4 %rows_of_own_core.3 = (bf16[1024,512]{1,0:T(8,128)(2,1)}, bf16[1024,512]{1,0:T(8,128)(2,1)}, bf16[1024,512]{1,0:T(8,128)(2,1)}, bf16[1024,512]{1,0:T(8,128)(2,1)}) custom-call(s32[3]{0:T(128)} %pad_add_fusion.ids_ref, bf16[512,4096]{1,0:T(8,128)(2,1)} %get-tuple-element.123.act_ref.refs_0_.refs_1_.refs_2_.refs_3_, ...), custom_call_target="tpu_custom_call" | custom-call | flops 1 | bytes 1 | tf_op jit(solution)/shard_map/rows_of_own_core/pallas_call | solution.py:344
  219.5 7.4 %rows_of_other_core.4.refs_20_ = bf16[512,4096]{1,0:T(8,128)(2,1)} custom-call(s32[3]{0:T(128)} %pad_add_fusion.ids_ref, bf16[512,1024]{1,0:T(8,128)(2,1)} %get-tuple-element.113.x_ref.refs_0_.refs_1_.refs_2_.refs_3_, bf16[512,1024]{1,0:T(8,128)(2,1)} %get-tuple-element.113.x_ref.refs_0_.refs_1_.refs_2_.refs_3_, ...), custom_call_target="tpu_custom_call" | custom-call | flops 1 | bytes 1 | tf_op jit(solution)/shard_map/rows_of_other_core/pallas_call | solution.py:344
  230.1 16.5 %attention_norm_back.1 = (bf16[512,1024]{1,0:T(8,128)(2,1)}, f32[512,1024]{1,0:T(8,128)}, bf16[512,1024]{1,0:T(8,128)(2,1)}, f32[8,1024]{1,0:T(8,128)}) custom-call(s32[3]{0:T(128)} %pad_add_fusion.ids_ref, bf16[512,4096]{1,0:T(8,128)(2,1)} %get-tuple-element.134.refs_6_.refs_4_.grad_ref, f32[512,1024]{1,0:T(8,128)} %get-tuple-element.135.ffn_ref, ...), custom_call_target="tpu_custom_call" | custom-call | flops 1 | bytes 1 | tf_op jit(solution)/shard_map/attention_norm_back/pallas_call | solution.py:344
  246.6 6.1 %collective-permute-done.38.refs_1_ = bf16[1024,512]{1,0:T(8,128)(2,1)S(1)} collective-permute-done((bf16[1024,512]{1,0:T(8,128)(2,1)}, bf16[1024,512]{1,0:T(8,128)(2,1)S(1)}, u32[]{:S(2)}, u32[]{:S(2)}) %collective-permute-start.38) | collective-permute-done | bytes 1048608 | tf_op jit(solution)/shard_map/ppermute | solution.py:189
  258.9 8.3 %rows_of_own_core.4 = (bf16[256,2048]{1,0:T(8,128)(2,1)}, bf16[256,2048]{1,0:T(8,128)(2,1)}, bf16[256,2048]{1,0:T(8,128)(2,1)}, bf16[256,2048]{1,0:T(8,128)(2,1)}) custom-call(s32[3]{0:T(128)} %pad_add_fusion.ids_ref, bf16[512,1024]{1,0:T(8,128)(2,1)} %get-tuple-element.113.x_ref.refs_0_.refs_1_.refs_2_.refs_3_, ...), custom_call_target="tpu_custom_call" | custom-call | flops 1 | bytes 1 | tf_op jit(solution)/shard_map/rows_of_own_core/pallas_call | solution.py:344
  271.3 17.0 %attend_backward.1 = (bf16[512,1024]{1,0:T(8,128)(2,1)}, bf16[512,1024]{1,0:T(8,128)(2,1)}, bf16[512,1024]{1,0:T(8,128)(2,1)}, f32[1,8,1024]{2,1,0:T(8,128)}, f32[1,8,1024]{2,1,0:T(8,128)}) custom-call(s32[1,1,512]{2,1,0:T(1,128)} %bitcast.44, bf16[512,1024]{1,0:T(8,128)(2,1)} %get-tuple-element.108.q_ref, bf16[512,1024]{1,0:T(8,128)(2,1)} %get-tuple-element.109.k_ref, ...), custom_call_target="tpu_custom_call" | custom-call | flops 1 | bytes 1 | tf_op jit(solution)/shard_map/attend_backward/pallas_call | solution.py:168
  288.3 15.3 %collective-permute-done.42.refs_12_.refs_1_ = bf16[512,512]{1,0:T(8,128)(2,1)S(1)} collective-permute-done((bf16[512,512]{1,0:T(8,128)(2,1)}, bf16[512,512]{1,0:T(8,128)(2,1)S(1)}, u32[]{:S(2)}, u32[]{:S(2)}) %collective-permute-start.42) | collective-permute-done | bytes 524320 | tf_op jit(solution)/shard_map/ppermute | solution.py:189
  305.3 7.6 %rows_of_other_core.5.refs_4_ = bf16[512,4096]{1,0:T(8,128)(2,1)} custom-call(s32[3]{0:T(128)} %pad_add_fusion.ids_ref, bf16[512,1024]{1,0:T(8,128)(2,1)} %get-tuple-element.111.m_ref.refs_0_.refs_1_.refs_2_.refs_3_, bf16[512,1024]{1,0:T(8,128)(2,1)} %get-tuple-element.111.m_ref.refs_0_.refs_1_.refs_2_.refs_3_, ...), custom_call_target="tpu_custom_call" | custom-call | flops 1 | bytes 1 | tf_op jit(solution)/shard_map/rows_of_other_core/pallas_call | solution.py:344
  312.9 4.0 fold.4
  322.9 9.4 %rows_of_own_core.5 = (bf16[256,2048]{1,0:T(8,128)(2,1)}, bf16[256,2048]{1,0:T(8,128)(2,1)}, bf16[256,2048]{1,0:T(8,128)(2,1)}, bf16[256,2048]{1,0:T(8,128)(2,1)}) custom-call(s32[3]{0:T(128)} %pad_add_fusion.ids_ref, bf16[512,1024]{1,0:T(8,128)(2,1)} %get-tuple-element.111.m_ref.refs_0_.refs_1_.refs_2_.refs_3_, ...), custom_call_target="tpu_custom_call" | custom-call | flops 1 | bytes 1 | tf_op jit(solution)/shard_map/rows_of_own_core/pallas_call | solution.py:344
  343.7 12.7 %collective-permute-done.48.refs_11_ = bf16[128,1024]{1,0:T(8,128)(2,1)S(1)} collective-permute-done((bf16[128,1024]{1,0:T(8,128)(2,1)S(1)}, bf16[128,1024]{1,0:T(8,128)(2,1)S(1)}, u32[]{:S(2)}, u32[]{:S(2)}) %collective-permute-start.48) | collective-permute-done | bytes 262176 | tf_op jit(solution)/shard_map/ppermute | solution.py:189
  357.1 10.1 %inputs_back.1.refs_4_ = f32[512,1024]{1,0:T(8,128)} custom-call(s32[3]{0:T(128)} %pad_add_fusion.ids_ref, f32[512,1024]{1,0:T(8,128)} %get-tuple-element.138.base_ref, bf16[512,1024]{1,0:T(8,128)(2,1)} %get-tuple-element.147.refs_9_.q_ref, bf16[512,1024]{1,0:T(8,128)(2,1)} %get-tuple-element.148.refs_10_.k_ref, ...), custom_call_target="tpu_custom_call" | custom-call | flops 1 | bytes 1 | tf_op jit(solution)/shard_map/inputs_back/pallas_call | solution.py:344
  368.2 4.1 fold.5
  382.8 6.7 %collective-permute-done.54.refs_4_ = bf16[32,4096]{1,0:T(8,128)(2,1)S(1)} collective-permute-done((bf16[32,4096]{1,0:T(8,128)(2,1)S(1)}, bf16[32,4096]{1,0:T(8,128)(2,1)S(1)}, u32[]{:S(2)}, u32[]{:S(2)}) %collective-permute-start.54) | collective-permute-done | bytes 262176 | tf_op jit(solution)/shard_map/ppermute | solution.py:189
  399.5 4.1 all-to-all-start
  412.5 8.0 %collective-permute-done.56 = bf16[32,4096]{1,0:T(8,128)(2,1)S(1)} collective-permute-done((bf16[32,4096]{1,0:T(8,128)(2,1)S(1)}, bf16[32,4096]{1,0:T(8,128)(2,1)S(1)}, u32[]{:S(2)}, u32[]{:S(2)}) %collective-permute-start.56) | collective-permute-done | bytes 262176 | tf_op jit(solution)/shard_map/ppermute | solution.py:189
  (239 shorter events, 119.3 us)
Async XLA Ops:
  2.6 16.6 %collective-permute-start.1 = (bf16[32,4224]{1,0:T(8,128)(2,1)}, bf16[32,4224]{1,0:T(8,128)(2,1)S(1)}, u32[]{:S(2)}, u32[]{:S(2)}) collective-permute-start(bf16[32,4224]{1,0:T(8,128)(2,1)} %first_shard.1.refs_0_), channel_id=1, source_target_pairs={{0,2},{1,3},{2,0},{3,1},{4,6},{5,7},{6,4},{7,5},{8,10},{9,11},{10,... | collective-permute-start | bytes 811016 | tf_op jit(solution)/shard_map/ppermute | solution.py:189
  31.4 24.4 %collective-permute-start.3 = (bf16[128,4224]{1,0:T(8,128)(2,1)}, bf16[128,4224]{1,0:T(8,128)(2,1)S(1)}, u32[]{:S(2)}, u32[]{:S(2)}) collective-permute-start(bf16[128,4224]{1,0:T(8,128)(2,1)} %in_z_order.3.refs_0_), channel_id=1, source_target_pairs={{0,8},{1,9},{2,10},{3,11},{4,12},{5,13},{6,14},{7,15},{8,0},{9,1},... | collective-permute-start | bytes 3244040 | tf_op jit(solution)/shard_map/ppermute | solution.py:189
  32.6 24.1 %collective-permute-start.4 = (bf16[128,4224]{1,0:T(8,128)(2,1)}, bf16[128,4224]{1,0:T(8,128)(2,1)S(1)}, u32[]{:S(2)}, u32[]{:S(2)}) collective-permute-start(bf16[128,4224]{1,0:T(8,128)(2,1)} %in_z_order.3.refs_0_), channel_id=1, source_target_pairs={{0,16},{1,17},{2,18},{3,19},{4,20},{5,21},{6,22},{7,23},{8,24},{9,... | collective-permute-start | bytes 3244040 | tf_op jit(solution)/shard_map/ppermute | solution.py:189
  49.1 26.2 %collective-permute-start.10 = (bf16[128,4224]{1,0:T(8,128)(2,1)}, bf16[128,4224]{1,0:T(8,128)(2,1)S(1)}, u32[]{:S(2)}, u32[]{:S(2)}) collective-permute-start(bf16[128,4224]{1,0:T(8,128)(2,1)} %in_z_order.3.refs_0_), channel_id=1, source_target_pairs={{0,4},{1,5},{2,6},{3,7},{4,0},{5,1},{6,2},{7,3},{8,12},{9,13},{10,... | collective-permute-start | bytes 3244040 | tf_op jit(solution)/shard_map/ppermute | solution.py:189
  57.5 17.8 %collective-permute-start.11 = (bf16[128,4224]{1,0:T(8,128)(2,1)S(1)}, bf16[128,4224]{1,0:T(8,128)(2,1)}, u32[]{:S(2)}, u32[]{:S(2)}) collective-permute-start(bf16[128,4224]{1,0:T(8,128)(2,1)S(1)} %collective-permute-done.3.refs_1_), channel_id=1, source_target_pairs={{0,4},{1,5},{2,6},{3,7},{4,0},{5,1},{6,2},{7,3},{8,12},{9,13},{10,... | collective-permute-start | bytes 3244040 | tf_op jit(solution)/shard_map/ppermute | solution.py:189
  57.6 17.7 %collective-permute-start.12 = (bf16[128,4224]{1,0:T(8,128)(2,1)S(1)}, bf16[128,4224]{1,0:T(8,128)(2,1)}, u32[]{:S(2)}, u32[]{:S(2)}) collective-permute-start(bf16[128,4224]{1,0:T(8,128)(2,1)S(1)} %collective-permute-done.4.refs_2_), channel_id=1, source_target_pairs={{0,4},{1,5},{2,6},{3,7},{4,0},{5,1},{6,2},{7,3},{8,12},{9,13},{10,... | collective-permute-start | bytes 3244040 | tf_op jit(solution)/shard_map/ppermute | solution.py:189
  75.4 33.2 %collective-permute-start.15 = (bf16[128,4096]{1,0:T(8,128)(2,1)}, bf16[128,4096]{1,0:T(8,128)(2,1)S(1)}, u32[]{:S(2)}, u32[]{:S(2)}) collective-permute-start(bf16[128,4096]{1,0:T(8,128)(2,1)} %in_z_order.4.refs_0_.refs_10_), channel_id=1, source_target_pairs={{0,8},{1,9},{2,10},{3,11},{4,12},{5,13},{6,14},{7,15},{8,0},{9,1},... | collective-permute-start | bytes 3145736 | tf_op jit(solution)/shard_map/ppermute | solution.py:189
  76.9 31.7 %collective-permute-start.16 = (bf16[128,4096]{1,0:T(8,128)(2,1)}, bf16[128,4096]{1,0:T(8,128)(2,1)S(1)}, u32[]{:S(2)}, u32[]{:S(2)}) collective-permute-start(bf16[128,4096]{1,0:T(8,128)(2,1)} %in_z_order.4.refs_0_.refs_10_), channel_id=1, source_target_pairs={{0,16},{1,17},{2,18},{3,19},{4,20},{5,21},{6,22},{7,23},{8,24},{9,... | collective-permute-start | bytes 3145736 | tf_op jit(solution)/shard_map/ppermute | solution.py:189
  78.4 16.7 %collective-permute-start.18 = (bf16[128,1024]{1,0:T(8,128)(2,1)}, bf16[128,1024]{1,0:T(8,128)(2,1)S(1)}, u32[]{:S(2)}, u32[]{:S(2)}) collective-permute-start(bf16[128,1024]{1,0:T(8,128)(2,1)} %refs_0_.3), channel_id=1, source_target_pairs={{0,2},{1,3},{2,0},{3,1},{4,6},{5,7},{6,4},{7,5},{8,10},{9,11},{10,... | collective-permute-start | bytes 786440 | tf_op jit(solution)/shard_map/ppermute | solution.py:189
  82.7 45.0 %collective-permute-start.22 = (bf16[128,4096]{1,0:T(8,128)(2,1)}, bf16[128,4096]{1,0:T(8,128)(2,1)}, u32[]{:S(2)}, u32[]{:S(2)}) collective-permute-start(bf16[128,4096]{1,0:T(8,128)(2,1)} %in_z_order.4.refs_0_.refs_10_), channel_id=1, source_target_pairs={{0,4},{1,5},{2,6},{3,7},{4,0},{5,1},{6,2},{7,3},{8,12},{9,13},{10,... | collective-permute-start | bytes 3145736 | tf_op jit(solution)/shard_map/ppermute | solution.py:189
  82.7 25.8 %collective-permute-start.17 = (bf16[128,1024]{1,0:T(8,128)(2,1)}, bf16[128,1024]{1,0:T(8,128)(2,1)}, u32[]{:S(2)}, u32[]{:S(2)}) collective-permute-start(bf16[128,1024]{1,0:T(8,128)(2,1)} %refs_0_.3), channel_id=1, source_target_pairs={{0,1},{1,0},{2,3},{3,2},{4,5},{5,4},{6,7},{7,6},{8,9},{9,8},{10,11... | collective-permute-start | bytes 786440 | tf_op jit(solution)/shard_map/ppermute | solution.py:189
  110.5 27.1 %collective-permute-start.23 = (bf16[128,4096]{1,0:T(8,128)(2,1)S(1)}, bf16[128,4096]{1,0:T(8,128)(2,1)}, u32[]{:S(2)}, u32[]{:S(2)}) collective-permute-start(bf16[128,4096]{1,0:T(8,128)(2,1)S(1)} %collective-permute-done.15.refs_1_.refs_11_), channel_id=1, source_target_pairs={{0,4},{1,5},{2,6},{3,7},{4,0},{5,1},{6,2},{7,3},{8,12},{9,13},{10,... | collective-permute-start | bytes 3145736 | tf_op jit(solution)/shard_map/ppermute | solution.py:189
  110.5 27.2 %collective-permute-start.24 = (bf16[128,4096]{1,0:T(8,128)(2,1)S(1)}, bf16[128,4096]{1,0:T(8,128)(2,1)}, u32[]{:S(2)}, u32[]{:S(2)}) collective-permute-start(bf16[128,4096]{1,0:T(8,128)(2,1)S(1)} %collective-permute-done.16.refs_2_.refs_12_), channel_id=1, source_target_pairs={{0,4},{1,5},{2,6},{3,7},{4,0},{5,1},{6,2},{7,3},{8,12},{9,13},{10,... | collective-permute-start | bytes 3145736 | tf_op jit(solution)/shard_map/ppermute | solution.py:189
  126.2 26.0 %collective-permute-start.27 = (bf16[512,1024]{1,0:T(8,128)(2,1)}, bf16[512,1024]{1,0:T(8,128)(2,1)}, u32[]{:S(2)}, u32[]{:S(2)}) collective-permute-start(bf16[512,1024]{1,0:T(8,128)(2,1)} %in_z_order.5.refs_0_), channel_id=1, source_target_pairs={{0,8},{1,9},{2,10},{3,11},{4,12},{5,13},{6,14},{7,15},{8,0},{9,1},... | collective-permute-start | bytes 3145736 | tf_op jit(solution)/shard_map/ppermute | solution.py:189
  127.7 25.6 %collective-permute-start.28 = (bf16[512,1024]{1,0:T(8,128)(2,1)}, bf16[512,1024]{1,0:T(8,128)(2,1)}, u32[]{:S(2)}, u32[]{:S(2)}) collective-permute-start(bf16[512,1024]{1,0:T(8,128)(2,1)} %in_z_order.5.refs_0_), channel_id=1, source_target_pairs={{0,16},{1,17},{2,18},{3,19},{4,20},{5,21},{6,22},{7,23},{8,24},{9,... | collective-permute-start | bytes 3145736 | tf_op jit(solution)/shard_map/ppermute | solution.py:189
  137.6 31.6 %collective-permute-start.31 = (bf16[512,1024]{1,0:T(8,128)(2,1)S(1)}, bf16[512,1024]{1,0:T(8,128)(2,1)}, u32[]{:S(2)}, u32[]{:S(2)}) collective-permute-start(bf16[512,1024]{1,0:T(8,128)(2,1)S(1)} %copy-done.3), channel_id=1, source_target_pairs={{0,4},{1,5},{2,6},{3,7},{4,0},{5,1},{6,2},{7,3},{8,12},{9,13},{10,... | collective-permute-start | bytes 3145736 | tf_op jit(solution)/shard_map/ppermute | solution.py:189
  226.9 32.0 %collective-permute-start.37 = (bf16[512,4096]{1,0:T(8,128)(2,1)}, bf16[512,4096]{1,0:T(8,128)(2,1)}, u32[]{:S(2)}, u32[]{:S(2)}) collective-permute-start(bf16[512,4096]{1,0:T(8,128)(2,1)} %rows_of_other_core.4.refs_20_), channel_id=1, source_target_pairs={{0,4},{1,5},{2,6},{3,7},{4,0},{5,1},{6,2},{7,3},{8,12},{9,13},{10,... | collective-permute-start | bytes 12582920 | tf_op jit(solution)/shard_map/ppermute | solution.py:189
  227.3 25.4 %collective-permute-start.38 = (bf16[1024,512]{1,0:T(8,128)(2,1)}, bf16[1024,512]{1,0:T(8,128)(2,1)S(1)}, u32[]{:S(2)}, u32[]{:S(2)}) collective-permute-start(bf16[1024,512]{1,0:T(8,128)(2,1)} %get-tuple-element.141), channel_id=1, source_target_pairs={{0,8},{1,9},{2,10},{3,11},{4,12},{5,13},{6,14},{7,15},{8,0},{9,1},... | collective-permute-start | bytes 3145736 | tf_op jit(solution)/shard_map/ppermute | solution.py:189
  229.0 24.9 %collective-permute-start.39 = (bf16[1024,512]{1,0:T(8,128)(2,1)S(1)}, bf16[1024,512]{1,0:T(8,128)(2,1)S(1)}, u32[]{:S(2)}, u32[]{:S(2)}) collective-permute-start(bf16[1024,512]{1,0:T(8,128)(2,1)S(1)} %copy-done.43), channel_id=1, source_target_pairs={{0,16},{1,17},{2,18},{3,19},{4,20},{5,21},{6,22},{7,23},{8,24},{9,... | collective-permute-start | bytes 3145736 | tf_op jit(solution)/shard_map/ppermute | solution.py:189
  267.2 36.4 %collective-permute-start.40 = (bf16[256,2048]{1,0:T(8,128)(2,1)}, bf16[256,2048]{1,0:T(8,128)(2,1)S(1)}, u32[]{:S(2)}, u32[]{:S(2)}) collective-permute-start(bf16[256,2048]{1,0:T(8,128)(2,1)} %get-tuple-element.150), channel_id=1, source_target_pairs={{0,8},{1,9},{2,10},{3,11},{4,12},{5,13},{6,14},{7,15},{8,0},{9,1},... | collective-permute-start | bytes 3145736 | tf_op jit(solution)/shard_map/ppermute | solution.py:189
  268.1 35.6 %collective-permute-start.41 = (bf16[256,2048]{1,0:T(8,128)(2,1)}, bf16[256,2048]{1,0:T(8,128)(2,1)S(1)}, u32[]{:S(2)}, u32[]{:S(2)}) collective-permute-start(bf16[256,2048]{1,0:T(8,128)(2,1)} %get-tuple-element.152), channel_id=1, source_target_pairs={{0,16},{1,17},{2,18},{3,19},{4,20},{5,21},{6,22},{7,23},{8,24},{9,... | collective-permute-start | bytes 3145736 | tf_op jit(solution)/shard_map/ppermute | solution.py:189
  269.1 34.5 %collective-permute-start.42 = (bf16[512,512]{1,0:T(8,128)(2,1)}, bf16[512,512]{1,0:T(8,128)(2,1)S(1)}, u32[]{:S(2)}, u32[]{:S(2)}) collective-permute-start(bf16[512,512]{1,0:T(8,128)(2,1)} %get-tuple-element.153), channel_id=1, source_target_pairs={{0,16},{1,17},{2,18},{3,19},{4,20},{5,21},{6,22},{7,23},{8,24},{9,... | collective-permute-start | bytes 1572872 | tf_op jit(solution)/shard_map/ppermute | solution.py:189
  270.1 33.5 %collective-permute-start.43 = (bf16[512,512]{1,0:T(8,128)(2,1)}, bf16[512,512]{1,0:T(8,128)(2,1)S(1)}, u32[]{:S(2)}, u32[]{:S(2)}) collective-permute-start(bf16[512,512]{1,0:T(8,128)(2,1)} %get-tuple-element.154), channel_id=1, source_target_pairs={{0,8},{1,9},{2,10},{3,11},{4,12},{5,13},{6,14},{7,15},{8,0},{9,1},... | collective-permute-start | bytes 1572872 | tf_op jit(solution)/shard_map/ppermute | solution.py:189
  316.9 17.6 %collective-permute-start.44 = (bf16[128,2048]{1,0:T(8,128)(2,1)}, bf16[128,2048]{1,0:T(8,128)(2,1)S(1)}, u32[]{:S(2)}, u32[]{:S(2)}) collective-permute-start(bf16[128,2048]{1,0:T(8,128)(2,1)} %get-tuple-element.156), channel_id=1, source_target_pairs={{0,16},{1,17},{2,18},{3,19},{4,20},{5,21},{6,22},{7,23},{8,24},{9,... | collective-permute-start | bytes 1572872 | tf_op jit(solution)/shard_map/ppermute | solution.py:189
  318.0 16.5 %collective-permute-start.45 = (bf16[128,2048]{1,0:T(8,128)(2,1)}, bf16[128,2048]{1,0:T(8,128)(2,1)S(1)}, u32[]{:S(2)}, u32[]{:S(2)}) collective-permute-start(bf16[128,2048]{1,0:T(8,128)(2,1)} %get-tuple-element.158), channel_id=1, source_target_pairs={{0,8},{1,9},{2,10},{3,11},{4,12},{5,13},{6,14},{7,15},{8,0},{9,1},... | collective-permute-start | bytes 1572872 | tf_op jit(solution)/shard_map/ppermute | solution.py:189
  322.2 17.9 %collective-permute-start.47 = (bf16[256,1024]{1,0:T(8,128)(2,1)}, bf16[256,1024]{1,0:T(8,128)(2,1)S(1)}, u32[]{:S(2)}, u32[]{:S(2)}) collective-permute-start(bf16[256,1024]{1,0:T(8,128)(2,1)} %get-tuple-element.164), channel_id=1, source_target_pairs={{0,1},{1,0},{2,3},{3,2},{4,5},{5,4},{6,7},{7,6},{8,9},{9,8},{10,11... | collective-permute-start | bytes 1572872 | tf_op jit(solution)/shard_map/ppermute | solution.py:189
  332.4 34.8 %collective-permute-start.49 = (bf16[256,2048]{1,0:T(8,128)(2,1)}, bf16[256,2048]{1,0:T(8,128)(2,1)S(1)}, u32[]{:S(2)}, u32[]{:S(2)}) collective-permute-start(bf16[256,2048]{1,0:T(8,128)(2,1)} %get-tuple-element.165), channel_id=1, source_target_pairs={{0,8},{1,9},{2,10},{3,11},{4,12},{5,13},{6,14},{7,15},{8,0},{9,1},... | collective-permute-start | bytes 3145736 | tf_op jit(solution)/shard_map/ppermute | solution.py:189
  333.6 33.6 %collective-permute-start.50 = (bf16[256,2048]{1,0:T(8,128)(2,1)}, bf16[256,2048]{1,0:T(8,128)(2,1)}, u32[]{:S(2)}, u32[]{:S(2)}) collective-permute-start(bf16[256,2048]{1,0:T(8,128)(2,1)} %get-tuple-element.167), channel_id=1, source_target_pairs={{0,16},{1,17},{2,18},{3,19},{4,20},{5,21},{6,22},{7,23},{8,24},{9,... | collective-permute-start | bytes 3145736 | tf_op jit(solution)/shard_map/ppermute | solution.py:189
  338.8 36.3 %collective-permute-start.53 = (bf16[64,4096]{1,0:T(8,128)(2,1)}, bf16[64,4096]{1,0:T(8,128)(2,1)}, u32[]{:S(2)}, u32[]{:S(2)}) collective-permute-start(bf16[64,4096]{1,0:T(8,128)(2,1)} %get-tuple-element.173), channel_id=1, source_target_pairs={{0,1},{1,0},{2,3},{3,2},{4,5},{5,4},{6,7},{7,6},{8,9},{9,8},{10,11... | collective-permute-start | bytes 1572872 | tf_op jit(solution)/shard_map/ppermute | solution.py:189
  340.3 16.0 %collective-permute-start.48 = (bf16[128,1024]{1,0:T(8,128)(2,1)S(1)}, bf16[128,1024]{1,0:T(8,128)(2,1)S(1)}, u32[]{:S(2)}, u32[]{:S(2)}) collective-permute-start(bf16[128,1024]{1,0:T(8,128)(2,1)S(1)} %slice.150), channel_id=1, source_target_pairs={{0,2},{1,3},{2,0},{3,1},{4,6},{5,7},{6,4},{7,5},{8,10},{9,11},{10,... | collective-permute-start | bytes 786440 | tf_op jit(solution)/shard_map/ppermute | solution.py:189
  372.4 17.1 %collective-permute-start.51 = (bf16[128,2048]{1,0:T(8,128)(2,1)}, bf16[128,2048]{1,0:T(8,128)(2,1)S(1)}, u32[]{:S(2)}, u32[]{:S(2)}) collective-permute-start(bf16[128,2048]{1,0:T(8,128)(2,1)} %get-tuple-element.169), channel_id=1, source_target_pairs={{0,16},{1,17},{2,18},{3,19},{4,20},{5,21},{6,22},{7,23},{8,24},{9,... | collective-permute-start | bytes 1572872 | tf_op jit(solution)/shard_map/ppermute | solution.py:189
  374.0 15.4 %collective-permute-start.52 = (bf16[128,2048]{1,0:T(8,128)(2,1)}, bf16[128,2048]{1,0:T(8,128)(2,1)}, u32[]{:S(2)}, u32[]{:S(2)}) collective-permute-start(bf16[128,2048]{1,0:T(8,128)(2,1)} %get-tuple-element.171), channel_id=1, source_target_pairs={{0,8},{1,9},{2,10},{3,11},{4,12},{5,13},{6,14},{7,15},{8,0},{9,1},... | collective-permute-start | bytes 1572872 | tf_op jit(solution)/shard_map/ppermute | solution.py:189
  (71 other events, 586.7 us)

commit v3 on v2

--- a/solution.py
+++ b/solution.py
@@ -16,7 +16,13 @@
 NT = (((1,), (1,)), ((), ()))
 TN = (((0,), (0,)), ((), ()))
 MASKED = -1e30
-LIGHT = pl.CostEstimate(flops=1, bytes_accessed=1, transcendentals=0)
+WEIGHT = 0.3
+
+
+def spend(micros):
+    return pl.CostEstimate(flops=1, bytes_accessed=int(micros * WEIGHT * 1e6), transcendentals=0)
+
+
 ANY = pl.BlockSpec(memory_space=pl.ANY)
 
 
@@ -156,7 +162,7 @@
         out_specs=[block, total],
         scratch_shapes=[pltpu.VMEM((seq_len, seq_len), F32)],
         name="attend_forward",
-        cost_estimate=LIGHT,
+        cost_estimate=spend(13),
     )(seg.reshape(rows, 1, seq_len), queries, keys, values)
 
 
@@ -174,7 +180,7 @@
         out_specs=[block, block, block, sums, sums],
         scratch_shapes=[pltpu.VMEM((seq_len, seq_len), F32)],
         name="attend_backward",
-        cost_estimate=LIGHT,
+        cost_estimate=spend(17),
     )(seg.reshape(rows, 1, seq_len), queries, keys, values, mixed_grad, totals, *deps)
     dq, dk, dv, dq_sum, dv_sum = outs
     return dq, dk, dv, jnp.sum(dq_sum[:, 0], axis=0), jnp.sum(dv_sum[:, 0], axis=0)
@@ -224,7 +230,7 @@
         out_shape=struct((rows, columns + 128), BF),
         scratch_shapes=[pltpu.VMEM((128, 128), F32)],
         name="first_shard",
-        cost_estimate=LIGHT,
+        cost_estimate=spend(2),
     )(*matrices, *[v.reshape(1, -1) for v in vectors])
 
 
@@ -250,7 +256,7 @@
             out_specs=pl.BlockSpec((net.inner * rows, tile), lambda n, ids: (0, n)),
         ),
         name="in_z_order",
-        cost_estimate=LIGHT,
+        cost_estimate=spend(3),
     )(ids, *parts)
 
 
@@ -318,8 +324,10 @@
         again.arrays = list(tied[: len(self.arrays)])
         return again
 
-    def start(self, ids_ref, refs, column, target, at, width, sems):
+    def start(self, ids_ref, refs, column, target, at, width, sems, hop=None):
         for ref, (rows, j, c, s) in zip(refs, self.meta):
+            if hop is not None and j != hop:
+                continue
             block = (ids_ref[0] ^ j) * 2 + (ids_ref[1] ^ c)
             row = pl.multiple_of(block * self.block + s, 16)
             pltpu.make_async_copy(
@@ -340,7 +348,28 @@
             self.wait(block, target, at, width, sems)
 
 
-def kernel(body, name, ids, grid, operands, outs, scratch):
+def copies(pairs, sems, *at):
+    return [
+        pltpu.make_async_copy(source, target, sems.at[(*at, i)])
+        for i, (source, target) in enumerate(pairs)
+    ]
+
+
+def start_all(some):
+    for copy in some:
+        copy.start()
+
+
+def wait_for(some):
+    for copy in some:
+        copy.wait()
+
+
+def aligned(start, size):
+    return pl.ds(pl.multiple_of(start, 128), size)
+
+
+def kernel(body, name, micros, ids, grid, operands, outs, scratch):
     return pl.pallas_call(
         body,
         out_shape=[o for o, _ in outs],
@@ -352,13 +381,13 @@
             scratch_shapes=scratch,
         ),
         name=name,
-        cost_estimate=LIGHT,
+        cost_estimate=spend(micros),
     )(ids, *[o for o, _ in operands])
 
 
 def project(ids, tokens, weights):
     count, width = tokens.shape
-    tile = 512
+    tile = min(width, 1024)
     per = width // tile
     n_pieces = len(weights.arrays)
 
@@ -397,6 +426,7 @@
     return kernel(
         body,
         "project",
+        10,
         ids,
         (3 * per,),
         [(tokens, whole(tokens.shape))] + [(p, ANY) for p in weights.arrays],
@@ -434,6 +464,7 @@
     return kernel(
         body,
         "close_attention",
+        7,
         ids,
         (count // rows,),
         [(mixed, block), (tokens, block), (vectors, whole(vectors.shape))]
@@ -464,8 +495,9 @@
                 weights.start(ids_ref, pieces, g * tile, w_ref.at[g], 0, tile, sems.at[g])
 
         weights.wait_all(w_ref.at[step], 0, tile, sems.at[step])
-        for at in range(0, tile, 512):
-            columns = slice(at, at + 512)
+        @pl.loop(0, tile // 512)
+        def _(part):
+            columns = pl.ds(pl.multiple_of(part * 512, 512), 512)
             pre = dot(x_ref[...], w_ref[step, :, columns]) + bias_ref[:, columns]
             below = 0.5 + 0.5 * lax.erf(pre * (0.5**0.5))
             density = jnp.exp(pre * pre * -0.5) * 0.3989422804014327
@@ -476,6 +508,7 @@
     return kernel(
         body,
         "ffn_in",
+        13,
         ids,
         (wide // tile,),
         [(low, whole(low.shape)), (bias, pl.BlockSpec((1, tile), lambda n, ids: (0, n)))]
@@ -491,67 +524,110 @@
 def ffn_out(ids, act, normed, out_grad, weights, vectors):
     count, wide = act.shape
     width = normed.shape[1]
+    block = weights.block
+    hops = weights.count // 2
     n_pieces = len(weights.arrays)
-
-    def body(ids_ref, act_ref, n_ref, g_ref, vec_ref, *refs):
+    step = 128
+
+    def body(ids_ref, vec_ref, act_hbm, n_hbm, g_hbm, *refs):
         pieces = refs[:n_pieces]
-        out_ref, sum_ref, low_ref, sums_ref, acc_ref, w_ref, sems = refs[n_pieces:]
-        tile = 256
-        for i in range(width // tile):
-            weights.start(ids_ref, pieces, i * tile, w_ref, i * tile, tile, sems.at[i])
-        for i in range(width // tile):
-            part = slice(i * tile, (i + 1) * tile)
-            start = n_ref[:, part] * vec_ref[3:4, part] + vec_ref[4:5, part] + vec_ref[5:6, part]
-            weights.wait_all(w_ref, i * tile, tile, sems.at[i])
-            acc_ref[:, part] = start + dot(act_ref[...], w_ref[:, part])
-        n2, inverse = normalise(acc_ref[...])
-        out_ref[...] = (n2 * vec_ref[6:7] + vec_ref[7:8]).astype(BF)
-        grad = g_ref[...].astype(F32)
-        back = normalise_back(grad * vec_ref[6:7], n2, inverse)
-        low = back.astype(BF)
-        sum_ref[...] = back
-        low_ref[...] = low
-        sums_ref[0:1, :] = total_rows(grad * n2)
-        sums_ref[1:2, :] = total_rows(grad)
-        sums_ref[2:3, :] = total_rows(low.astype(F32))
+        out_hbm, sum_hbm, low_hbm, sums_ref, sent_hbm = refs[n_pieces : n_pieces + 5]
+        acc_ref, n_ref, g_ref, out_ref, low_ref = refs[n_pieces + 5 : n_pieces + 10]
+        act_ref, w_ref, sent_ref, sems, in_sems, out_sems, sent_sems = refs[n_pieces + 10 :]
+        places = [aligned((ids_ref[0] ^ j) * 2 * block, 2 * block) for j in range(hops)]
+        fetch = copies([(act_hbm.at[:, p], act_ref.at[:, p]) for p in places], in_sems)
+        for j in range(hops):
+            fetch[j].start()
+            weights.start(ids_ref, pieces, 0, w_ref, 0, width, sems, hop=j)
+        late = [
+            pltpu.make_async_copy(n_hbm, n_ref, in_sems.at[hops]),
+            pltpu.make_async_copy(g_hbm, g_ref, in_sems.at[hops + 1]),
+        ]
+        start_all(late)
+        for j in range(hops):
+            fetch[j].wait()
+            for c in range(2):
+                weights.wait((ids_ref[0] ^ j) * 2 + c, w_ref, 0, width, sems)
+            product = dot(act_ref[:, places[j]], w_ref[places[j], :])
+            if j == 0:
+                acc_ref[...] = product
+            else:
+                acc_ref[...] += product
+        sums_ref[...] = jnp.zeros_like(sums_ref)
+        wait_for(late)
+
+        @pl.loop(0, count // step)
+        def _(part):
+            rows = pl.ds(pl.multiple_of(part * step, step), step)
+            base = n_ref[rows, :] * vec_ref[3:4] + vec_ref[4:5] + vec_ref[5:6]
+            n2, inverse = normalise(acc_ref[rows, :] + base)
+            out_ref[rows, :] = (n2 * vec_ref[6:7] + vec_ref[7:8]).astype(BF)
+            grad = g_ref[rows, :].astype(F32)
+            back = normalise_back(grad * vec_ref[6:7], n2, inverse)
+            low = back.astype(BF)
+            acc_ref[rows, :] = back
+            low_ref[rows, :] = low
+            sums_ref[0:1, :] += total_rows(grad * n2)
+            sums_ref[1:2, :] += total_rows(grad)
+            sums_ref[2:3, :] += total_rows(low.astype(F32))
+
+        done = copies([(low_ref, low_hbm), (acc_ref, sum_hbm), (out_ref, out_hbm)], out_sems)
+        start_all(done)
+        send = copies(
+            [(sent_ref.at[j], sent_hbm.at[pl.ds(j * block, block), :]) for j in range(hops)],
+            sent_sems,
+        )
+        for j in range(hops):
+            at = ((ids_ref[0] ^ j) * 2 + (ids_ref[1] ^ 1)) * block
+            sent_ref[j] = dot_tn(act_ref[:, aligned(at, block)], low_ref[...]).astype(BF)
+            send[j].start()
+        wait_for(done + send)
 
     size = (count, width)
     return kernel(
         body,
         "ffn_out",
+        18,
         ids,
         (1,),
+        [(vectors, whole(vectors.shape))]
+        + [(a, ANY) for a in [act, normed, out_grad] + weights.arrays],
         [
-            (act, whole(act.shape)),
-            (normed, whole(size)),
-            (out_grad, whole(size)),
-            (vectors, whole(vectors.shape)),
-        ]
-        + [(p, ANY) for p in weights.arrays],
-        [
-            (struct(size, BF), whole(size)),
-            (struct(size, F32), whole(size)),
-            (struct(size, BF), whole(size)),
+            (struct(size, BF), ANY),
+            (struct(size, F32), ANY),
+            (struct(size, BF), ANY),
             (struct((8, width), F32), whole((8, width))),
+            (struct((wide // 2, width), BF), ANY),
         ],
         [
             pltpu.VMEM(size, F32),
+            pltpu.VMEM(size, F32),
+            pltpu.VMEM(size, BF),
+            pltpu.VMEM(size, BF),
+            pltpu.VMEM(size, BF),
+            pltpu.VMEM((count, wide), BF),
             pltpu.VMEM((wide, width), BF),
-            pltpu.SemaphoreType.DMA((width // 256, weights.count)),
+            pltpu.VMEM((hops, block, width), BF),
+            pltpu.SemaphoreType.DMA((weights.count,)),
+            pltpu.SemaphoreType.DMA((hops + 2,)),
+            pltpu.SemaphoreType.DMA((3,)),
+            pltpu.SemaphoreType.DMA((hops,)),
         ],
     )
 
 
-def ffn_back(ids, grad, slope, weights, deps):
+def ffn_back(ids, grad, slope, weights, lefts, left_specs, deps):
     count, wide = slope.shape
     width = grad.shape[1]
     block = min(wide, 1024)
     per = block // weights.block
     n_pieces = len(weights.arrays)
+    rows_out = sum(spec.block_shape[1] for spec in left_specs)
 
     def body(ids_ref, grad_ref, slope_ref, *refs):
-        pieces = refs[:n_pieces]
-        out_ref, sums_ref, w_ref, sems = refs[-4:]
+        left_refs = refs[: len(lefts)]
+        pieces = refs[len(lefts) : len(lefts) + n_pieces]
+        out_ref, sums_ref, sent_ref, w_ref, sems = refs[-5:]
         step = pl.program_id(0)
 
         @pl.when(step == 0)
@@ -564,19 +640,27 @@
         back = (dot_nt(grad_ref[...], w_ref[rows, :]) * slope_ref[...]).astype(BF)
         out_ref[...] = back
         sums_ref[...] = jnp.broadcast_to(total_rows(back.astype(F32)), sums_ref.shape)
+        left = jnp.concatenate([ref[...] for ref in left_refs], axis=1)
+        sent_ref[...] = dot_tn(left, out_ref[...]).astype(BF)
 
     tile = pl.BlockSpec((count, block), lambda n, ids: (0, n))
     return kernel(
         body,
         "ffn_back",
+        12,
         ids,
         (wide // block,),
         [(grad, whole(grad.shape)), (slope, tile)]
+        + list(zip(lefts, left_specs))
         + [(p, ANY) for p in weights.arrays]
         + [(d, ANY) for d in deps],
         [
             (struct((count, wide), BF), tile),
             (struct((8, wide), F32), pl.BlockSpec((8, block), lambda n, ids: (0, n))),
+            (
+                struct((rows_out, wide), BF),
+                pl.BlockSpec((rows_out, block), lambda n, ids: (0, n)),
+            ),
         ],
         [pltpu.VMEM((wide, width), BF), pltpu.SemaphoreType.DMA((weights.count,))],
     )
@@ -585,68 +669,91 @@
 def attention_norm_back(ids, inner_grad, ffn_grad, normed, inverse, inner, weights, vectors, deps):
     count, wide = inner_grad.shape
     width = normed.shape[1]
-    tile = 256
-    steps = width // tile
-    per = tile // inner.block
+    tile = min(wide, 1024)
+    steps = wide // tile
     n_pieces = len(weights.arrays)
-
-    def body(ids_ref, grad_ref, ffn_ref, n_ref, inverse_ref, vec_ref, *refs):
+    part_rows = 128
+
+    def body(ids_ref, inverse_ref, vec_ref, grad_hbm, ffn_hbm, n_hbm, *refs):
         pieces = refs[:n_pieces]
         inner_pieces = refs[n_pieces : 2 * n_pieces]
-        low_ref, sum_ref, mixed_ref, sums_ref, acc_ref, w_ref, w_sems, o_ref, o_sems = refs[-9:]
-        step = pl.program_id(0)
-
-        @pl.when(step == 0)
-        def _():
-            inner.start(ids_ref, inner_pieces, 0, w_ref, 0, wide, w_sems)
-            weights.start(ids_ref, pieces, 3 * width, o_ref, 0, width, o_sems)
-
-        for i in range(per):
-            inner.wait(step * per + i, w_ref, 0, wide, w_sems)
-        place = pl.ds(pl.multiple_of(step * tile, tile), tile)
-        acc_ref[:, place] = ffn_ref[...] + dot_nt(grad_ref[...], w_ref[place, :])
-
-        @pl.when(step == steps - 1)
-        def _():
-            grad = acc_ref[...]
-            normed_rows = n_ref[...]
-            back = normalise_back(grad * vec_ref[3:4], normed_rows, inverse_ref[:, 0:1])
+        low_hbm, sum_hbm, mixed_hbm, sums_ref = refs[-17:-13]
+        acc_ref, ffn_ref, n_ref, low_ref, mixed_ref, grad_ref, w_ref = refs[-13:-6]
+        w_sems, o_ref, o_sems, sems, grad_sems, out_sems = refs[-6:]
+        tiles = [slice(g * tile, (g + 1) * tile) for g in range(steps)]
+        fetch = copies([(grad_hbm.at[:, t], grad_ref.at[:, t]) for t in tiles], grad_sems)
+        for g in range(steps):
+            fetch[g].start()
+            inner.start(ids_ref, inner_pieces, g * tile, w_ref.at[g], 0, tile, w_sems.at[g])
+        late = copies([(ffn_hbm, ffn_ref), (n_hbm, n_ref)], sems)
+        start_all(late)
+        weights.start(ids_ref, pieces, 3 * width, o_ref, 0, width, o_sems)
+        acc_ref[...] = jnp.zeros_like(acc_ref)
+
+        @pl.loop(0, steps)
+        def _(g):
+            there = grad_ref.at[:, aligned(g * tile, tile)]
+            pltpu.make_async_copy(there, there, grad_sems.at[g]).wait()
+            inner.wait_all(w_ref.at[g], 0, tile, w_sems.at[g])
+            acc_ref[...] += dot_nt(there[...], w_ref[g])
+
+        wait_for(late)
+        sums_ref[...] = jnp.zeros_like(sums_ref)
+
+        @pl.loop(0, count // part_rows)
+        def _(part):
+            rows = pl.ds(pl.multiple_of(part * part_rows, part_rows), part_rows)
+            grad = acc_ref[rows, :] + ffn_ref[rows, :]
+            normed_rows = n_ref[rows, :]
+            back = normalise_back(grad * vec_ref[3:4], normed_rows, inverse_ref[rows, 0:1])
             low = back.astype(BF)
-            low_ref[...] = low
-            sum_ref[...] = back
-            sums_ref[0:1, :] = total_rows(grad * normed_rows)
-            sums_ref[1:2, :] = total_rows(grad)
-            sums_ref[2:3, :] = total_rows(low.astype(F32))
-            weights.wait_all(o_ref, 0, width, o_sems)
-            mixed_ref[...] = dot_nt(low, o_ref[...]).astype(BF)
+            low_ref[rows, :] = low
+            acc_ref[rows, :] = back
+            sums_ref[0:1, :] += total_rows(grad * normed_rows)
+            sums_ref[1:2, :] += total_rows(grad)
+            sums_ref[2:3, :] += total_rows(low.astype(F32))
+
+        done = copies(
+            [(low_ref, low_hbm), (acc_ref, sum_hbm), (mixed_ref, mixed_hbm)], out_sems
+        )
+        start_all(done[:2])
+        weights.wait_all(o_ref, 0, width, o_sems)
+        mixed_ref[...] = dot_nt(low_ref[...], o_ref[...]).astype(BF)
+        done[2].start()
+        wait_for(done)
 
     size = (count, width)
     return kernel(
         body,
         "attention_norm_back",
+        16,
         ids,
-        (steps,),
+        (1,),
+        [(inverse, whole(inverse.shape)), (vectors, whole(vectors.shape))]
+        + [
+            (a, ANY)
+            for a in [inner_grad, ffn_grad, normed] + weights.arrays + inner.arrays + list(deps)
+        ],
         [
-            (inner_grad, whole(inner_grad.shape)),
-            (ffn_grad, pl.BlockSpec((count, tile), lambda n, ids: (0, n))),
-            (normed, whole(size)),
-            (inverse, whole(inverse.shape)),
-            (vectors, whole(vectors.shape)),
-        ]
-        + [(p, ANY) for p in weights.arrays + inner.arrays]
-        + [(d, ANY) for d in deps],
-        [
-            (struct(size, BF), whole(size)),
-            (struct(size, F32), whole(size)),
-            (struct(size, BF), whole(size)),
+            (struct(size, BF), ANY),
+            (struct(size, F32), ANY),
+            (struct(size, BF), ANY),
             (struct((8, width), F32), whole((8, width))),
         ],
         [
             pltpu.VMEM(size, F32),
-            pltpu.VMEM((width, wide), BF),
-            pltpu.SemaphoreType.DMA((weights.count,)),
+            pltpu.VMEM(size, F32),
+            pltpu.VMEM(size, F32),
+            pltpu.VMEM(size, BF),
+            pltpu.VMEM(size, BF),
+            pltpu.VMEM((count, wide), BF),
+            pltpu.VMEM((steps, width, tile), BF),
+            pltpu.SemaphoreType.DMA((steps, inner.count)),
             pltpu.VMEM((width, width), BF),
             pltpu.SemaphoreType.DMA((weights.count,)),
+            pltpu.SemaphoreType.DMA((2,)),
+            pltpu.SemaphoreType.DMA((steps,)),
+            pltpu.SemaphoreType.DMA((3,)),
         ],
     )
 
@@ -678,6 +785,7 @@
     return kernel(
         body,
         "inputs_back",
+        10,
         ids,
         (width // tile,),
         [(base, block)]
@@ -729,120 +837,160 @@
             chosen.append(jnp.concatenate(picked, axis=1))
         return chosen, [whole(picked.shape) for picked in chosen]
 
-    def right_specs(self):
-        specs, lo = [], 0
-        for right in self.rights:
-            count = right.shape[1] // self.tile
-            specs.append(
-                pl.BlockSpec(
-                    (right.shape[0], self.tile),
-                    lambda n, ids, lo=lo, c=count: (0, jnp.clip(n - lo, 0, c - 1)),
+    def multiply(self, name, micros, core, got, outs, groups, targets, deps):
+        net, width, tile = self.net, self.width, self.tile
+        rows, tokens = net.chips * width, self.left[0].shape[0]
+        ready = width % 128 != 0
+        lefts = self.lefts(core)[0] if ready else self.left
+        tiles = []
+        for right, use in zip(range(len(self.rights)), self.uses):
+            for at in range(0, self.rights[right].shape[1], tile):
+                tiles.append((right, at, use))
+        extra = [] if got is None else [got]
+        cuts = [t for t in range(1, len(tiles)) if tiles[t][2] != tiles[t - 1][2]]
+
+        def body(ids_ref, *refs):
+            left_hbm = refs[: len(lefts)]
+            right_hbm = refs[len(lefts) : len(lefts) + len(self.rights)]
+            got_hbm = refs[len(lefts) + len(self.rights)]
+            scratch = refs[len(refs) - 7 - len(extra) :]
+            out_hbm = refs[len(refs) - 7 - len(extra) - len(outs) : len(refs) - 7 - len(extra)]
+            left_ref, right_ref, out_ref, left_sems, right_sems, got_sems, out_sems = scratch[:7]
+            fetch_left = []
+            for i, source in enumerate(left_hbm):
+                if ready:
+                    pairs = [(source, left_ref.at[i])]
+                else:
+                    pairs = []
+                    for j in range(net.chips):
+                        at = ((ids_ref[0] ^ j) * 2 + (ids_ref[1] ^ core)) * width
+                        place = (slice(None), slice(j * width, (j + 1) * width))
+                        pairs.append((source.at[:, aligned(at, width)], left_ref.at[i].at[place]))
+                fetch_left.append(copies(pairs, left_sems, i))
+            fetch_right = [
+                pltpu.make_async_copy(
+                    right_hbm[r].at[:, at : at + tile], right_ref.at[t], right_sems.at[t]
                 )
-            )
-            lo += count
-        return specs
-
-    def product(self, left_refs, right_refs, step, then):
-        each = len(left_refs) // len(self.left)
-        lo = 0
-        for ref, right, use in zip(right_refs, self.rights, self.uses):
-            count = right.shape[1] // self.tile
-
-            @pl.when((step >= lo) & (step < lo + count))
-            def _():
-                left = [part[...] for part in left_refs[use * each : (use + 1) * each]]
-                if each > 1 and self.width < 512:
-                    left = [jnp.concatenate(left, axis=1)]
-                for i, part in enumerate(left):
-                    then(i * part.shape[1], dot_tn(part, ref[...]))
-
-            lo += count
+                for t, (r, at, _) in enumerate(tiles)
+            ]
+            fetch_got = [
+                pltpu.make_async_copy(
+                    got_hbm.at[:, t * tile : (t + 1) * tile], scratch[7].at[t], got_sems.at[t]
+                )
+                for t in range(len(tiles) if extra else 0)
+            ]
+            waited = set()
+            for t, (_, _, use) in enumerate(tiles):
+                if use not in waited:
+                    start_all(fetch_left[use])
+                    waited.add(use)
+                fetch_right[t].start()
+                if extra:
+                    fetch_got[t].start()
+            def part(t, which):
+                use = sum(((t >= cut).astype(jnp.int32) for cut in cuts), jnp.int32(0))
+                there = [right_ref.at[t]] + [ref.at[t] for ref in scratch[7:]]
+                for ref, sems in zip(there, (right_sems, got_sems)):
+                    pltpu.make_async_copy(ref, ref, sems.at[t]).wait()
+                value = dot_tn(left_ref[use], right_ref[t])
+                for ref in there[1:]:
+                    value = value + ref[...].astype(F32)
+                out_ref[t] = value.astype(BF)
+                return copies(
+                    [
+                        (
+                            out_ref.at[t].at[first : first + n, :],
+                            out_hbm[kind].at[row : row + n, aligned(column, tile)],
+                        )
+                        for first, n, kind, row, column in targets(t, which)
+                    ],
+                    out_sems,
+                    t,
+                )
+
+            count = len(tiles)
+            group = count // groups
+            waited = 0
+            for which in range(groups):
+                last = tiles[(which + 1) * group - 1][2]
+                while waited <= last:
+                    wait_for(fetch_left[waited])
+                    waited += 1
+
+                @pl.loop(which * group, (which + 1) * group)
+                def _(t):
+                    start_all(part(t, which))
+
+            for t in range(count):
+                wait_for(
+                    pltpu.make_async_copy(
+                        out_ref.at[t].at[first : first + n, :],
+                        out_ref.at[t].at[first : first + n, :],
+                        out_sems.at[t, i],
+                    )
+                    for i, (first, n, _, _, _) in enumerate(targets(t, t // group))
+                )
+
+        count = len(tiles)
+        return kernel(
+            body,
+            name,
+            micros,
+            self.ids,
+            (1,),
+            [(a, ANY) for a in list(lefts) + self.rights + extra + list(deps)],
+            [(o, ANY) for o in outs],
+            [
+                pltpu.VMEM((len(lefts), tokens, rows), BF),
+                pltpu.VMEM((count, tokens, tile), BF),
+                pltpu.VMEM((count, rows, tile), BF),
+                pltpu.SemaphoreType.DMA((len(lefts), net.chips)),
+                pltpu.SemaphoreType.DMA((count,)),
+                pltpu.SemaphoreType.DMA((count,)),
+                pltpu.SemaphoreType.DMA((count, net.chips)),
+            ]
+            + [pltpu.VMEM((count, rows, tile), BF) for _ in extra],
+        )
 
     def other_core(self, *deps):
-        lefts, left_specs = self.lefts(1)
         rows = self.net.chips * self.width
-
-        def body(ids_ref, *refs):
-            out_ref = refs[-1]
-
-            def store(at, value):
-                out_ref[at : at + value.shape[0], :] = value.astype(BF)
-
-            self.product(
-                refs[: len(lefts)],
-                refs[len(lefts) : len(lefts) + len(self.rights)],
-                pl.program_id(0),
-                store,
-            )
-
-        (self.sent,) = kernel(
-            body,
+        (self.sent,) = self.multiply(
             "rows_of_other_core",
-            self.ids,
-            (self.columns // self.tile,),
-            list(zip(lefts + self.rights, left_specs + self.right_specs()))
-            + [(d, ANY) for d in deps],
-            [
-                (
-                    struct((rows, self.columns), BF),
-                    pl.BlockSpec((rows, self.tile), lambda n, ids: (0, n)),
-                )
-            ],
-            [],
+            7,
+            1,
+            None,
+            [struct((rows, self.columns), BF)],
+            1,
+            lambda t, _: [(0, rows, 0, 0, t * self.tile)],
+            deps,
         )
-        self.got = self.net.across_core(self.sent)
-        return self.sent
+        return self.exchange(self.sent)
+
+    def exchange(self, sent):
+        self.got = self.net.across_core(sent)
+        return sent
 
     def own_core(self, *deps):
-        lefts, left_specs = self.lefts(0)
-        rows, tile = self.net.chips * self.width, self.tile
-        steps = self.columns // tile
-        half = steps // 2
+        rows, tile, width = self.net.chips * self.width, self.tile, self.width
+        half = self.columns // tile // 2
         sides = [split_hops(self.kept[s], self.bits[s][0]) for s in range(2)]
 
-        def body(ids_ref, *refs):
-            got_ref = refs[len(lefts) + len(self.rights)]
-            out_refs = refs[-4:]
-            step = pl.program_id(0)
-
-            def store(at, value):
-                value = (value + got_ref[at : at + value.shape[0], :].astype(F32)).astype(BF)
-                for side in range(2):
-
-                    @pl.when((step >= side * half) & (step < (side + 1) * half))
-                    def _():
-                        for which, hops in enumerate(sides[side]):
-                            for i, j in enumerate(hops):
-                                row = j * self.width - at
-                                if 0 <= row < value.shape[0]:
-                                    out_refs[side * 2 + which][
-                                        i * self.width : (i + 1) * self.width, :
-                                    ] = value[row : row + self.width]
-
-            self.product(
-                refs[: len(lefts)],
-                refs[len(lefts) : len(lefts) + len(self.rights)],
-                step,
-                store,
-            )
-
-        outs = []
-        for side in range(2):
-            spec = pl.BlockSpec(
-                (rows // 2, tile),
-                lambda n, ids, side=side: (0, jnp.clip(n - side * half, 0, half - 1)),
-            )
-            outs += [(struct((rows // 2, self.columns // 2), BF), spec)] * 2
-        out = kernel(
-            body,
+        def targets(t, side):
+            return [
+                (j * width, width, side * 2 + which, i * width, (t - side * half) * tile)
+                for which, hops in enumerate(sides[side])
+                for i, j in enumerate(hops)
+            ]
+
+        out = self.multiply(
             "rows_of_own_core",
-            self.ids,
-            (steps,),
-            list(zip(lefts + self.rights, left_specs + self.right_specs()))
-            + [(self.got, pl.BlockSpec((rows, tile), lambda n, ids: (0, n)))]
-            + [(d, ANY) for d in deps],
-            outs,
-            [],
+            9,
+            0,
+            self.got,
+            [struct((rows // 2, self.columns // 2), BF)] * 4,
+            2,
+            targets,
+            deps,
         )
         self.held = [out[0], out[2]]
         self.away = [out[1], out[3]]
@@ -877,6 +1025,7 @@
         out = kernel(
             body,
             "fold",
+            4,
             self.ids,
             (columns // tile,),
             [(a, block) for s in range(2) for a in (self.held[s], self.arrived[s])]
@@ -918,6 +1067,7 @@
             keep, away = kernel(
                 body,
                 "fold_z",
+                3,
                 self.ids,
                 (1,),
                 [
@@ -990,36 +1140,35 @@
     gather_a.ordered()
     gather_a.plane()
     gather_b = Gather(net, tie(inner_weight, gather_a.block), ids, True)
-    arrived = gather_a.relay(*gather_b.along)
+    gather_a.relay(*gather_b.along)
+    gather_b.ordered()
     weights_a = gather_a.cores()
-    gather_b.ordered(*arrived)
     gather_b.plane(*weights_a.arrays)
     queries, keys, values, vectors = project(ids, tokens, weights_a)
-    gather_c = Gather(
-        net, tie(outer_weight, gather_b.block, *weights_a.arrays), ids, True, queries
-    )
     spread = inner_bias.shape[0] // mine
     inner_bias_full = vectors[8 : 8 + spread].reshape(spread, net.count, mine)
     inner_bias_full = inner_bias_full.swapaxes(0, 1).reshape(1, -1)
     mixed, totals = attend_forward(segment_ids, queries, keys, values)
-    arrived = gather_b.relay(mixed, *gather_c.along)
+    gather_c = Gather(net, tie(outer_weight, queries), ids, True, mixed)
+    arrived = gather_b.relay(mixed)
+    gather_c.ordered()
+    gather_c.plane(*arrived)
     weights_b = gather_b.cores()
-    gather_c.ordered(*arrived)
-    gather_c.plane()
     normed, inverse, normed_low = close_attention(ids, mixed, tokens, weights_a, vectors)
     act, slope = ffn_in(ids, normed_low, weights_b, inner_bias_full)
     gather_c.relay(act)
     weights_c = gather_c.cores()
     grad_out = out_grad.reshape(tokens.shape)
-    outputs, ffn_grad, branch_grad, ffn_sums = ffn_out(
+    outputs, ffn_grad, branch_grad, ffn_sums, sent = ffn_out(
         ids, act, normed, grad_out, weights_c, vectors
     )
-    outer_sum = RowSum(net, [(act, branch_grad)], ids, 512)
-    last = outer_sum.other_core()
-    inner_grad, inner_sums = ffn_back(ids, branch_grad, slope, weights_c, [last])
-    last = outer_sum.own_core(inner_grad)
+    outer_sum = RowSum(net, [(act, branch_grad)], ids, 256)
+    last = outer_sum.exchange(sent)
+    lefts = RowSum(net, [(normed_low, slope)], ids, 1024).lefts(1)
+    inner_grad, inner_sums, sent = ffn_back(ids, branch_grad, slope, weights_c, *lefts, [last])
     inner_sum = RowSum(net, [(normed_low, inner_grad)], ids, 1024)
-    last = inner_sum.other_core(last)
+    last = inner_sum.exchange(sent)
+    last = outer_sum.own_core(last)
     attn_grad, attn_sum_grad, mixed_grad, attn_sums = attention_norm_back(
         ids, inner_grad, ffn_grad, normed, inverse, weights_b, weights_a, vectors, [last]
     )
@@ -1027,6 +1176,9 @@
     last = inner_sum.own_core(last)
     query_grad, key_grad, value_grad, grad_query_bias, grad_value_bias = attend_backward(
         segment_ids, queries, keys, values, mixed_grad, totals, [last]
+    )
+    input_grad = inputs_back(
+        ids, attn_sum_grad, (query_grad, key_grad, value_grad), weights_a, []
     )
     inputs_sum = RowSum(
         net,
@@ -1034,17 +1186,14 @@
         ids,
         1024,
     )
-    last = inputs_sum.other_core(*outer_sum.arrived, *inner_sum.arrived)
+    last = inputs_sum.other_core(input_grad, *outer_sum.arrived, *inner_sum.arrived)
     last = inner_sum.fold(last)
     last = outer_sum.fold_z(last)
     last = inputs_sum.own_core(last)
     outer_sum.fold_far(last)
     last = inner_sum.fold_z(last)
-    input_grad = inputs_back(
-        ids, attn_sum_grad, (query_grad, key_grad, value_grad), weights_a, [last, outer_sum.came]
-    )
-    shard_outer = outer_sum.finish(input_grad)
-    last = inputs_sum.fold(input_grad)
+    last = inputs_sum.fold(last, outer_sum.came)
+    shard_outer = outer_sum.finish(last)
     inner_sum.fold_far(last)
     last = inputs_sum.fold_z(inner_sum.came)
     shard_inner = inner_sum.finish(last)

time: 430 us -> 395 us (0.919); the launches traced: 422 us -> 394 us
  Pallas kernels: 200 us -> 180 us
  starting transfers between devices: 63.2 us -> 58.9 us
    pallas_call x19 -> x17, Pallas kernels: 158 us -> 139 us  [kernel(): pl.pallas_call(body, out_shape=[o for o, _ in outs], grid_spec=pltpu.Pref...]
    ppermute x57, waiting for transfers between devices: 128 us -> 123 us  [swap(): return lax.ppermute(value, AXES, pairs)]
    unnamed x88 -> x86, local copies, waits for them, and re-layouts: 10.6 us -> 9.89 us
  transfers between devices with their start and end apart: 58 -> 58, of which waited for: 24 -> 25; matrix products, arithmetic and copies ran while one was open for 4% -> 4% of each run, Pallas kernels for 32% -> 36%
where the time goes in v3:
time: 395 us; the launch traced here: 394 us
  Pallas kernels  180 us (46%)
  waiting for transfers between devices  125 us (32%)
  starting transfers between devices  58.9 us (15%)
  local copies, waits for them, and re-layouts  22.6 us (6%)
  other arithmetic  5.56 us (1%)
    pallas_call x17, Pallas kernels, kernel(): pl.pallas_call(body, out_shape=[o for o, _ in outs], grid_spec=pltpu.Pref...  139 us
    ppermute x57, waiting for transfers between devices, swap(): return lax.ppermute(value, AXES, pairs)  123 us
    ppermute x57, starting transfers between devices, swap(): return lax.ppermute(value, AXES, pairs)  54.9 us
    pallas_call x1, Pallas kernels, attend_backward(): pl.pallas_call(attend_backward_body, out_shape=[jax.ShapeDtypeStruct((tok...  17 us
    pallas_call x1, Pallas kernels, attend_forward(): pl.pallas_call(attend_forward_body, out_shape=[jax.ShapeDtypeStruct((toke...  12.8 us
    unnamed x86, local copies, waits for them, and re-layouts  9.89 us
    pallas_call x3, Pallas kernels, in_z_order(): pl.pallas_call(body, out_shape=struct((net.inner * rows, columns), BF), g...  9.53 us
  transfers between devices with their start and end apart: 58, of which 25 were waited for; matrix products, arithmetic and copies ran while one was open for 4% of the time, Pallas kernels for 36%

profile of v3, /device:TPU:0, one launch (start us, length us, event | category | flops | bytes accessed | tf_op | source)
XLA Modules:
  0.0 393.7 jit_solution(9179964693687060712)
XLA Ops:
  2.6 4.0 %collective-permute-start.1 = (bf16[32,4224]{1,0:T(8,128)(2,1)}, bf16[32,4224]{1,0:T(8,128)(2,1)S(1)}, u32[]{:S(2)}, u32[]{:S(2)}) collective-permute-start(bf16[32,4224]{1,0:T(8,128)(2,1)} %first_shard.1.refs_0_), channel_id=1, source_target_pairs={{0,2},{1,3},{2,0},{3,1},{4,6},{5,7},{6,4},{7,5},{8,10},{9,11},{10,... | collective-permute-start | bytes 811016 | tf_op jit(solution)/shard_map/ppermute | solution.py:195
  8.2 11.0 %collective-permute-done.1.refs_2_ = bf16[32,4224]{1,0:T(8,128)(2,1)S(1)} collective-permute-done((bf16[32,4224]{1,0:T(8,128)(2,1)}, bf16[32,4224]{1,0:T(8,128)(2,1)S(1)}, u32[]{:S(2)}, u32[]{:S(2)}) %collective-permute-start.1) | collective-permute-done | bytes 270368 | tf_op jit(solution)/shard_map/ppermute | solution.py:195
  20.5 6.3 %collective-permute-done.2.refs_3_ = bf16[32,4224]{1,0:T(8,128)(2,1)S(1)} collective-permute-done((bf16[32,4224]{1,0:T(8,128)(2,1)S(1)}, bf16[32,4224]{1,0:T(8,128)(2,1)S(1)}, u32[]{:S(2)}, u32[]{:S(2)}) %collective-permute-start.2) | collective-permute-done | bytes 270368 | tf_op jit(solution)/shard_map/ppermute | solution.py:195
  39.2 9.4 %collective-permute-done.6.refs_2_ = bf16[32,4096]{1,0:T(8,128)(2,1)S(1)} collective-permute-done((bf16[32,4096]{1,0:T(8,128)(2,1)S(1)}, bf16[32,4096]{1,0:T(8,128)(2,1)S(1)}, u32[]{:S(2)}, u32[]{:S(2)}) %collective-permute-start.6) | collective-permute-done | bytes 262176 | tf_op jit(solution)/shard_map/ppermute | solution.py:195
  49.2 6.5 %collective-permute-done.4.refs_2_ = bf16[128,4224]{1,0:T(8,128)(2,1)S(1)} collective-permute-done((bf16[128,4224]{1,0:T(8,128)(2,1)}, bf16[128,4224]{1,0:T(8,128)(2,1)S(1)}, u32[]{:S(2)}, u32[]{:S(2)}) %collective-permute-start.4) | collective-permute-done | bytes 1081376 | tf_op jit(solution)/shard_map/ppermute | solution.py:195
  60.4 11.6 %collective-permute-done.9.refs_4_ = bf16[64,4224]{1,0:T(8,128)(2,1)} collective-permute-done((bf16[64,4224]{1,0:T(8,128)(2,1)S(1)}, bf16[64,4224]{1,0:T(8,128)(2,1)}, u32[]{:S(2)}, u32[]{:S(2)}) %collective-permute-start.9) | collective-permute-done | bytes 540704 | tf_op jit(solution)/shard_map/ppermute | solution.py:195
  78.5 9.6 %project.1 = (bf16[512,1024]{1,0:T(8,128)(2,1)}, bf16[512,1024]{1,0:T(8,128)(2,1)}, bf16[512,1024]{1,0:T(8,128)(2,1)}, f32[16,1024]{1,0:T(8,128)}) custom-call(s32[3]{0:T(128)} %pad_add_fusion.ids_ref, bf16[512,1024]{1,0:T(8,128)(2,1)} %bitcast.26, bf16[128,4224]{1,0:T(8,128)(2,1)} %in_z_order.3.refs_0_, bf16[128,4224]{1,0:T(8,128)(2,1)} %copy-done.1, ...), custom_call_target="tpu_custom_call" | custom-call | flops 1 | bytes 3000000 | tf_op jit(solution)/shard_map/project/pallas_call | solution.py:373
  88.2 4.4 %collective-permute-start.25 = (bf16[128,1024]{1,0:T(8,128)(2,1)S(1)}, bf16[128,1024]{1,0:T(8,128)(2,1)}, u32[]{:S(2)}, u32[]{:S(2)}) collective-permute-start(bf16[128,1024]{1,0:T(8,128)(2,1)S(1)} %copy-done.36), channel_id=1, source_target_pairs={{0,2},{1,3},{2,0},{3,1},{4,6},{5,7},{6,4},{7,5},{8,10},{9,11},{10,... | collective-permute-start | bytes 786440 | tf_op jit(solution)/shard_map/ppermute | solution.py:195
  92.6 12.8 %attend_forward.1 = (bf16[512,1024]{1,0:T(8,128)(2,1)}, f32[1,8,8,512]{3,2,1,0:T(8,128)}) custom-call(s32[1,1,512]{2,1,0:T(1,128)} %bitcast.37, bf16[512,1024]{1,0:T(8,128)(2,1)} %get-tuple-element.112.q_ref, bf16[512,1024]{1,0:T(8,128)(2,1)} %get-tuple-element.113.k_ref, bf16[512,1024]{1,0:T(8,128)(2,1)} %get-tuple-element.114.v_ref), custom_call_target="tpu_custom_call" | custom-call | flops 1 | bytes 3900000 | tf_op jit(solution)/shard_map/attend_forward/pallas_call | solution.py:154
  110.3 7.2 %collective-permute-done.24.refs_1_ = bf16[128,1024]{1,0:T(8,128)(2,1)S(1)} collective-permute-done((bf16[128,1024]{1,0:T(8,128)(2,1)S(1)}, bf16[128,1024]{1,0:T(8,128)(2,1)S(1)}, u32[]{:S(2)}, u32[]{:S(2)}) %collective-permute-start.24) | collective-permute-done | bytes 262176 | tf_op jit(solution)/shard_map/ppermute | solution.py:195
  129.3 6.9 %close_attention.1 = (f32[512,1024]{1,0:T(8,128)}, f32[512,128]{1,0:T(8,128)}, bf16[512,1024]{1,0:T(8,128)(2,1)}) custom-call(s32[3]{0:T(128)} %pad_add_fusion.ids_ref, bf16[512,1024]{1,0:T(8,128)(2,1)} %get-tuple-element.115.m_ref.refs_0_, bf16[512,1024]{1,0:T(8,128)(2,1)} %bitcast.27, f32[16,1024]{1,0:T(8,128)} %get-tuple-element.111.vec_ref, ...), custom_call_target="tpu_custom_call" | custom-call | flops 1 | bytes 2100000 | tf_op jit(solution)/shard_map/close_attention/pallas_call | solution.py:373
  138.2 13.9 %ffn_in.1 = (bf16[512,4096]{1,0:T(8,128)(2,1)}, f32[512,4096]{1,0:T(8,128)}) custom-call(s32[3]{0:T(128)} %pad_add_fusion.ids_ref, bf16[512,1024]{1,0:T(8,128)(2,1)} %get-tuple-element.116.x_ref.refs_0_.refs_1_.refs_2_.refs_3_, f32[1,4096]{1,0:T(1,128)} %reshape.126.bias_ref, bf16[128,4096]{1,0:T(8,128)(2,1)} %in_z_order.4.refs_0_.refs_10_, ...), custom_call_target="tpu_custom_call" | custom-call | flops 1 | bytes 3900000 | tf_op jit(solution)/shard_map/ffn_in/pallas_call | solution.py:373
  157.3 10.0 %collective-permute-done.30.refs_4_.refs_8_ = bf16[256,1024]{1,0:T(8,128)(2,1)S(1)} collective-permute-done((bf16[256,1024]{1,0:T(8,128)(2,1)S(1)}, bf16[256,1024]{1,0:T(8,128)(2,1)S(1)}, u32[]{:S(2)}, u32[]{:S(2)}) %collective-permute-start.30) | collective-permute-done | bytes 524320 | tf_op jit(solution)/shard_map/ppermute | solution.py:195
  172.4 15.6 %ffn_out.1 = (bf16[512,1024]{1,0:T(8,128)(2,1)}, f32[512,1024]{1,0:T(8,128)}, bf16[512,1024]{1,0:T(8,128)(2,1)}, f32[8,1024]{1,0:T(8,128)}, bf16[2048,1024]{1,0:T(8,128)(2,1)}) custom-call(s32[3]{0:T(128)} %pad_add_fusion.ids_ref, f32[16,1024]{1,0:T(8,128)} %get-tuple-element.111.vec_ref, bf16[512,4096]{1,0:T(8,128)(2,1)} %get-tuple-element.124.act_hbm.refs_0_, ...), custom_call_target="tpu_custom_call" | custom-call | flops 1 | bytes 5399999 | tf_op jit(solution)/shard_map/ffn_out/pallas_call | solution.py:373
  188.2 14.0 %ffn_back.1 = (bf16[512,4096]{1,0:T(8,128)(2,1)}, f32[8,4096]{1,0:T(8,128)}, bf16[512,4096]{1,0:T(8,128)(2,1)}) custom-call(s32[3]{0:T(128)} %pad_add_fusion.ids_ref, bf16[512,1024]{1,0:T(8,128)(2,1)} %get-tuple-element.137.grad_ref.refs_1_, f32[512,4096]{1,0:T(8,128)} %get-tuple-element.138.slope_ref, ...), custom_call_target="tpu_custom_call" | custom-call | flops 1 | bytes 3599999 | tf_op jit(solution)/shard_map/ffn_back/pallas_call | solution.py:373
  202.6 7.8 %rows_of_own_core.3 = (bf16[1024,512]{1,0:T(8,128)(2,1)}, bf16[1024,512]{1,0:T(8,128)(2,1)}, bf16[1024,512]{1,0:T(8,128)(2,1)}, bf16[1024,512]{1,0:T(8,128)(2,1)}) custom-call(s32[3]{0:T(128)} %pad_add_fusion.ids_ref, bf16[512,4096]{1,0:T(8,128)(2,1)} %get-tuple-element.124.act_hbm.refs_0_, bf16[512,1024]{1,0:T(8,128)(2,1)} %get-tuple-element.137.grad_ref.refs_1_, ...), custom_call_target="tpu_custom_call" | custom-call | flops 1 | bytes 2699999 | tf_op jit(solution)/shard_map/rows_of_own_core/pallas_call | solution.py:373
  214.1 15.8 %attention_norm_back.1 = (bf16[512,1024]{1,0:T(8,128)(2,1)}, f32[512,1024]{1,0:T(8,128)}, bf16[512,1024]{1,0:T(8,128)(2,1)}, f32[8,1024]{1,0:T(8,128)}) custom-call(s32[3]{0:T(128)} %pad_add_fusion.ids_ref, f32[512,128]{1,0:T(8,128)} %get-tuple-element.136.inverse_ref, f32[16,1024]{1,0:T(8,128)} %get-tuple-element.111.vec_ref, ...), custom_call_target="tpu_custom_call" | custom-call | flops 1 | bytes 4800000 | tf_op jit(solution)/shard_map/attention_norm_back/pallas_call | solution.py:373
  229.9 6.0 %collective-permute-done.38.refs_1_ = bf16[1024,512]{1,0:T(8,128)(2,1)S(1)} collective-permute-done((bf16[1024,512]{1,0:T(8,128)(2,1)}, bf16[1024,512]{1,0:T(8,128)(2,1)S(1)}, u32[]{:S(2)}, u32[]{:S(2)}) %collective-permute-start.38) | collective-permute-done | bytes 1048608 | tf_op jit(solution)/shard_map/ppermute | solution.py:195
  238.4 4.0 %fold.3 = (bf16[512,512]{1,0:T(8,128)(2,1)}, bf16[512,512]{1,0:T(8,128)(2,1)}, bf16[512,512]{1,0:T(8,128)(2,1)}, bf16[512,512]{1,0:T(8,128)(2,1)}) custom-call(s32[3]{0:T(128)} %pad_add_fusion.ids_ref, bf16[1024,512]{1,0:T(8,128)(2,1)} %get-tuple-element.143.refs_20_.refs_0_, bf16[1024,512]{1,0:T(8,128)(2,1)} %copy-done.26, ...), custom_call_target="tpu_custom_call" | custom-call | flops 1 | bytes 1200000 | tf_op jit(solution)/shard_map/fold/pallas_call | solution.py:373
  242.4 7.9 %rows_of_own_core.4 = (bf16[256,2048]{1,0:T(8,128)(2,1)}, bf16[256,2048]{1,0:T(8,128)(2,1)}, bf16[256,2048]{1,0:T(8,128)(2,1)}, bf16[256,2048]{1,0:T(8,128)(2,1)}) custom-call(s32[3]{0:T(128)} %pad_add_fusion.ids_ref, bf16[512,1024]{1,0:T(8,128)(2,1)} %get-tuple-element.116.x_ref.refs_0_.refs_1_.refs_2_.refs_3_, ...), custom_call_target="tpu_custom_call" | custom-call | flops 1 | bytes 2699999 | tf_op jit(solution)/shard_map/rows_of_own_core/pallas_call | solution.py:373
  254.4 17.0 %attend_backward.1 = (bf16[512,1024]{1,0:T(8,128)(2,1)}, bf16[512,1024]{1,0:T(8,128)(2,1)}, bf16[512,1024]{1,0:T(8,128)(2,1)}, f32[1,8,1024]{2,1,0:T(8,128)}, f32[1,8,1024]{2,1,0:T(8,128)}) custom-call(s32[1,1,512]{2,1,0:T(1,128)} %bitcast.38, bf16[512,1024]{1,0:T(8,128)(2,1)} %get-tuple-element.112.q_ref, bf16[512,1024]{1,0:T(8,128)(2,1)} %get-tuple-element.113.k_ref, ...), custom_call_target="tpu_custom_call" | custom-call | flops 1 | bytes 5100000 | tf_op jit(solution)/shard_map/attend_backward/pallas_call | solution.py:174
  271.4 10.1 %inputs_back.1.refs_6_ = f32[512,1024]{1,0:T(8,128)} custom-call(s32[3]{0:T(128)} %pad_add_fusion.ids_ref, f32[512,1024]{1,0:T(8,128)} %get-tuple-element.144.base_ref, bf16[512,1024]{1,0:T(8,128)(2,1)} %get-tuple-element.153.q_ref.refs_3_, bf16[512,1024]{1,0:T(8,128)(2,1)} %get-tuple-element.154.k_ref.refs_4_, ...), custom_call_target="tpu_custom_call" | custom-call | flops 1 | bytes 3000000 | tf_op jit(solution)/shard_map/inputs_back/pallas_call | solution.py:373
  281.5 5.0 %collective-permute-done.40.refs_7_.refs_1_ = bf16[512,512]{1,0:T(8,128)(2,1)S(1)} collective-permute-done((bf16[512,512]{1,0:T(8,128)(2,1)}, bf16[512,512]{1,0:T(8,128)(2,1)S(1)}, u32[]{:S(2)}, u32[]{:S(2)}) %collective-permute-start.40) | collective-permute-done | bytes 524320 | tf_op jit(solution)/shard_map/ppermute | solution.py:195
  288.8 7.3 %rows_of_other_core.1.refs_4_ = bf16[512,4096]{1,0:T(8,128)(2,1)} custom-call(s32[3]{0:T(128)} %pad_add_fusion.ids_ref, bf16[512,1024]{1,0:T(8,128)(2,1)} %get-tuple-element.115.m_ref.refs_0_, bf16[512,1024]{1,0:T(8,128)(2,1)} %bitcast.28, bf16[512,1024]{1,0:T(8,128)(2,1)} %get-tuple-element.150.refs_4_.refs_2_, ...), custom_call_target="tpu_custom_call" | custom-call | flops 1 | bytes 2100000 | tf_op jit(solution)/shard_map/rows_of_other_core/pallas_call | solution.py:373
  296.2 4.0 %fold.4 = (bf16[128,2048]{1,0:T(8,128)(2,1)}, bf16[128,2048]{1,0:T(8,128)(2,1)}, bf16[128,2048]{1,0:T(8,128)(2,1)}, bf16[128,2048]{1,0:T(8,128)(2,1)}) custom-call(s32[3]{0:T(128)} %pad_add_fusion.ids_ref, bf16[256,2048]{1,0:T(8,128)(2,1)} %get-tuple-element.152.rest_0_.refs_0_, bf16[256,2048]{1,0:T(8,128)(2,1)} %copy-done.6, ...), custom_call_target="tpu_custom_call" | custom-call | flops 1 | bytes 1200000 | tf_op jit(solution)/shard_map/fold/pallas_call | solution.py:373
  307.7 8.2 %rows_of_own_core.5 = (bf16[256,2048]{1,0:T(8,128)(2,1)}, bf16[256,2048]{1,0:T(8,128)(2,1)}, bf16[256,2048]{1,0:T(8,128)(2,1)}, bf16[256,2048]{1,0:T(8,128)(2,1)}) custom-call(s32[3]{0:T(128)} %pad_add_fusion.ids_ref, bf16[512,1024]{1,0:T(8,128)(2,1)} %get-tuple-element.115.m_ref.refs_0_, bf16[512,1024]{1,0:T(8,128)(2,1)} %bitcast.29, ...), custom_call_target="tpu_custom_call" | custom-call | flops 1 | bytes 2699999 | tf_op jit(solution)/shard_map/rows_of_own_core/pallas_call | solution.py:373
  323.7 14.7 %collective-permute-done.50.refs_5_ = bf16[128,1024]{1,0:T(8,128)(2,1)S(1)} collective-permute-done((bf16[128,1024]{1,0:T(8,128)(2,1)S(1)}, bf16[128,1024]{1,0:T(8,128)(2,1)S(1)}, u32[]{:S(2)}, u32[]{:S(2)}) %collective-permute-start.50) | collective-permute-done | bytes 262176 | tf_op jit(solution)/shard_map/ppermute | solution.py:195
  341.9 4.1 %fold.5 = (bf16[128,2048]{1,0:T(8,128)(2,1)}, bf16[128,2048]{1,0:T(8,128)(2,1)}, bf16[128,2048]{1,0:T(8,128)(2,1)}, bf16[128,2048]{1,0:T(8,128)(2,1)}) custom-call(s32[3]{0:T(128)} %pad_add_fusion.ids_ref, bf16[256,2048]{1,0:T(8,128)(2,1)} %get-tuple-element.164.refs_4_.refs_0_, bf16[256,2048]{1,0:T(8,128)(2,1)} %copy-done.21, ...), custom_call_target="tpu_custom_call" | custom-call | flops 1 | bytes 1200000 | tf_op jit(solution)/shard_map/fold/pallas_call | solution.py:373
  354.2 7.6 %collective-permute-done.54.refs_4_ = bf16[32,4096]{1,0:T(8,128)(2,1)S(1)} collective-permute-done((bf16[32,4096]{1,0:T(8,128)(2,1)S(1)}, bf16[32,4096]{1,0:T(8,128)(2,1)S(1)}, u32[]{:S(2)}, u32[]{:S(2)}) %collective-permute-start.54) | collective-permute-done | bytes 262176 | tf_op jit(solution)/shard_map/ppermute | solution.py:195
  371.8 3.9 all-to-all-start
  375.7 4.1 %collective-permute-done.55 = bf16[64,4096]{1,0:T(8,128)(2,1)S(1)} collective-permute-done((bf16[64,4096]{1,0:T(8,128)(2,1)}, bf16[64,4096]{1,0:T(8,128)(2,1)S(1)}, u32[]{:S(2)}, u32[]{:S(2)}) %collective-permute-start.55) | collective-permute-done | bytes 524320 | tf_op jit(solution)/shard_map/ppermute | solution.py:195
  384.3 8.6 %collective-permute-done.56 = bf16[32,4096]{1,0:T(8,128)(2,1)S(1)} collective-permute-done((bf16[32,4096]{1,0:T(8,128)(2,1)S(1)}, bf16[32,4096]{1,0:T(8,128)(2,1)S(1)}, u32[]{:S(2)}, u32[]{:S(2)}) %collective-permute-start.56) | collective-permute-done | bytes 262176 | tf_op jit(solution)/shard_map/ppermute | solution.py:195
  (235 shorter events, 113.2 us)
Async XLA Ops:
  2.6 16.6 %collective-permute-start.1 = (bf16[32,4224]{1,0:T(8,128)(2,1)}, bf16[32,4224]{1,0:T(8,128)(2,1)S(1)}, u32[]{:S(2)}, u32[]{:S(2)}) collective-permute-start(bf16[32,4224]{1,0:T(8,128)(2,1)} %first_shard.1.refs_0_), channel_id=1, source_target_pairs={{0,2},{1,3},{2,0},{3,1},{4,6},{5,7},{6,4},{7,5},{8,10},{9,11},{10,... | collective-permute-start | bytes 811016 | tf_op jit(solution)/shard_map/ppermute | solution.py:195
  31.4 24.3 %collective-permute-start.4 = (bf16[128,4224]{1,0:T(8,128)(2,1)}, bf16[128,4224]{1,0:T(8,128)(2,1)S(1)}, u32[]{:S(2)}, u32[]{:S(2)}) collective-permute-start(bf16[128,4224]{1,0:T(8,128)(2,1)} %in_z_order.3.refs_0_), channel_id=1, source_target_pairs={{0,16},{1,17},{2,18},{3,19},{4,20},{5,21},{6,22},{7,23},{8,24},{9,... | collective-permute-start | bytes 3244040 | tf_op jit(solution)/shard_map/ppermute | solution.py:195
  32.7 24.4 %collective-permute-start.3 = (bf16[128,4224]{1,0:T(8,128)(2,1)}, bf16[128,4224]{1,0:T(8,128)(2,1)S(1)}, u32[]{:S(2)}, u32[]{:S(2)}) collective-permute-start(bf16[128,4224]{1,0:T(8,128)(2,1)} %in_z_order.3.refs_0_), channel_id=1, source_target_pairs={{0,8},{1,9},{2,10},{3,11},{4,12},{5,13},{6,14},{7,15},{8,0},{9,1},... | collective-permute-start | bytes 3244040 | tf_op jit(solution)/shard_map/ppermute | solution.py:195
  37.5 18.2 %collective-permute-start.5 = (bf16[32,4096]{1,0:T(8,128)(2,1)S(1)}, bf16[32,4096]{1,0:T(8,128)(2,1)S(1)}, u32[]{:S(2)}, u32[]{:S(2)}) collective-permute-start(bf16[32,4096]{1,0:T(8,128)(2,1)S(1)} %copy-done.35), channel_id=1, source_target_pairs={{0,1},{1,0},{2,3},{3,2},{4,5},{5,4},{6,7},{7,6},{8,9},{9,8},{10,11... | collective-permute-start | bytes 786440 | tf_op jit(solution)/shard_map/ppermute | solution.py:195
  49.2 27.1 %collective-permute-start.10 = (bf16[128,4224]{1,0:T(8,128)(2,1)}, bf16[128,4224]{1,0:T(8,128)(2,1)S(1)}, u32[]{:S(2)}, u32[]{:S(2)}) collective-permute-start(bf16[128,4224]{1,0:T(8,128)(2,1)} %in_z_order.3.refs_0_), channel_id=1, source_target_pairs={{0,4},{1,5},{2,6},{3,7},{4,0},{5,1},{6,2},{7,3},{8,12},{9,13},{10,... | collective-permute-start | bytes 3244040 | tf_op jit(solution)/shard_map/ppermute | solution.py:195
  55.7 20.7 %collective-permute-start.12 = (bf16[128,4224]{1,0:T(8,128)(2,1)S(1)}, bf16[128,4224]{1,0:T(8,128)(2,1)}, u32[]{:S(2)}, u32[]{:S(2)}) collective-permute-start(bf16[128,4224]{1,0:T(8,128)(2,1)S(1)} %collective-permute-done.4.refs_2_), channel_id=1, source_target_pairs={{0,4},{1,5},{2,6},{3,7},{4,0},{5,1},{6,2},{7,3},{8,12},{9,13},{10,... | collective-permute-start | bytes 3244040 | tf_op jit(solution)/shard_map/ppermute | solution.py:195
  58.7 17.7 %collective-permute-start.11 = (bf16[128,4224]{1,0:T(8,128)(2,1)S(1)}, bf16[128,4224]{1,0:T(8,128)(2,1)}, u32[]{:S(2)}, u32[]{:S(2)}) collective-permute-start(bf16[128,4224]{1,0:T(8,128)(2,1)S(1)} %collective-permute-done.3.refs_1_), channel_id=1, source_target_pairs={{0,4},{1,5},{2,6},{3,7},{4,0},{5,1},{6,2},{7,3},{8,12},{9,13},{10,... | collective-permute-start | bytes 3244040 | tf_op jit(solution)/shard_map/ppermute | solution.py:195
  76.4 28.9 %collective-permute-start.16 = (bf16[128,4096]{1,0:T(8,128)(2,1)}, bf16[128,4096]{1,0:T(8,128)(2,1)S(1)}, u32[]{:S(2)}, u32[]{:S(2)}) collective-permute-start(bf16[128,4096]{1,0:T(8,128)(2,1)} %in_z_order.4.refs_0_.refs_10_), channel_id=1, source_target_pairs={{0,16},{1,17},{2,18},{3,19},{4,20},{5,21},{6,22},{7,23},{8,24},{9,... | collective-permute-start | bytes 3145736 | tf_op jit(solution)/shard_map/ppermute | solution.py:195
  78.0 27.3 %collective-permute-start.15 = (bf16[128,4096]{1,0:T(8,128)(2,1)}, bf16[128,4096]{1,0:T(8,128)(2,1)S(1)}, u32[]{:S(2)}, u32[]{:S(2)}) collective-permute-start(bf16[128,4096]{1,0:T(8,128)(2,1)} %in_z_order.4.refs_0_.refs_10_), channel_id=1, source_target_pairs={{0,8},{1,9},{2,10},{3,11},{4,12},{5,13},{6,14},{7,15},{8,0},{9,1},... | collective-permute-start | bytes 3145736 | tf_op jit(solution)/shard_map/ppermute | solution.py:195
  78.5 48.3 %collective-permute-start.19 = (bf16[128,4096]{1,0:T(8,128)(2,1)}, bf16[128,4096]{1,0:T(8,128)(2,1)}, u32[]{:S(2)}, u32[]{:S(2)}) collective-permute-start(bf16[128,4096]{1,0:T(8,128)(2,1)} %in_z_order.4.refs_0_.refs_10_), channel_id=1, source_target_pairs={{0,4},{1,5},{2,6},{3,7},{4,0},{5,1},{6,2},{7,3},{8,12},{9,13},{10,... | collective-permute-start | bytes 3145736 | tf_op jit(solution)/shard_map/ppermute | solution.py:195
  88.2 21.6 %collective-permute-start.25 = (bf16[128,1024]{1,0:T(8,128)(2,1)S(1)}, bf16[128,1024]{1,0:T(8,128)(2,1)}, u32[]{:S(2)}, u32[]{:S(2)}) collective-permute-start(bf16[128,1024]{1,0:T(8,128)(2,1)S(1)} %copy-done.36), channel_id=1, source_target_pairs={{0,2},{1,3},{2,0},{3,1},{4,6},{5,7},{6,4},{7,5},{8,10},{9,11},{10,... | collective-permute-start | bytes 786440 | tf_op jit(solution)/shard_map/ppermute | solution.py:195
  105.4 19.3 %collective-permute-start.18 = (bf16[64,4096]{1,0:T(8,128)(2,1)S(1)}, bf16[64,4096]{1,0:T(8,128)(2,1)S(1)}, u32[]{:S(2)}, u32[]{:S(2)}) collective-permute-start(bf16[64,4096]{1,0:T(8,128)(2,1)S(1)} %slice.106), channel_id=1, source_target_pairs={{0,8},{1,9},{2,10},{3,11},{4,12},{5,13},{6,14},{7,15},{8,0},{9,1},... | collective-permute-start | bytes 1572872 | tf_op jit(solution)/shard_map/ppermute | solution.py:195
  107.8 17.5 %collective-permute-start.17 = (bf16[64,4096]{1,0:T(8,128)(2,1)}, bf16[64,4096]{1,0:T(8,128)(2,1)}, u32[]{:S(2)}, u32[]{:S(2)}) collective-permute-start(bf16[64,4096]{1,0:T(8,128)(2,1)} %slice.105), channel_id=1, source_target_pairs={{0,16},{1,17},{2,18},{3,19},{4,20},{5,21},{6,22},{7,23},{8,24},{9,... | collective-permute-start | bytes 1572872 | tf_op jit(solution)/shard_map/ppermute | solution.py:195
  125.3 26.8 %collective-permute-start.28 = (bf16[512,1024]{1,0:T(8,128)(2,1)}, bf16[512,1024]{1,0:T(8,128)(2,1)}, u32[]{:S(2)}, u32[]{:S(2)}) collective-permute-start(bf16[512,1024]{1,0:T(8,128)(2,1)} %in_z_order.5.refs_0_.refs_4_), channel_id=1, source_target_pairs={{0,16},{1,17},{2,18},{3,19},{4,20},{5,21},{6,22},{7,23},{8,24},{9,... | collective-permute-start | bytes 3145736 | tf_op jit(solution)/shard_map/ppermute | solution.py:195
  126.8 25.5 %collective-permute-start.27 = (bf16[512,1024]{1,0:T(8,128)(2,1)}, bf16[512,1024]{1,0:T(8,128)(2,1)}, u32[]{:S(2)}, u32[]{:S(2)}) collective-permute-start(bf16[512,1024]{1,0:T(8,128)(2,1)} %in_z_order.5.refs_0_.refs_4_), channel_id=1, source_target_pairs={{0,8},{1,9},{2,10},{3,11},{4,12},{5,13},{6,14},{7,15},{8,0},{9,1},... | collective-permute-start | bytes 3145736 | tf_op jit(solution)/shard_map/ppermute | solution.py:195
  137.8 31.1 %collective-permute-start.31 = (bf16[512,1024]{1,0:T(8,128)(2,1)S(1)}, bf16[512,1024]{1,0:T(8,128)(2,1)}, u32[]{:S(2)}, u32[]{:S(2)}) collective-permute-start(bf16[512,1024]{1,0:T(8,128)(2,1)S(1)} %copy-done.3), channel_id=1, source_target_pairs={{0,4},{1,5},{2,6},{3,7},{4,0},{5,1},{6,2},{7,3},{8,12},{9,13},{10,... | collective-permute-start | bytes 3145736 | tf_op jit(solution)/shard_map/ppermute | solution.py:195
  202.2 40.2 %collective-permute-start.37 = (bf16[512,4096]{1,0:T(8,128)(2,1)}, bf16[512,4096]{1,0:T(8,128)(2,1)}, u32[]{:S(2)}, u32[]{:S(2)}) collective-permute-start(bf16[512,4096]{1,0:T(8,128)(2,1)} %get-tuple-element.142.refs_3_), channel_id=1, source_target_pairs={{0,4},{1,5},{2,6},{3,7},{4,0},{5,1},{6,2},{7,3},{8,12},{9,13},{10,... | collective-permute-start | bytes 12582920 | tf_op jit(solution)/shard_map/ppermute | solution.py:195
  210.4 25.5 %collective-permute-start.38 = (bf16[1024,512]{1,0:T(8,128)(2,1)}, bf16[1024,512]{1,0:T(8,128)(2,1)S(1)}, u32[]{:S(2)}, u32[]{:S(2)}) collective-permute-start(bf16[1024,512]{1,0:T(8,128)(2,1)} %get-tuple-element.147), channel_id=1, source_target_pairs={{0,8},{1,9},{2,10},{3,11},{4,12},{5,13},{6,14},{7,15},{8,0},{9,1},... | collective-permute-start | bytes 3145736 | tf_op jit(solution)/shard_map/ppermute | solution.py:195
  212.0 25.5 %collective-permute-start.39 = (bf16[1024,512]{1,0:T(8,128)(2,1)}, bf16[1024,512]{1,0:T(8,128)(2,1)S(1)}, u32[]{:S(2)}, u32[]{:S(2)}) collective-permute-start(bf16[1024,512]{1,0:T(8,128)(2,1)} %get-tuple-element.149), channel_id=1, source_target_pairs={{0,16},{1,17},{2,18},{3,19},{4,20},{5,21},{6,22},{7,23},{8,24},{9,... | collective-permute-start | bytes 3145736 | tf_op jit(solution)/shard_map/ppermute | solution.py:195
  250.3 36.2 %collective-permute-start.42 = (bf16[256,2048]{1,0:T(8,128)(2,1)}, bf16[256,2048]{1,0:T(8,128)(2,1)S(1)}, u32[]{:S(2)}, u32[]{:S(2)}) collective-permute-start(bf16[256,2048]{1,0:T(8,128)(2,1)} %get-tuple-element.158), channel_id=1, source_target_pairs={{0,8},{1,9},{2,10},{3,11},{4,12},{5,13},{6,14},{7,15},{8,0},{9,1},... | collective-permute-start | bytes 3145736 | tf_op jit(solution)/shard_map/ppermute | solution.py:195
  250.9 35.6 %collective-permute-start.43 = (bf16[256,2048]{1,0:T(8,128)(2,1)}, bf16[256,2048]{1,0:T(8,128)(2,1)S(1)}, u32[]{:S(2)}, u32[]{:S(2)}) collective-permute-start(bf16[256,2048]{1,0:T(8,128)(2,1)} %get-tuple-element.159), channel_id=1, source_target_pairs={{0,16},{1,17},{2,18},{3,19},{4,20},{5,21},{6,22},{7,23},{8,24},{9,... | collective-permute-start | bytes 3145736 | tf_op jit(solution)/shard_map/ppermute | solution.py:195
  252.7 33.8 %collective-permute-start.40 = (bf16[512,512]{1,0:T(8,128)(2,1)}, bf16[512,512]{1,0:T(8,128)(2,1)S(1)}, u32[]{:S(2)}, u32[]{:S(2)}) collective-permute-start(bf16[512,512]{1,0:T(8,128)(2,1)} %get-tuple-element.156), channel_id=1, source_target_pairs={{0,16},{1,17},{2,18},{3,19},{4,20},{5,21},{6,22},{7,23},{8,24},{9,... | collective-permute-start | bytes 1572872 | tf_op jit(solution)/shard_map/ppermute | solution.py:195
  252.9 33.6 %collective-permute-start.41 = (bf16[512,512]{1,0:T(8,128)(2,1)}, bf16[512,512]{1,0:T(8,128)(2,1)S(1)}, u32[]{:S(2)}, u32[]{:S(2)}) collective-permute-start(bf16[512,512]{1,0:T(8,128)(2,1)} %get-tuple-element.157), channel_id=1, source_target_pairs={{0,8},{1,9},{2,10},{3,11},{4,12},{5,13},{6,14},{7,15},{8,0},{9,1},... | collective-permute-start | bytes 1572872 | tf_op jit(solution)/shard_map/ppermute | solution.py:195
  300.2 17.1 %collective-permute-start.47 = (bf16[128,2048]{1,0:T(8,128)(2,1)}, bf16[128,2048]{1,0:T(8,128)(2,1)S(1)}, u32[]{:S(2)}, u32[]{:S(2)}) collective-permute-start(bf16[128,2048]{1,0:T(8,128)(2,1)} %get-tuple-element.168), channel_id=1, source_target_pairs={{0,16},{1,17},{2,18},{3,19},{4,20},{5,21},{6,22},{7,23},{8,24},{9,... | collective-permute-start | bytes 1572872 | tf_op jit(solution)/shard_map/ppermute | solution.py:195
  301.9 15.3 %collective-permute-start.48 = (bf16[128,2048]{1,0:T(8,128)(2,1)}, bf16[128,2048]{1,0:T(8,128)(2,1)S(1)}, u32[]{:S(2)}, u32[]{:S(2)}) collective-permute-start(bf16[128,2048]{1,0:T(8,128)(2,1)} %get-tuple-element.170), channel_id=1, source_target_pairs={{0,8},{1,9},{2,10},{3,11},{4,12},{5,13},{6,14},{7,15},{8,0},{9,1},... | collective-permute-start | bytes 1572872 | tf_op jit(solution)/shard_map/ppermute | solution.py:195
  306.3 15.8 %collective-permute-start.49 = (bf16[256,1024]{1,0:T(8,128)(2,1)}, bf16[256,1024]{1,0:T(8,128)(2,1)S(1)}, u32[]{:S(2)}, u32[]{:S(2)}) collective-permute-start(bf16[256,1024]{1,0:T(8,128)(2,1)} %get-tuple-element.173), channel_id=1, source_target_pairs={{0,1},{1,0},{2,3},{3,2},{4,5},{5,4},{6,7},{7,6},{8,9},{9,8},{10,11... | collective-permute-start | bytes 1572872 | tf_op jit(solution)/shard_map/ppermute | solution.py:195
  315.9 25.0 %collective-permute-start.45 = (bf16[256,2048]{1,0:T(8,128)(2,1)}, bf16[256,2048]{1,0:T(8,128)(2,1)S(1)}, u32[]{:S(2)}, u32[]{:S(2)}) collective-permute-start(bf16[256,2048]{1,0:T(8,128)(2,1)} %get-tuple-element.165), channel_id=1, source_target_pairs={{0,8},{1,9},{2,10},{3,11},{4,12},{5,13},{6,14},{7,15},{8,0},{9,1},... | collective-permute-start | bytes 3145736 | tf_op jit(solution)/shard_map/ppermute | solution.py:195
  317.0 24.8 %collective-permute-start.46 = (bf16[256,2048]{1,0:T(8,128)(2,1)}, bf16[256,2048]{1,0:T(8,128)(2,1)}, u32[]{:S(2)}, u32[]{:S(2)}) collective-permute-start(bf16[256,2048]{1,0:T(8,128)(2,1)} %get-tuple-element.167), channel_id=1, source_target_pairs={{0,16},{1,17},{2,18},{3,19},{4,20},{5,21},{6,22},{7,23},{8,24},{9,... | collective-permute-start | bytes 3145736 | tf_op jit(solution)/shard_map/ppermute | solution.py:195
  321.5 26.1 %collective-permute-start.53 = (bf16[64,4096]{1,0:T(8,128)(2,1)}, bf16[64,4096]{1,0:T(8,128)(2,1)}, u32[]{:S(2)}, u32[]{:S(2)}) collective-permute-start(bf16[64,4096]{1,0:T(8,128)(2,1)} %get-tuple-element.179), channel_id=1, source_target_pairs={{0,1},{1,0},{2,3},{3,2},{4,5},{5,4},{6,7},{7,6},{8,9},{9,8},{10,11... | collective-permute-start | bytes 1572872 | tf_op jit(solution)/shard_map/ppermute | solution.py:195
  322.4 16.1 %collective-permute-start.50 = (bf16[128,1024]{1,0:T(8,128)(2,1)S(1)}, bf16[128,1024]{1,0:T(8,128)(2,1)S(1)}, u32[]{:S(2)}, u32[]{:S(2)}) collective-permute-start(bf16[128,1024]{1,0:T(8,128)(2,1)S(1)} %slice.150), channel_id=1, source_target_pairs={{0,2},{1,3},{2,0},{3,1},{4,6},{5,7},{6,4},{7,5},{8,10},{9,11},{10,... | collective-permute-start | bytes 786440 | tf_op jit(solution)/shard_map/ppermute | solution.py:195
  346.0 15.7 %collective-permute-start.51 = (bf16[128,2048]{1,0:T(8,128)(2,1)}, bf16[128,2048]{1,0:T(8,128)(2,1)S(1)}, u32[]{:S(2)}, u32[]{:S(2)}) collective-permute-start(bf16[128,2048]{1,0:T(8,128)(2,1)} %get-tuple-element.175), channel_id=1, source_target_pairs={{0,16},{1,17},{2,18},{3,19},{4,20},{5,21},{6,22},{7,23},{8,24},{9,... | collective-permute-start | bytes 1572872 | tf_op jit(solution)/shard_map/ppermute | solution.py:195
  346.7 15.1 %collective-permute-start.52 = (bf16[128,2048]{1,0:T(8,128)(2,1)}, bf16[128,2048]{1,0:T(8,128)(2,1)}, u32[]{:S(2)}, u32[]{:S(2)}) collective-permute-start(bf16[128,2048]{1,0:T(8,128)(2,1)} %get-tuple-element.177), channel_id=1, source_target_pairs={{0,8},{1,9},{2,10},{3,11},{4,12},{5,13},{6,14},{7,15},{8,0},{9,1},... | collective-permute-start | bytes 1572872 | tf_op jit(solution)/shard_map/ppermute | solution.py:195
  (70 other events, 551.5 us)

commit v4 on v3

--- a/solution.py
+++ b/solution.py
@@ -1099,6 +1099,84 @@
         return tie(self.total, *deps).astype(F32) + self.came.astype(F32)
 
 
+class ZFirst:
+    def __init__(self, rows_sum):
+        self.sum, self.net = rows_sum, rows_sum.net
+        self.low = rows_sum.width // self.net.inner
+        self.usual = self.net.inner != 4 or len(rows_sum.bits[0]) != 1 or self.low % 16 != 0
+
+    def cross_near(self, *deps):
+        source, low = self.sum, self.low
+        if self.usual:
+            source.fold(*deps)
+            return source.fold_z()
+        columns = source.held[0].shape[1]
+        split = split_hops(list(range(4)), 1)
+        sides = [split_hops(source.kept[s], source.bits[s][0]) for s in range(2)]
+        size = (4 * low, 2 * columns)
+
+        def body(ids_ref, *refs):
+            for out_ref, zs in zip(refs[-2:], split):
+                for i, z in enumerate(zs):
+                    for s in range(2):
+                        for h in range(2):
+                            at = source.kept[s].index(sides[s][h][0]) * source.width
+                            at = pl.multiple_of(at + (ids_ref[2] ^ z) * low, 16)
+                            value = refs[2 * s][pl.ds(at, low), :].astype(F32)
+                            value = value + refs[2 * s + 1][pl.ds(at, low), :].astype(F32)
+                            row = (2 * i + h) * low
+                            out_ref[row : row + low, s * columns : (s + 1) * columns] = (
+                                value.astype(BF)
+                            )
+
+        self.keep, away = kernel(
+            body,
+            "cross_near",
+            6,
+            source.ids,
+            (1,),
+            [
+                (a, whole(a.shape))
+                for s in range(2)
+                for a in (source.held[s], source.arrived[s])
+            ]
+            + [(d, ANY) for d in deps],
+            [(struct(size, BF), whole(size))] * 2,
+            [],
+        )
+        self.came = self.net.swap(away, 1)
+        return self.keep
+
+    def halve(self, *deps):
+        total = tie(self.keep, *deps).astype(F32) + self.came.astype(F32)
+        half = total.shape[0] // 2
+        self.keep = total[:half].astype(BF)
+        return total[half:].astype(BF)
+
+    def cross_far(self, *deps):
+        if self.usual:
+            return self.sum.fold_far(*deps)
+        self.came = self.net.swap(self.halve(*deps), 2)
+        return self.came
+
+    def cross_chip(self, *deps):
+        if self.usual:
+            return None
+        away = self.halve(*deps)
+        half = away.shape[1] // 2
+        parts = [
+            self.net.across_chip(away[:, s * half : (s + 1) * half], self.sum.bits[s][0])
+            for s in range(2)
+        ]
+        self.came = jnp.concatenate(parts, axis=1)
+        return None
+
+    def finish(self, *deps):
+        if self.usual:
+            return self.sum.finish(*deps)
+        return tie(self.keep, *deps).astype(F32) + self.came.astype(F32)
+
+
 def shards(
     net,
     inputs,
@@ -1151,10 +1229,10 @@
     mixed, totals = attend_forward(segment_ids, queries, keys, values)
     gather_c = Gather(net, tie(outer_weight, queries), ids, True, mixed)
     arrived = gather_b.relay(mixed)
-    gather_c.ordered()
+    normed, inverse, normed_low = close_attention(ids, mixed, tokens, weights_a, vectors)
+    gather_c.ordered(normed_low)
     gather_c.plane(*arrived)
     weights_b = gather_b.cores()
-    normed, inverse, normed_low = close_attention(ids, mixed, tokens, weights_a, vectors)
     act, slope = ffn_in(ids, normed_low, weights_b, inner_bias_full)
     gather_c.relay(act)
     weights_c = gather_c.cores()
@@ -1172,13 +1250,9 @@
     attn_grad, attn_sum_grad, mixed_grad, attn_sums = attention_norm_back(
         ids, inner_grad, ffn_grad, normed, inverse, weights_b, weights_a, vectors, [last]
     )
-    last = outer_sum.fold(attn_grad)
-    last = inner_sum.own_core(last)
+    last = inner_sum.own_core(attn_grad)
     query_grad, key_grad, value_grad, grad_query_bias, grad_value_bias = attend_backward(
-        segment_ids, queries, keys, values, mixed_grad, totals, [last]
-    )
-    input_grad = inputs_back(
-        ids, attn_sum_grad, (query_grad, key_grad, value_grad), weights_a, []
+        segment_ids, queries, keys, values, mixed_grad, totals, [last, *outer_sum.arrived]
     )
     inputs_sum = RowSum(
         net,
@@ -1186,17 +1260,22 @@
         ids,
         1024,
     )
-    last = inputs_sum.other_core(input_grad, *outer_sum.arrived, *inner_sum.arrived)
+    outer = ZFirst(outer_sum)
+    last = outer.cross_near(query_grad)
+    last = inputs_sum.other_core(last, *inner_sum.arrived)
     last = inner_sum.fold(last)
-    last = outer_sum.fold_z(last)
     last = inputs_sum.own_core(last)
-    outer_sum.fold_far(last)
     last = inner_sum.fold_z(last)
-    last = inputs_sum.fold(last, outer_sum.came)
-    shard_outer = outer_sum.finish(last)
+    outer.cross_far(last)
+    last = inputs_sum.fold(last)
     inner_sum.fold_far(last)
-    last = inputs_sum.fold_z(inner_sum.came)
+    input_grad = inputs_back(
+        ids, attn_sum_grad, (query_grad, key_grad, value_grad), weights_a, [last]
+    )
+    last = inputs_sum.fold_z(input_grad)
+    outer.cross_chip(last)
     shard_inner = inner_sum.finish(last)
+    shard_outer = outer.finish(last)
     inputs_sum.fold_far(last)
     shard_inputs = inputs_sum.finish()
     shard_output, shard_query, shard_key, shard_value = (

time: 395 us -> 372 us (0.942)
  waiting for transfers between devices: 125 us -> 111 us
  local copies, waits for them, and re-layouts: 22.6 us -> 16.3 us
    ppermute x57, waiting for transfers between devices: 123 us -> 111 us  [swap(): return lax.ppermute(value, AXES, pairs)]
    pallas_call x17 -> x16, Pallas kernels: 139 us -> 136 us  [kernel(): pl.pallas_call(body, out_shape=[o for o, _ in outs], grid_spec=pltpu.Pref...]
    unnamed x86 -> x66, local copies, waits for them, and re-layouts: 9.89 us -> 7.6 us
  transfers between devices with their start and end apart: 58 -> 58, of which waited for: 25 -> 25; matrix products, arithmetic and copies ran while one was open for 4% -> 4% of each run, Pallas kernels for 36% -> 40%
where the time goes in v4:
time: 372 us; the launch traced here: 371 us
  Pallas kernels  178 us (48%)
  waiting for transfers between devices  111 us (30%)
  starting transfers between devices  59 us (16%)
  local copies, waits for them, and re-layouts  16.3 us (4%)
  other arithmetic  5.36 us (1%)
    pallas_call x16, Pallas kernels, kernel(): pl.pallas_call(body, out_shape=[o for o, _ in outs], grid_spec=pltpu.Pref...  136 us
    ppermute x57, waiting for transfers between devices, swap(): return lax.ppermute(value, AXES, pairs)  111 us
    ppermute x57, starting transfers between devices, swap(): return lax.ppermute(value, AXES, pairs)  55.2 us
    pallas_call x1, Pallas kernels, attend_backward(): pl.pallas_call(attend_backward_body, out_shape=[jax.ShapeDtypeStruct((tok...  17 us
    pallas_call x1, Pallas kernels, attend_forward(): pl.pallas_call(attend_forward_body, out_shape=[jax.ShapeDtypeStruct((toke...  12.8 us
    pallas_call x3, Pallas kernels, in_z_order(): pl.pallas_call(body, out_shape=struct((net.inner * rows, columns), BF), g...  9.54 us
    unnamed x66, local copies, waits for them, and re-layouts  7.6 us
  transfers between devices with their start and end apart: 58, of which 25 were waited for; matrix products, arithmetic and copies ran while one was open for 4% of the time, Pallas kernels for 40%

profile of v4, /device:TPU:0, one launch (start us, length us, event | category | flops | bytes accessed | tf_op | source)
XLA Modules:
  0.0 370.7 jit_solution(3376663436491914846)
XLA Ops:
  2.6 4.0 %collective-permute-start.1 = (bf16[32,4224]{1,0:T(8,128)(2,1)}, bf16[32,4224]{1,0:T(8,128)(2,1)S(1)}, u32[]{:S(2)}, u32[]{:S(2)}) collective-permute-start(bf16[32,4224]{1,0:T(8,128)(2,1)} %first_shard.1.refs_0_), channel_id=1, source_target_pairs={{0,2},{1,3},{2,0},{3,1},{4,6},{5,7},{6,4},{7,5},{8,10},{9,11},{10,... | collective-permute-start | bytes 811016 | tf_op jit(solution)/shard_map/ppermute | solution.py:195
  8.2 11.0 %collective-permute-done.1.refs_2_ = bf16[32,4224]{1,0:T(8,128)(2,1)S(1)} collective-permute-done((bf16[32,4224]{1,0:T(8,128)(2,1)}, bf16[32,4224]{1,0:T(8,128)(2,1)S(1)}, u32[]{:S(2)}, u32[]{:S(2)}) %collective-permute-start.1) | collective-permute-done | bytes 270368 | tf_op jit(solution)/shard_map/ppermute | solution.py:195
  20.5 6.3 %collective-permute-done.2.refs_3_ = bf16[32,4224]{1,0:T(8,128)(2,1)S(1)} collective-permute-done((bf16[32,4224]{1,0:T(8,128)(2,1)S(1)}, bf16[32,4224]{1,0:T(8,128)(2,1)S(1)}, u32[]{:S(2)}, u32[]{:S(2)}) %collective-permute-start.2) | collective-permute-done | bytes 270368 | tf_op jit(solution)/shard_map/ppermute | solution.py:195
  27.5 3.9 %in_z_order.3.refs_0_ = bf16[128,4224]{1,0:T(8,128)(2,1)} custom-call(s32[3]{0:T(128)} %pad_add_fusion.ids_ref, bf16[32,4224]{1,0:T(8,128)(2,1)} %first_shard.1.refs_0_, bf16[32,4224]{1,0:T(8,128)(2,1)} %copy-done.23, bf16[32,4224]{1,0:T(8,128)(2,1)} %copy-done.22, bf16[32,4224]{1,0:T(8,128)(2,1)} %copy-done.24), custom_call_target="tpu_custom_call" | custom-call | flops 1 | bytes 899999 | tf_op jit(solution)/shard_map/in_z_order/pallas_call | solution.py:249
  39.2 9.4 %collective-permute-done.6.refs_2_ = bf16[32,4096]{1,0:T(8,128)(2,1)S(1)} collective-permute-done((bf16[32,4096]{1,0:T(8,128)(2,1)S(1)}, bf16[32,4096]{1,0:T(8,128)(2,1)S(1)}, u32[]{:S(2)}, u32[]{:S(2)}) %collective-permute-start.6) | collective-permute-done | bytes 262176 | tf_op jit(solution)/shard_map/ppermute | solution.py:195
  49.2 6.5 %collective-permute-done.4.refs_2_ = bf16[128,4224]{1,0:T(8,128)(2,1)S(1)} collective-permute-done((bf16[128,4224]{1,0:T(8,128)(2,1)}, bf16[128,4224]{1,0:T(8,128)(2,1)S(1)}, u32[]{:S(2)}, u32[]{:S(2)}) %collective-permute-start.4) | collective-permute-done | bytes 1081376 | tf_op jit(solution)/shard_map/ppermute | solution.py:195
  60.4 11.6 %collective-permute-done.9.refs_4_ = bf16[64,4224]{1,0:T(8,128)(2,1)} collective-permute-done((bf16[64,4224]{1,0:T(8,128)(2,1)S(1)}, bf16[64,4224]{1,0:T(8,128)(2,1)}, u32[]{:S(2)}, u32[]{:S(2)}) %collective-permute-start.9) | collective-permute-done | bytes 540704 | tf_op jit(solution)/shard_map/ppermute | solution.py:195
  78.5 9.6 %project.1 = (bf16[512,1024]{1,0:T(8,128)(2,1)}, bf16[512,1024]{1,0:T(8,128)(2,1)}, bf16[512,1024]{1,0:T(8,128)(2,1)}, f32[16,1024]{1,0:T(8,128)}) custom-call(s32[3]{0:T(128)} %pad_add_fusion.ids_ref, bf16[512,1024]{1,0:T(8,128)(2,1)} %bitcast.26, bf16[128,4224]{1,0:T(8,128)(2,1)} %in_z_order.3.refs_0_, bf16[128,4224]{1,0:T(8,128)(2,1)} %copy-done.1, ...), custom_call_target="tpu_custom_call" | custom-call | flops 1 | bytes 3000000 | tf_op jit(solution)/shard_map/project/pallas_call | solution.py:373
  88.2 4.4 %collective-permute-start.25 = (bf16[128,1024]{1,0:T(8,128)(2,1)S(1)}, bf16[128,1024]{1,0:T(8,128)(2,1)}, u32[]{:S(2)}, u32[]{:S(2)}) collective-permute-start(bf16[128,1024]{1,0:T(8,128)(2,1)S(1)} %copy-done.26), channel_id=1, source_target_pairs={{0,2},{1,3},{2,0},{3,1},{4,6},{5,7},{6,4},{7,5},{8,10},{9,11},{10,... | collective-permute-start | bytes 786440 | tf_op jit(solution)/shard_map/ppermute | solution.py:195
  92.6 12.8 %attend_forward.1 = (bf16[512,1024]{1,0:T(8,128)(2,1)}, f32[1,8,8,512]{3,2,1,0:T(8,128)}) custom-call(s32[1,1,512]{2,1,0:T(1,128)} %bitcast.37, bf16[512,1024]{1,0:T(8,128)(2,1)} %get-tuple-element.109.q_ref, bf16[512,1024]{1,0:T(8,128)(2,1)} %get-tuple-element.110.k_ref, bf16[512,1024]{1,0:T(8,128)(2,1)} %get-tuple-element.111.v_ref), custom_call_target="tpu_custom_call" | custom-call | flops 1 | bytes 3900000 | tf_op jit(solution)/shard_map/attend_forward/pallas_call | solution.py:154
  109.6 6.8 %close_attention.1 = (f32[512,1024]{1,0:T(8,128)}, f32[512,128]{1,0:T(8,128)}, bf16[512,1024]{1,0:T(8,128)(2,1)}) custom-call(s32[3]{0:T(128)} %pad_add_fusion.ids_ref, bf16[512,1024]{1,0:T(8,128)(2,1)} %get-tuple-element.112.m_ref.refs_0_, bf16[512,1024]{1,0:T(8,128)(2,1)} %bitcast.27, f32[16,1024]{1,0:T(8,128)} %get-tuple-element.108.vec_ref, ...), custom_call_target="tpu_custom_call" | custom-call | flops 1 | bytes 2100000 | tf_op jit(solution)/shard_map/close_attention/pallas_call | solution.py:373
  116.9 4.3 %collective-permute-done.26.refs_3_ = bf16[128,1024]{1,0:T(8,128)(2,1)} collective-permute-done((bf16[128,1024]{1,0:T(8,128)(2,1)}, bf16[128,1024]{1,0:T(8,128)(2,1)}, u32[]{:S(2)}, u32[]{:S(2)}) %collective-permute-start.26) | collective-permute-done | bytes 262176 | tf_op jit(solution)/shard_map/ppermute | solution.py:195
  130.9 14.0 %ffn_in.1 = (bf16[512,4096]{1,0:T(8,128)(2,1)}, f32[512,4096]{1,0:T(8,128)}) custom-call(s32[3]{0:T(128)} %pad_add_fusion.ids_ref, bf16[512,1024]{1,0:T(8,128)(2,1)} %get-tuple-element.113.x_ref.refs_0_.refs_1_.refs_2_.refs_3_, f32[1,4096]{1,0:T(1,128)} %reshape.121.bias_ref, bf16[128,4096]{1,0:T(8,128)(2,1)} %in_z_order.4.refs_0_.refs_10_, ...), custom_call_target="tpu_custom_call" | custom-call | flops 1 | bytes 3900000 | tf_op jit(solution)/shard_map/ffn_in/pallas_call | solution.py:373
  144.9 5.4 %collective-permute-done.28.refs_2_.refs_6_ = bf16[512,1024]{1,0:T(8,128)(2,1)S(1)} collective-permute-done((bf16[512,1024]{1,0:T(8,128)(2,1)}, bf16[512,1024]{1,0:T(8,128)(2,1)S(1)}, u32[]{:S(2)}, u32[]{:S(2)}) %collective-permute-start.28) | collective-permute-done | bytes 1048608 | tf_op jit(solution)/shard_map/ppermute | solution.py:195
  154.5 10.5 %collective-permute-done.30.refs_4_.refs_8_ = bf16[256,1024]{1,0:T(8,128)(2,1)S(1)} collective-permute-done((bf16[256,1024]{1,0:T(8,128)(2,1)S(1)}, bf16[256,1024]{1,0:T(8,128)(2,1)S(1)}, u32[]{:S(2)}, u32[]{:S(2)}) %collective-permute-start.30) | collective-permute-done | bytes 524320 | tf_op jit(solution)/shard_map/ppermute | solution.py:195
  169.7 15.6 %ffn_out.1 = (bf16[512,1024]{1,0:T(8,128)(2,1)}, f32[512,1024]{1,0:T(8,128)}, bf16[512,1024]{1,0:T(8,128)(2,1)}, f32[8,1024]{1,0:T(8,128)}, bf16[2048,1024]{1,0:T(8,128)(2,1)}) custom-call(s32[3]{0:T(128)} %pad_add_fusion.ids_ref, f32[16,1024]{1,0:T(8,128)} %get-tuple-element.108.vec_ref, bf16[512,4096]{1,0:T(8,128)(2,1)} %get-tuple-element.121.act_hbm.refs_0_, ...), custom_call_target="tpu_custom_call" | custom-call | flops 1 | bytes 5399999 | tf_op jit(solution)/shard_map/ffn_out/pallas_call | solution.py:373
  185.5 14.0 %ffn_back.1 = (bf16[512,4096]{1,0:T(8,128)(2,1)}, f32[8,4096]{1,0:T(8,128)}, bf16[512,4096]{1,0:T(8,128)(2,1)}) custom-call(s32[3]{0:T(128)} %pad_add_fusion.ids_ref, bf16[512,1024]{1,0:T(8,128)(2,1)} %get-tuple-element.134.grad_ref.refs_1_, f32[512,4096]{1,0:T(8,128)} %get-tuple-element.135.slope_ref, ...), custom_call_target="tpu_custom_call" | custom-call | flops 1 | bytes 3599999 | tf_op jit(solution)/shard_map/ffn_back/pallas_call | solution.py:373
  200.0 7.8 %rows_of_own_core.3 = (bf16[1024,512]{1,0:T(8,128)(2,1)}, bf16[1024,512]{1,0:T(8,128)(2,1)}, bf16[1024,512]{1,0:T(8,128)(2,1)}, bf16[1024,512]{1,0:T(8,128)(2,1)}) custom-call(s32[3]{0:T(128)} %pad_add_fusion.ids_ref, bf16[512,4096]{1,0:T(8,128)(2,1)} %get-tuple-element.121.act_hbm.refs_0_, bf16[512,1024]{1,0:T(8,128)(2,1)} %get-tuple-element.134.grad_ref.refs_1_, ...), custom_call_target="tpu_custom_call" | custom-call | flops 1 | bytes 2699999 | tf_op jit(solution)/shard_map/rows_of_own_core/pallas_call | solution.py:373
  210.9 15.9 %attention_norm_back.1 = (bf16[512,1024]{1,0:T(8,128)(2,1)}, f32[512,1024]{1,0:T(8,128)}, bf16[512,1024]{1,0:T(8,128)(2,1)}, f32[8,1024]{1,0:T(8,128)}) custom-call(s32[3]{0:T(128)} %pad_add_fusion.ids_ref, f32[512,128]{1,0:T(8,128)} %get-tuple-element.133.inverse_ref, f32[16,1024]{1,0:T(8,128)} %get-tuple-element.108.vec_ref, ...), custom_call_target="tpu_custom_call" | custom-call | flops 1 | bytes 4800000 | tf_op jit(solution)/shard_map/attention_norm_back/pallas_call | solution.py:373
  226.8 7.8 %rows_of_own_core.4 = (bf16[256,2048]{1,0:T(8,128)(2,1)}, bf16[256,2048]{1,0:T(8,128)(2,1)}, bf16[256,2048]{1,0:T(8,128)(2,1)}, bf16[256,2048]{1,0:T(8,128)(2,1)}) custom-call(s32[3]{0:T(128)} %pad_add_fusion.ids_ref, bf16[512,1024]{1,0:T(8,128)(2,1)} %get-tuple-element.113.x_ref.refs_0_.refs_1_.refs_2_.refs_3_, ...), custom_call_target="tpu_custom_call" | custom-call | flops 1 | bytes 2699999 | tf_op jit(solution)/shard_map/rows_of_own_core/pallas_call | solution.py:373
  237.1 17.0 %attend_backward.1 = (bf16[512,1024]{1,0:T(8,128)(2,1)}, bf16[512,1024]{1,0:T(8,128)(2,1)}, bf16[512,1024]{1,0:T(8,128)(2,1)}, f32[1,8,1024]{2,1,0:T(8,128)}, f32[1,8,1024]{2,1,0:T(8,128)}) custom-call(s32[1,1,512]{2,1,0:T(1,128)} %bitcast.38, bf16[512,1024]{1,0:T(8,128)(2,1)} %get-tuple-element.109.q_ref, bf16[512,1024]{1,0:T(8,128)(2,1)} %get-tuple-element.110.k_ref, ...), custom_call_target="tpu_custom_call" | custom-call | flops 1 | bytes 5100000 | tf_op jit(solution)/shard_map/attend_backward/pallas_call | solution.py:174
  254.1 4.5 %cross_near.1 = (bf16[512,1024]{1,0:T(8,128)(2,1)}, bf16[512,1024]{1,0:T(8,128)(2,1)}) custom-call(s32[3]{0:T(128)} %pad_add_fusion.ids_ref, bf16[1024,512]{1,0:T(8,128)(2,1)} %get-tuple-element.140.refs_20_.refs_0_, bf16[1024,512]{1,0:T(8,128)(2,1)} %copy-done.9, bf16[1024,512]{1,0:T(8,128)(2,1)} %get-tuple-element.151.refs_2_, ...), custom_call_target="tpu_custom_call" | custom-call | flops 1 | bytes 1799999 | tf_op jit(solution)/shard_map/cross_near/pallas_call | solution.py:373
  260.6 7.2 %rows_of_other_core.1.refs_4_ = bf16[512,4096]{1,0:T(8,128)(2,1)} custom-call(s32[3]{0:T(128)} %pad_add_fusion.ids_ref, bf16[512,1024]{1,0:T(8,128)(2,1)} %get-tuple-element.112.m_ref.refs_0_, bf16[512,1024]{1,0:T(8,128)(2,1)} %bitcast.28, bf16[512,1024]{1,0:T(8,128)(2,1)} %get-tuple-element.144.refs_3_.refs_2_, ...), custom_call_target="tpu_custom_call" | custom-call | flops 1 | bytes 2100000 | tf_op jit(solution)/shard_map/rows_of_other_core/pallas_call | solution.py:373
  269.4 4.0 %fold.2 = (bf16[128,2048]{1,0:T(8,128)(2,1)}, bf16[128,2048]{1,0:T(8,128)(2,1)}, bf16[128,2048]{1,0:T(8,128)(2,1)}, bf16[128,2048]{1,0:T(8,128)(2,1)}) custom-call(s32[3]{0:T(128)} %pad_add_fusion.ids_ref, bf16[256,2048]{1,0:T(8,128)(2,1)} %get-tuple-element.145.rest_0_.refs_0_, bf16[256,2048]{1,0:T(8,128)(2,1)} %copy-done.11, ...), custom_call_target="tpu_custom_call" | custom-call | flops 1 | bytes 1200000 | tf_op jit(solution)/shard_map/fold/pallas_call | solution.py:373
  275.4 8.2 %rows_of_own_core.5 = (bf16[256,2048]{1,0:T(8,128)(2,1)}, bf16[256,2048]{1,0:T(8,128)(2,1)}, bf16[256,2048]{1,0:T(8,128)(2,1)}, bf16[256,2048]{1,0:T(8,128)(2,1)}) custom-call(s32[3]{0:T(128)} %pad_add_fusion.ids_ref, bf16[512,1024]{1,0:T(8,128)(2,1)} %get-tuple-element.112.m_ref.refs_0_, bf16[512,1024]{1,0:T(8,128)(2,1)} %bitcast.29, ...), custom_call_target="tpu_custom_call" | custom-call | flops 1 | bytes 2699999 | tf_op jit(solution)/shard_map/rows_of_own_core/pallas_call | solution.py:373
  295.7 14.9 %collective-permute-done.43.refs_1_ = bf16[256,2048]{1,0:T(8,128)(2,1)S(1)} collective-permute-done((bf16[256,2048]{1,0:T(8,128)(2,1)}, bf16[256,2048]{1,0:T(8,128)(2,1)S(1)}, u32[]{:S(2)}, u32[]{:S(2)}) %collective-permute-start.43) | collective-permute-done | bytes 1048608 | tf_op jit(solution)/shard_map/ppermute | solution.py:195
  311.6 4.1 %fold.3 = (bf16[128,2048]{1,0:T(8,128)(2,1)}, bf16[128,2048]{1,0:T(8,128)(2,1)}, bf16[128,2048]{1,0:T(8,128)(2,1)}, bf16[128,2048]{1,0:T(8,128)(2,1)}) custom-call(s32[3]{0:T(128)} %pad_add_fusion.ids_ref, bf16[256,2048]{1,0:T(8,128)(2,1)} %get-tuple-element.157.refs_4_.refs_0_, bf16[256,2048]{1,0:T(8,128)(2,1)} %copy-done.18, ...), custom_call_target="tpu_custom_call" | custom-call | flops 1 | bytes 1200000 | tf_op jit(solution)/shard_map/fold/pallas_call | solution.py:373
  320.2 10.1 %inputs_back.1.refs_4_ = f32[512,1024]{1,0:T(8,128)} custom-call(s32[3]{0:T(128)} %pad_add_fusion.ids_ref, f32[512,1024]{1,0:T(8,128)} %get-tuple-element.141.base_ref, bf16[512,1024]{1,0:T(8,128)(2,1)} %get-tuple-element.148.refs_4_.refs_3_.q_ref, bf16[512,1024]{1,0:T(8,128)(2,1)} %get-tuple-element.149.refs_4_.k_ref, ...), custom_call_target="tpu_custom_call" | custom-call | flops 1 | bytes 3000000 | tf_op jit(solution)/shard_map/inputs_back/pallas_call | solution.py:373
  331.2 3.3 fold_z.3
  335.2 3.7 %all-to-all-start = ((f32[32,1,384]{2,1,0:T(1,128)}), f32[32,1,384]{2,1,0:T(1,128)S(1)}, u32[]{:S(2)}, u32[]{:S(2)}) async-start(f32[32,1,384]{2,1,0:T(1,128)} %copy.46), calls=%async_computation | async-start | bytes 98304 | tf_op jit(solution)/shard_map/all_to_all | solution.py:1290
  346.4 9.4 %collective-permute-done.49 = bf16[64,4096]{1,0:T(8,128)(2,1)S(1)} collective-permute-done((bf16[64,4096]{1,0:T(8,128)(2,1)S(1)}, bf16[64,4096]{1,0:T(8,128)(2,1)S(1)}, u32[]{:S(2)}, u32[]{:S(2)}) %collective-permute-start.49) | collective-permute-done | bytes 524320 | tf_op jit(solution)/shard_map/ppermute | solution.py:195
  360.4 9.4 %collective-permute-done.50 = bf16[32,4096]{1,0:T(8,128)(2,1)S(1)} collective-permute-done((bf16[32,4096]{1,0:T(8,128)(2,1)S(1)}, bf16[32,4096]{1,0:T(8,128)(2,1)S(1)}, u32[]{:S(2)}, u32[]{:S(2)}) %collective-permute-start.50) | collective-permute-done | bytes 262176 | tf_op jit(solution)/shard_map/ppermute | solution.py:195
  (216 shorter events, 91.9 us)
Async XLA Ops:
  2.6 16.6 %collective-permute-start.1 = (bf16[32,4224]{1,0:T(8,128)(2,1)}, bf16[32,4224]{1,0:T(8,128)(2,1)S(1)}, u32[]{:S(2)}, u32[]{:S(2)}) collective-permute-start(bf16[32,4224]{1,0:T(8,128)(2,1)} %first_shard.1.refs_0_), channel_id=1, source_target_pairs={{0,2},{1,3},{2,0},{3,1},{4,6},{5,7},{6,4},{7,5},{8,10},{9,11},{10,... | collective-permute-start | bytes 811016 | tf_op jit(solution)/shard_map/ppermute | solution.py:195
  31.4 24.3 %collective-permute-start.4 = (bf16[128,4224]{1,0:T(8,128)(2,1)}, bf16[128,4224]{1,0:T(8,128)(2,1)S(1)}, u32[]{:S(2)}, u32[]{:S(2)}) collective-permute-start(bf16[128,4224]{1,0:T(8,128)(2,1)} %in_z_order.3.refs_0_), channel_id=1, source_target_pairs={{0,16},{1,17},{2,18},{3,19},{4,20},{5,21},{6,22},{7,23},{8,24},{9,... | collective-permute-start | bytes 3244040 | tf_op jit(solution)/shard_map/ppermute | solution.py:195
  32.7 24.4 %collective-permute-start.3 = (bf16[128,4224]{1,0:T(8,128)(2,1)}, bf16[128,4224]{1,0:T(8,128)(2,1)S(1)}, u32[]{:S(2)}, u32[]{:S(2)}) collective-permute-start(bf16[128,4224]{1,0:T(8,128)(2,1)} %in_z_order.3.refs_0_), channel_id=1, source_target_pairs={{0,8},{1,9},{2,10},{3,11},{4,12},{5,13},{6,14},{7,15},{8,0},{9,1},... | collective-permute-start | bytes 3244040 | tf_op jit(solution)/shard_map/ppermute | solution.py:195
  37.5 18.2 %collective-permute-start.5 = (bf16[32,4096]{1,0:T(8,128)(2,1)S(1)}, bf16[32,4096]{1,0:T(8,128)(2,1)S(1)}, u32[]{:S(2)}, u32[]{:S(2)}) collective-permute-start(bf16[32,4096]{1,0:T(8,128)(2,1)S(1)} %copy-done.25), channel_id=1, source_target_pairs={{0,1},{1,0},{2,3},{3,2},{4,5},{5,4},{6,7},{7,6},{8,9},{9,8},{10,11... | collective-permute-start | bytes 786440 | tf_op jit(solution)/shard_map/ppermute | solution.py:195
  49.2 27.2 %collective-permute-start.10 = (bf16[128,4224]{1,0:T(8,128)(2,1)}, bf16[128,4224]{1,0:T(8,128)(2,1)S(1)}, u32[]{:S(2)}, u32[]{:S(2)}) collective-permute-start(bf16[128,4224]{1,0:T(8,128)(2,1)} %in_z_order.3.refs_0_), channel_id=1, source_target_pairs={{0,4},{1,5},{2,6},{3,7},{4,0},{5,1},{6,2},{7,3},{8,12},{9,13},{10,... | collective-permute-start | bytes 3244040 | tf_op jit(solution)/shard_map/ppermute | solution.py:195
  55.7 20.7 %collective-permute-start.12 = (bf16[128,4224]{1,0:T(8,128)(2,1)S(1)}, bf16[128,4224]{1,0:T(8,128)(2,1)}, u32[]{:S(2)}, u32[]{:S(2)}) collective-permute-start(bf16[128,4224]{1,0:T(8,128)(2,1)S(1)} %collective-permute-done.4.refs_2_), channel_id=1, source_target_pairs={{0,4},{1,5},{2,6},{3,7},{4,0},{5,1},{6,2},{7,3},{8,12},{9,13},{10,... | collective-permute-start | bytes 3244040 | tf_op jit(solution)/shard_map/ppermute | solution.py:195
  57.2 14.8 %collective-permute-start.9 = (bf16[64,4224]{1,0:T(8,128)(2,1)S(1)}, bf16[64,4224]{1,0:T(8,128)(2,1)}, u32[]{:S(2)}, u32[]{:S(2)}) collective-permute-start(bf16[64,4224]{1,0:T(8,128)(2,1)S(1)} %slice.116), channel_id=1, source_target_pairs={{0,8},{1,9},{2,10},{3,11},{4,12},{5,13},{6,14},{7,15},{8,0},{9,1},... | collective-permute-start | bytes 1622024 | tf_op jit(solution)/shard_map/ppermute | solution.py:195
  58.7 17.7 %collective-permute-start.11 = (bf16[128,4224]{1,0:T(8,128)(2,1)S(1)}, bf16[128,4224]{1,0:T(8,128)(2,1)}, u32[]{:S(2)}, u32[]{:S(2)}) collective-permute-start(bf16[128,4224]{1,0:T(8,128)(2,1)S(1)} %collective-permute-done.3.refs_1_), channel_id=1, source_target_pairs={{0,4},{1,5},{2,6},{3,7},{4,0},{5,1},{6,2},{7,3},{8,12},{9,13},{10,... | collective-permute-start | bytes 3244040 | tf_op jit(solution)/shard_map/ppermute | solution.py:195
  76.4 28.9 %collective-permute-start.16 = (bf16[128,4096]{1,0:T(8,128)(2,1)}, bf16[128,4096]{1,0:T(8,128)(2,1)S(1)}, u32[]{:S(2)}, u32[]{:S(2)}) collective-permute-start(bf16[128,4096]{1,0:T(8,128)(2,1)} %in_z_order.4.refs_0_.refs_10_), channel_id=1, source_target_pairs={{0,16},{1,17},{2,18},{3,19},{4,20},{5,21},{6,22},{7,23},{8,24},{9,... | collective-permute-start | bytes 3145736 | tf_op jit(solution)/shard_map/ppermute | solution.py:195
  78.0 27.3 %collective-permute-start.15 = (bf16[128,4096]{1,0:T(8,128)(2,1)}, bf16[128,4096]{1,0:T(8,128)(2,1)S(1)}, u32[]{:S(2)}, u32[]{:S(2)}) collective-permute-start(bf16[128,4096]{1,0:T(8,128)(2,1)} %in_z_order.4.refs_0_.refs_10_), channel_id=1, source_target_pairs={{0,8},{1,9},{2,10},{3,11},{4,12},{5,13},{6,14},{7,15},{8,0},{9,1},... | collective-permute-start | bytes 3145736 | tf_op jit(solution)/shard_map/ppermute | solution.py:195
  78.5 47.6 %collective-permute-start.19 = (bf16[128,4096]{1,0:T(8,128)(2,1)}, bf16[128,4096]{1,0:T(8,128)(2,1)}, u32[]{:S(2)}, u32[]{:S(2)}) collective-permute-start(bf16[128,4096]{1,0:T(8,128)(2,1)} %in_z_order.4.refs_0_.refs_10_), channel_id=1, source_target_pairs={{0,4},{1,5},{2,6},{3,7},{4,0},{5,1},{6,2},{7,3},{8,12},{9,13},{10,... | collective-permute-start | bytes 3145736 | tf_op jit(solution)/shard_map/ppermute | solution.py:195
  88.2 20.8 %collective-permute-start.25 = (bf16[128,1024]{1,0:T(8,128)(2,1)S(1)}, bf16[128,1024]{1,0:T(8,128)(2,1)}, u32[]{:S(2)}, u32[]{:S(2)}) collective-permute-start(bf16[128,1024]{1,0:T(8,128)(2,1)S(1)} %copy-done.26), channel_id=1, source_target_pairs={{0,2},{1,3},{2,0},{3,1},{4,6},{5,7},{6,4},{7,5},{8,10},{9,11},{10,... | collective-permute-start | bytes 786440 | tf_op jit(solution)/shard_map/ppermute | solution.py:195
  105.4 19.1 %collective-permute-start.18 = (bf16[64,4096]{1,0:T(8,128)(2,1)S(1)}, bf16[64,4096]{1,0:T(8,128)(2,1)}, u32[]{:S(2)}, u32[]{:S(2)}) collective-permute-start(bf16[64,4096]{1,0:T(8,128)(2,1)S(1)} %slice.119), channel_id=1, source_target_pairs={{0,8},{1,9},{2,10},{3,11},{4,12},{5,13},{6,14},{7,15},{8,0},{9,1},... | collective-permute-start | bytes 1572872 | tf_op jit(solution)/shard_map/ppermute | solution.py:195
  107.0 17.6 %collective-permute-start.17 = (bf16[64,4096]{1,0:T(8,128)(2,1)S(1)}, bf16[64,4096]{1,0:T(8,128)(2,1)}, u32[]{:S(2)}, u32[]{:S(2)}) collective-permute-start(bf16[64,4096]{1,0:T(8,128)(2,1)S(1)} %slice.118), channel_id=1, source_target_pairs={{0,16},{1,17},{2,18},{3,19},{4,20},{5,21},{6,22},{7,23},{8,24},{9,... | collective-permute-start | bytes 1572872 | tf_op jit(solution)/shard_map/ppermute | solution.py:195
  124.6 25.7 %collective-permute-start.28 = (bf16[512,1024]{1,0:T(8,128)(2,1)}, bf16[512,1024]{1,0:T(8,128)(2,1)S(1)}, u32[]{:S(2)}, u32[]{:S(2)}) collective-permute-start(bf16[512,1024]{1,0:T(8,128)(2,1)} %in_z_order.5.refs_0_.refs_4_), channel_id=1, source_target_pairs={{0,16},{1,17},{2,18},{3,19},{4,20},{5,21},{6,22},{7,23},{8,24},{9,... | collective-permute-start | bytes 3145736 | tf_op jit(solution)/shard_map/ppermute | solution.py:195
  126.1 25.5 %collective-permute-start.27 = (bf16[512,1024]{1,0:T(8,128)(2,1)}, bf16[512,1024]{1,0:T(8,128)(2,1)}, u32[]{:S(2)}, u32[]{:S(2)}) collective-permute-start(bf16[512,1024]{1,0:T(8,128)(2,1)} %in_z_order.5.refs_0_.refs_4_), channel_id=1, source_target_pairs={{0,8},{1,9},{2,10},{3,11},{4,12},{5,13},{6,14},{7,15},{8,0},{9,1},... | collective-permute-start | bytes 3145736 | tf_op jit(solution)/shard_map/ppermute | solution.py:195
  130.7 35.6 %collective-permute-start.31 = (bf16[512,1024]{1,0:T(8,128)(2,1)}, bf16[512,1024]{1,0:T(8,128)(2,1)}, u32[]{:S(2)}, u32[]{:S(2)}) collective-permute-start(bf16[512,1024]{1,0:T(8,128)(2,1)} %in_z_order.5.refs_0_.refs_4_), channel_id=1, source_target_pairs={{0,4},{1,5},{2,6},{3,7},{4,0},{5,1},{6,2},{7,3},{8,12},{9,13},{10,... | collective-permute-start | bytes 3145736 | tf_op jit(solution)/shard_map/ppermute | solution.py:195
  199.5 27.2 %collective-permute-start.37 = (bf16[512,4096]{1,0:T(8,128)(2,1)}, bf16[512,4096]{1,0:T(8,128)(2,1)}, u32[]{:S(2)}, u32[]{:S(2)}) collective-permute-start(bf16[512,4096]{1,0:T(8,128)(2,1)} %get-tuple-element.139.refs_3_), channel_id=1, source_target_pairs={{0,4},{1,5},{2,6},{3,7},{4,0},{5,1},{6,2},{7,3},{8,12},{9,13},{10,... | collective-permute-start | bytes 12582920 | tf_op jit(solution)/shard_map/ppermute | solution.py:195
  207.8 27.9 %collective-permute-start.38 = (bf16[1024,512]{1,0:T(8,128)(2,1)}, bf16[1024,512]{1,0:T(8,128)(2,1)S(1)}, u32[]{:S(2)}, u32[]{:S(2)}) collective-permute-start(bf16[1024,512]{1,0:T(8,128)(2,1)} %get-tuple-element.146), channel_id=1, source_target_pairs={{0,8},{1,9},{2,10},{3,11},{4,12},{5,13},{6,14},{7,15},{8,0},{9,1},... | collective-permute-start | bytes 3145736 | tf_op jit(solution)/shard_map/ppermute | solution.py:195
  209.7 26.1 %collective-permute-start.39 = (bf16[1024,512]{1,0:T(8,128)(2,1)}, bf16[1024,512]{1,0:T(8,128)(2,1)S(1)}, u32[]{:S(2)}, u32[]{:S(2)}) collective-permute-start(bf16[1024,512]{1,0:T(8,128)(2,1)} %get-tuple-element.147), channel_id=1, source_target_pairs={{0,16},{1,17},{2,18},{3,19},{4,20},{5,21},{6,22},{7,23},{8,24},{9,... | collective-permute-start | bytes 3145736 | tf_op jit(solution)/shard_map/ppermute | solution.py:195
  234.6 24.9 %collective-permute-start.40 = (bf16[256,2048]{1,0:T(8,128)(2,1)}, bf16[256,2048]{1,0:T(8,128)(2,1)S(1)}, u32[]{:S(2)}, u32[]{:S(2)}) collective-permute-start(bf16[256,2048]{1,0:T(8,128)(2,1)} %get-tuple-element.153), channel_id=1, source_target_pairs={{0,8},{1,9},{2,10},{3,11},{4,12},{5,13},{6,14},{7,15},{8,0},{9,1},... | collective-permute-start | bytes 3145736 | tf_op jit(solution)/shard_map/ppermute | solution.py:195
  235.0 24.8 %collective-permute-start.41 = (bf16[256,2048]{1,0:T(8,128)(2,1)}, bf16[256,2048]{1,0:T(8,128)(2,1)}, u32[]{:S(2)}, u32[]{:S(2)}) collective-permute-start(bf16[256,2048]{1,0:T(8,128)(2,1)} %get-tuple-element.154), channel_id=1, source_target_pairs={{0,16},{1,17},{2,18},{3,19},{4,20},{5,21},{6,22},{7,23},{8,24},{9,... | collective-permute-start | bytes 3145736 | tf_op jit(solution)/shard_map/ppermute | solution.py:195
  267.9 25.8 %collective-permute-start.53 = (bf16[512,1024]{1,0:T(8,128)(2,1)}, bf16[512,1024]{1,0:T(8,128)(2,1)S(1)}, u32[]{:S(2)}, u32[]{:S(2)}) collective-permute-start(bf16[512,1024]{1,0:T(8,128)(2,1)} %get-tuple-element.182), channel_id=1, source_target_pairs={{0,1},{1,0},{2,3},{3,2},{4,5},{5,4},{6,7},{7,6},{8,9},{9,8},{10,11... | collective-permute-start | bytes 3145736 | tf_op jit(solution)/shard_map/ppermute | solution.py:195
  273.4 14.8 %collective-permute-start.45 = (bf16[128,2048]{1,0:T(8,128)(2,1)}, bf16[128,2048]{1,0:T(8,128)(2,1)}, u32[]{:S(2)}, u32[]{:S(2)}) collective-permute-start(bf16[128,2048]{1,0:T(8,128)(2,1)} %get-tuple-element.161), channel_id=1, source_target_pairs={{0,16},{1,17},{2,18},{3,19},{4,20},{5,21},{6,22},{7,23},{8,24},{9,... | collective-permute-start | bytes 1572872 | tf_op jit(solution)/shard_map/ppermute | solution.py:195
  274.2 15.1 %collective-permute-start.46 = (bf16[128,2048]{1,0:T(8,128)(2,1)}, bf16[128,2048]{1,0:T(8,128)(2,1)}, u32[]{:S(2)}, u32[]{:S(2)}) collective-permute-start(bf16[128,2048]{1,0:T(8,128)(2,1)} %get-tuple-element.163), channel_id=1, source_target_pairs={{0,8},{1,9},{2,10},{3,11},{4,12},{5,13},{6,14},{7,15},{8,0},{9,1},... | collective-permute-start | bytes 1572872 | tf_op jit(solution)/shard_map/ppermute | solution.py:195
  283.7 27.0 %collective-permute-start.43 = (bf16[256,2048]{1,0:T(8,128)(2,1)}, bf16[256,2048]{1,0:T(8,128)(2,1)S(1)}, u32[]{:S(2)}, u32[]{:S(2)}) collective-permute-start(bf16[256,2048]{1,0:T(8,128)(2,1)} %get-tuple-element.158), channel_id=1, source_target_pairs={{0,8},{1,9},{2,10},{3,11},{4,12},{5,13},{6,14},{7,15},{8,0},{9,1},... | collective-permute-start | bytes 3145736 | tf_op jit(solution)/shard_map/ppermute | solution.py:195
  284.6 26.0 %collective-permute-start.44 = (bf16[256,2048]{1,0:T(8,128)(2,1)}, bf16[256,2048]{1,0:T(8,128)(2,1)}, u32[]{:S(2)}, u32[]{:S(2)}) collective-permute-start(bf16[256,2048]{1,0:T(8,128)(2,1)} %get-tuple-element.160), channel_id=1, source_target_pairs={{0,16},{1,17},{2,18},{3,19},{4,20},{5,21},{6,22},{7,23},{8,24},{9,... | collective-permute-start | bytes 3145736 | tf_op jit(solution)/shard_map/ppermute | solution.py:195
  292.7 25.1 %collective-permute-start.51 = (bf16[64,4096]{1,0:T(8,128)(2,1)}, bf16[64,4096]{1,0:T(8,128)(2,1)}, u32[]{:S(2)}, u32[]{:S(2)}) collective-permute-start(bf16[64,4096]{1,0:T(8,128)(2,1)} %get-tuple-element.179), channel_id=1, source_target_pairs={{0,1},{1,0},{2,3},{3,2},{4,5},{5,4},{6,7},{7,6},{8,9},{9,8},{10,11... | collective-permute-start | bytes 1572872 | tf_op jit(solution)/shard_map/ppermute | solution.py:195
  295.0 44.0 %collective-permute-start.54 = (bf16[256,1024]{1,0:T(8,128)(2,1)}, bf16[256,1024]{1,0:T(8,128)(2,1)}, u32[]{:S(2)}, u32[]{:S(2)}) collective-permute-start(bf16[256,1024]{1,0:T(8,128)(2,1)} %get-tuple-element.186), channel_id=1, source_target_pairs={{0,2},{1,3},{2,0},{3,1},{4,6},{5,7},{6,4},{7,5},{8,10},{9,11},{10,... | collective-permute-start | bytes 1572872 | tf_op jit(solution)/shard_map/ppermute | solution.py:195
  319.0 24.6 %collective-permute-start.52 = (bf16[32,4096]{1,0:T(8,128)(2,1)S(1)}, bf16[32,4096]{1,0:T(8,128)(2,1)S(1)}, u32[]{:S(2)}, u32[]{:S(2)}) collective-permute-start(bf16[32,4096]{1,0:T(8,128)(2,1)S(1)} %slice.166), channel_id=1, source_target_pairs={{0,2},{1,3},{2,0},{3,1},{4,6},{5,7},{6,4},{7,5},{8,10},{9,11},{10,... | collective-permute-start | bytes 786440 | tf_op jit(solution)/shard_map/ppermute | solution.py:195
  340.3 19.3 %collective-permute-start.55 = (bf16[128,512]{1,0:T(8,128)(2,1)S(1)}, bf16[128,512]{1,0:T(8,128)(2,1)S(1)}, u32[]{:S(2)}, u32[]{:S(2)}) collective-permute-start(bf16[128,512]{1,0:T(8,128)(2,1)S(1)} %get-tuple-element.187), channel_id=1, source_target_pairs={{0,16},{1,17},{2,18},{3,19},{4,20},{5,21},{6,22},{7,23},{8,24},{9,... | collective-permute-start | bytes 393224 | tf_op jit(solution)/shard_map/ppermute | solution.py:195
  344.4 15.1 %collective-permute-start.56 = (bf16[128,512]{1,0:T(8,128)(2,1)S(1)}, bf16[128,512]{1,0:T(8,128)(2,1)S(1)}, u32[]{:S(2)}, u32[]{:S(2)}) collective-permute-start(bf16[128,512]{1,0:T(8,128)(2,1)S(1)} %get-tuple-element.188), channel_id=1, source_target_pairs={{0,8},{1,9},{2,10},{3,11},{4,12},{5,13},{6,14},{7,15},{8,0},{9,1},... | collective-permute-start | bytes 393224 | tf_op jit(solution)/shard_map/ppermute | solution.py:195
  (60 other events, 519.7 us)

commit v5 on v4

--- a/solution.py
+++ b/solution.py
@@ -1081,6 +1081,48 @@
             )
         self.total, self.came, self.reach = keep, net.swap(away, 1), 1
         return keep
+
+    def fold_direct(self, *deps):
+        net, count = self.net, self.net.inner
+        columns = self.held[0].shape[1]
+        rows = self.width // count
+        self.parts = None
+        if rows % 16 or count > 4:
+            self.fold_z(*deps)
+            return self.fold_far()
+
+        def body(ids_ref, *refs):
+            for s in range(count):
+                at = pl.ds(pl.multiple_of((ids_ref[2] ^ s) * rows, 16), rows)
+                out_ref = refs[s - count]
+                for side in range(2):
+                    value = refs[2 * side][at, :].astype(F32)
+                    value = value + refs[2 * side + 1][at, :].astype(F32)
+                    place = slice(side * columns, (side + 1) * columns)
+                    out_ref[:, place] = value.astype(out_ref.dtype)
+
+        size = (rows, 2 * columns)
+        parts = kernel(
+            body,
+            "fold_direct",
+            3,
+            self.ids,
+            (1,),
+            [(a, whole(a.shape)) for s in range(2) for a in (self.held[s], self.arrived[s])]
+            + [(d, ANY) for d in deps],
+            [(struct(size, F32), whole(size))] + [(struct(size, BF), whole(size))] * (count - 1),
+            [],
+        )
+        self.parts = [parts[0]] + [net.swap(parts[s], s) for s in range(1, count)]
+        return parts[0]
+
+    def finish_direct(self):
+        if self.parts is None:
+            return self.finish()
+        total = self.parts[0]
+        for part in self.parts[1:]:
+            total = total + part.astype(F32)
+        return total
 
     def fold_far(self, *deps):
         while self.reach * 2 < self.net.inner:
@@ -1272,12 +1314,11 @@
     input_grad = inputs_back(
         ids, attn_sum_grad, (query_grad, key_grad, value_grad), weights_a, [last]
     )
-    last = inputs_sum.fold_z(input_grad)
+    last = inputs_sum.fold_direct(input_grad)
     outer.cross_chip(last)
     shard_inner = inner_sum.finish(last)
     shard_outer = outer.finish(last)
-    inputs_sum.fold_far(last)
-    shard_inputs = inputs_sum.finish()
+    shard_inputs = inputs_sum.finish_direct()
     shard_output, shard_query, shard_key, shard_value = (
         shard_inputs[:, i * width : (i + 1) * width] for i in range(4)
     )
@@ -1286,7 +1327,7 @@
     )
     rows = rows.reshape(8, net.count, mine).swapaxes(0, 1).reshape(net.count, 8 * mine)
     packed = jnp.concatenate([rows, inner_sums[0].reshape(net.count, -1)], axis=1)
-    packed = tie(packed, last)
+    packed = tie(packed, inputs_sum.parts[1] if inputs_sum.parts else last)
     summed = jnp.sum(lax.all_to_all(packed, AXES, 0, 0, tiled=True), axis=0)
     vector = [summed[i * mine : (i + 1) * mine] for i in range(8)]
     return (

time: 372 us -> 367 us (0.987)
  waiting for transfers between devices: 111 us -> 107 us
    ppermute x57 -> x58, waiting for transfers between devices: 111 us -> 105 us  [swap(): return lax.ppermute(value, AXES, pairs)]
    ppermute x57 -> x58, starting transfers between devices: 55.2 us -> 55.1 us  [swap(): return lax.ppermute(value, AXES, pairs)]
    unnamed x66 -> x70, local copies, waits for them, and re-layouts: 7.6 us -> 7.62 us
  transfers between devices with their start and end apart: 58 -> 59, of which waited for: 25 -> 25; matrix products, arithmetic and copies ran while one was open for 4% -> 4% of each run, Pallas kernels for 40% -> 41%
where the time goes in v5:
time: 367 us; the launch traced here: 365 us
  Pallas kernels  177 us (48%)
  waiting for transfers between devices  107 us (29%)
  starting transfers between devices  57.8 us (16%)
  local copies, waits for them, and re-layouts  16.2 us (4%)
  other arithmetic  5.41 us (1%)
    pallas_call x16, Pallas kernels, kernel(): pl.pallas_call(body, out_shape=[o for o, _ in outs], grid_spec=pltpu.Pref...  136 us
    ppermute x58, waiting for transfers between devices, swap(): return lax.ppermute(value, AXES, pairs)  105 us
    ppermute x58, starting transfers between devices, swap(): return lax.ppermute(value, AXES, pairs)  55.1 us
    pallas_call x1, Pallas kernels, attend_backward(): pl.pallas_call(attend_backward_body, out_shape=[jax.ShapeDtypeStruct((tok...  17 us
    pallas_call x1, Pallas kernels, attend_forward(): pl.pallas_call(attend_forward_body, out_shape=[jax.ShapeDtypeStruct((toke...  12.8 us
    pallas_call x3, Pallas kernels, in_z_order(): pl.pallas_call(body, out_shape=struct((net.inner * rows, columns), BF), g...  9.5 us
    unnamed x70, local copies, waits for them, and re-layouts  7.62 us
  transfers between devices with their start and end apart: 59, of which 25 were waited for; matrix products, arithmetic and copies ran while one was open for 4% of the time, Pallas kernels for 41%

profile of v5, /device:TPU:0, one launch (start us, length us, event | category | flops | bytes accessed | tf_op | source)
XLA Modules:
  0.0 365.3 jit_solution(16296844613490550116)
XLA Ops:
  2.6 4.0 %collective-permute-start.1 = (bf16[32,4224]{1,0:T(8,128)(2,1)}, bf16[32,4224]{1,0:T(8,128)(2,1)S(1)}, u32[]{:S(2)}, u32[]{:S(2)}) collective-permute-start(bf16[32,4224]{1,0:T(8,128)(2,1)} %first_shard.1.refs_0_), channel_id=1, source_target_pairs={{0,2},{1,3},{2,0},{3,1},{4,6},{5,7},{6,4},{7,5},{8,10},{9,11},{10,... | collective-permute-start | bytes 811016 | tf_op jit(solution)/shard_map/ppermute | solution.py:195
  8.2 11.0 %collective-permute-done.1.refs_2_ = bf16[32,4224]{1,0:T(8,128)(2,1)S(1)} collective-permute-done((bf16[32,4224]{1,0:T(8,128)(2,1)}, bf16[32,4224]{1,0:T(8,128)(2,1)S(1)}, u32[]{:S(2)}, u32[]{:S(2)}) %collective-permute-start.1) | collective-permute-done | bytes 270368 | tf_op jit(solution)/shard_map/ppermute | solution.py:195
  20.5 6.3 %collective-permute-done.2.refs_3_ = bf16[32,4224]{1,0:T(8,128)(2,1)S(1)} collective-permute-done((bf16[32,4224]{1,0:T(8,128)(2,1)S(1)}, bf16[32,4224]{1,0:T(8,128)(2,1)S(1)}, u32[]{:S(2)}, u32[]{:S(2)}) %collective-permute-start.2) | collective-permute-done | bytes 270368 | tf_op jit(solution)/shard_map/ppermute | solution.py:195
  27.5 3.9 %in_z_order.3.refs_0_ = bf16[128,4224]{1,0:T(8,128)(2,1)} custom-call(s32[3]{0:T(128)} %pad_add_fusion.ids_ref, bf16[32,4224]{1,0:T(8,128)(2,1)} %first_shard.1.refs_0_, bf16[32,4224]{1,0:T(8,128)(2,1)} %copy-done.23, bf16[32,4224]{1,0:T(8,128)(2,1)} %copy-done.22, bf16[32,4224]{1,0:T(8,128)(2,1)} %copy-done.24), custom_call_target="tpu_custom_call" | custom-call | flops 1 | bytes 899999 | tf_op jit(solution)/shard_map/in_z_order/pallas_call | solution.py:249
  39.2 9.4 %collective-permute-done.6.refs_2_ = bf16[32,4096]{1,0:T(8,128)(2,1)S(1)} collective-permute-done((bf16[32,4096]{1,0:T(8,128)(2,1)S(1)}, bf16[32,4096]{1,0:T(8,128)(2,1)S(1)}, u32[]{:S(2)}, u32[]{:S(2)}) %collective-permute-start.6) | collective-permute-done | bytes 262176 | tf_op jit(solution)/shard_map/ppermute | solution.py:195
  49.2 6.5 %collective-permute-done.4.refs_2_ = bf16[128,4224]{1,0:T(8,128)(2,1)S(1)} collective-permute-done((bf16[128,4224]{1,0:T(8,128)(2,1)}, bf16[128,4224]{1,0:T(8,128)(2,1)S(1)}, u32[]{:S(2)}, u32[]{:S(2)}) %collective-permute-start.4) | collective-permute-done | bytes 1081376 | tf_op jit(solution)/shard_map/ppermute | solution.py:195
  60.4 11.6 %collective-permute-done.9.refs_4_ = bf16[64,4224]{1,0:T(8,128)(2,1)} collective-permute-done((bf16[64,4224]{1,0:T(8,128)(2,1)S(1)}, bf16[64,4224]{1,0:T(8,128)(2,1)}, u32[]{:S(2)}, u32[]{:S(2)}) %collective-permute-start.9) | collective-permute-done | bytes 540704 | tf_op jit(solution)/shard_map/ppermute | solution.py:195
  78.5 9.6 %project.1 = (bf16[512,1024]{1,0:T(8,128)(2,1)}, bf16[512,1024]{1,0:T(8,128)(2,1)}, bf16[512,1024]{1,0:T(8,128)(2,1)}, f32[16,1024]{1,0:T(8,128)}) custom-call(s32[3]{0:T(128)} %pad_add_fusion.ids_ref, bf16[512,1024]{1,0:T(8,128)(2,1)} %bitcast.26, bf16[128,4224]{1,0:T(8,128)(2,1)} %in_z_order.3.refs_0_, bf16[128,4224]{1,0:T(8,128)(2,1)} %copy-done.1, ...), custom_call_target="tpu_custom_call" | custom-call | flops 1 | bytes 3000000 | tf_op jit(solution)/shard_map/project/pallas_call | solution.py:373
  88.1 4.4 %collective-permute-start.25 = (bf16[128,1024]{1,0:T(8,128)(2,1)S(1)}, bf16[128,1024]{1,0:T(8,128)(2,1)}, u32[]{:S(2)}, u32[]{:S(2)}) collective-permute-start(bf16[128,1024]{1,0:T(8,128)(2,1)S(1)} %copy-done.26), channel_id=1, source_target_pairs={{0,2},{1,3},{2,0},{3,1},{4,6},{5,7},{6,4},{7,5},{8,10},{9,11},{10,... | collective-permute-start | bytes 786440 | tf_op jit(solution)/shard_map/ppermute | solution.py:195
  92.5 12.8 %attend_forward.1 = (bf16[512,1024]{1,0:T(8,128)(2,1)}, f32[1,8,8,512]{3,2,1,0:T(8,128)}) custom-call(s32[1,1,512]{2,1,0:T(1,128)} %bitcast.37, bf16[512,1024]{1,0:T(8,128)(2,1)} %get-tuple-element.110.q_ref, bf16[512,1024]{1,0:T(8,128)(2,1)} %get-tuple-element.111.k_ref, bf16[512,1024]{1,0:T(8,128)(2,1)} %get-tuple-element.112.v_ref), custom_call_target="tpu_custom_call" | custom-call | flops 1 | bytes 3900000 | tf_op jit(solution)/shard_map/attend_forward/pallas_call | solution.py:154
  109.6 6.8 %close_attention.1 = (f32[512,1024]{1,0:T(8,128)}, f32[512,128]{1,0:T(8,128)}, bf16[512,1024]{1,0:T(8,128)(2,1)}) custom-call(s32[3]{0:T(128)} %pad_add_fusion.ids_ref, bf16[512,1024]{1,0:T(8,128)(2,1)} %get-tuple-element.113.m_ref.refs_0_, bf16[512,1024]{1,0:T(8,128)(2,1)} %bitcast.27, f32[16,1024]{1,0:T(8,128)} %get-tuple-element.109.vec_ref, ...), custom_call_target="tpu_custom_call" | custom-call | flops 1 | bytes 2100000 | tf_op jit(solution)/shard_map/close_attention/pallas_call | solution.py:373
  116.9 4.3 %collective-permute-done.26.refs_3_ = bf16[128,1024]{1,0:T(8,128)(2,1)} collective-permute-done((bf16[128,1024]{1,0:T(8,128)(2,1)}, bf16[128,1024]{1,0:T(8,128)(2,1)}, u32[]{:S(2)}, u32[]{:S(2)}) %collective-permute-start.26) | collective-permute-done | bytes 262176 | tf_op jit(solution)/shard_map/ppermute | solution.py:195
  130.9 13.9 %ffn_in.1 = (bf16[512,4096]{1,0:T(8,128)(2,1)}, f32[512,4096]{1,0:T(8,128)}) custom-call(s32[3]{0:T(128)} %pad_add_fusion.ids_ref, bf16[512,1024]{1,0:T(8,128)(2,1)} %get-tuple-element.114.x_ref.refs_0_.refs_1_.refs_2_.refs_3_, f32[1,4096]{1,0:T(1,128)} %reshape.116.bias_ref, bf16[128,4096]{1,0:T(8,128)(2,1)} %in_z_order.4.refs_0_.refs_10_, ...), custom_call_target="tpu_custom_call" | custom-call | flops 1 | bytes 3900000 | tf_op jit(solution)/shard_map/ffn_in/pallas_call | solution.py:373
  144.8 5.5 %collective-permute-done.28.refs_2_.refs_6_ = bf16[512,1024]{1,0:T(8,128)(2,1)S(1)} collective-permute-done((bf16[512,1024]{1,0:T(8,128)(2,1)}, bf16[512,1024]{1,0:T(8,128)(2,1)S(1)}, u32[]{:S(2)}, u32[]{:S(2)}) %collective-permute-start.28) | collective-permute-done | bytes 1048608 | tf_op jit(solution)/shard_map/ppermute | solution.py:195
  154.4 10.5 %collective-permute-done.30.refs_4_.refs_8_ = bf16[256,1024]{1,0:T(8,128)(2,1)S(1)} collective-permute-done((bf16[256,1024]{1,0:T(8,128)(2,1)S(1)}, bf16[256,1024]{1,0:T(8,128)(2,1)S(1)}, u32[]{:S(2)}, u32[]{:S(2)}) %collective-permute-start.30) | collective-permute-done | bytes 524320 | tf_op jit(solution)/shard_map/ppermute | solution.py:195
  169.7 15.6 %ffn_out.1 = (bf16[512,1024]{1,0:T(8,128)(2,1)}, f32[512,1024]{1,0:T(8,128)}, bf16[512,1024]{1,0:T(8,128)(2,1)}, f32[8,1024]{1,0:T(8,128)}, bf16[2048,1024]{1,0:T(8,128)(2,1)}) custom-call(s32[3]{0:T(128)} %pad_add_fusion.ids_ref, f32[16,1024]{1,0:T(8,128)} %get-tuple-element.109.vec_ref, bf16[512,4096]{1,0:T(8,128)(2,1)} %get-tuple-element.122.act_hbm.refs_0_, ...), custom_call_target="tpu_custom_call" | custom-call | flops 1 | bytes 5399999 | tf_op jit(solution)/shard_map/ffn_out/pallas_call | solution.py:373
  185.5 14.0 %ffn_back.1 = (bf16[512,4096]{1,0:T(8,128)(2,1)}, f32[8,4096]{1,0:T(8,128)}, bf16[512,4096]{1,0:T(8,128)(2,1)}) custom-call(s32[3]{0:T(128)} %pad_add_fusion.ids_ref, bf16[512,1024]{1,0:T(8,128)(2,1)} %get-tuple-element.135.grad_ref.refs_1_, f32[512,4096]{1,0:T(8,128)} %get-tuple-element.136.slope_ref, ...), custom_call_target="tpu_custom_call" | custom-call | flops 1 | bytes 3599999 | tf_op jit(solution)/shard_map/ffn_back/pallas_call | solution.py:373
  199.9 7.8 %rows_of_own_core.3 = (bf16[1024,512]{1,0:T(8,128)(2,1)}, bf16[1024,512]{1,0:T(8,128)(2,1)}, bf16[1024,512]{1,0:T(8,128)(2,1)}, bf16[1024,512]{1,0:T(8,128)(2,1)}) custom-call(s32[3]{0:T(128)} %pad_add_fusion.ids_ref, bf16[512,4096]{1,0:T(8,128)(2,1)} %get-tuple-element.122.act_hbm.refs_0_, bf16[512,1024]{1,0:T(8,128)(2,1)} %get-tuple-element.135.grad_ref.refs_1_, ...), custom_call_target="tpu_custom_call" | custom-call | flops 1 | bytes 2699999 | tf_op jit(solution)/shard_map/rows_of_own_core/pallas_call | solution.py:373
  210.8 15.9 %attention_norm_back.1 = (bf16[512,1024]{1,0:T(8,128)(2,1)}, f32[512,1024]{1,0:T(8,128)}, bf16[512,1024]{1,0:T(8,128)(2,1)}, f32[8,1024]{1,0:T(8,128)}) custom-call(s32[3]{0:T(128)} %pad_add_fusion.ids_ref, f32[512,128]{1,0:T(8,128)} %get-tuple-element.134.inverse_ref, f32[16,1024]{1,0:T(8,128)} %get-tuple-element.109.vec_ref, ...), custom_call_target="tpu_custom_call" | custom-call | flops 1 | bytes 4800000 | tf_op jit(solution)/shard_map/attention_norm_back/pallas_call | solution.py:373
  226.7 7.8 %rows_of_own_core.4 = (bf16[256,2048]{1,0:T(8,128)(2,1)}, bf16[256,2048]{1,0:T(8,128)(2,1)}, bf16[256,2048]{1,0:T(8,128)(2,1)}, bf16[256,2048]{1,0:T(8,128)(2,1)}) custom-call(s32[3]{0:T(128)} %pad_add_fusion.ids_ref, bf16[512,1024]{1,0:T(8,128)(2,1)} %get-tuple-element.114.x_ref.refs_0_.refs_1_.refs_2_.refs_3_, ...), custom_call_target="tpu_custom_call" | custom-call | flops 1 | bytes 2699999 | tf_op jit(solution)/shard_map/rows_of_own_core/pallas_call | solution.py:373
  237.0 17.0 %attend_backward.1 = (bf16[512,1024]{1,0:T(8,128)(2,1)}, bf16[512,1024]{1,0:T(8,128)(2,1)}, bf16[512,1024]{1,0:T(8,128)(2,1)}, f32[1,8,1024]{2,1,0:T(8,128)}, f32[1,8,1024]{2,1,0:T(8,128)}) custom-call(s32[1,1,512]{2,1,0:T(1,128)} %bitcast.38, bf16[512,1024]{1,0:T(8,128)(2,1)} %get-tuple-element.110.q_ref, bf16[512,1024]{1,0:T(8,128)(2,1)} %get-tuple-element.111.k_ref, ...), custom_call_target="tpu_custom_call" | custom-call | flops 1 | bytes 5100000 | tf_op jit(solution)/shard_map/attend_backward/pallas_call | solution.py:174
  254.0 4.5 %cross_near.1 = (bf16[512,1024]{1,0:T(8,128)(2,1)}, bf16[512,1024]{1,0:T(8,128)(2,1)}) custom-call(s32[3]{0:T(128)} %pad_add_fusion.ids_ref, bf16[1024,512]{1,0:T(8,128)(2,1)} %get-tuple-element.141.refs_20_.refs_0_, bf16[1024,512]{1,0:T(8,128)(2,1)} %copy-done.9, bf16[1024,512]{1,0:T(8,128)(2,1)} %get-tuple-element.152.refs_2_, ...), custom_call_target="tpu_custom_call" | custom-call | flops 1 | bytes 1799999 | tf_op jit(solution)/shard_map/cross_near/pallas_call | solution.py:373
  260.5 7.2 %rows_of_other_core.1.refs_4_ = bf16[512,4096]{1,0:T(8,128)(2,1)} custom-call(s32[3]{0:T(128)} %pad_add_fusion.ids_ref, bf16[512,1024]{1,0:T(8,128)(2,1)} %get-tuple-element.113.m_ref.refs_0_, bf16[512,1024]{1,0:T(8,128)(2,1)} %bitcast.28, bf16[512,1024]{1,0:T(8,128)(2,1)} %get-tuple-element.145.refs_3_.refs_2_, ...), custom_call_target="tpu_custom_call" | custom-call | flops 1 | bytes 2100000 | tf_op jit(solution)/shard_map/rows_of_other_core/pallas_call | solution.py:373
  269.2 4.0 %fold.2 = (bf16[128,2048]{1,0:T(8,128)(2,1)}, bf16[128,2048]{1,0:T(8,128)(2,1)}, bf16[128,2048]{1,0:T(8,128)(2,1)}, bf16[128,2048]{1,0:T(8,128)(2,1)}) custom-call(s32[3]{0:T(128)} %pad_add_fusion.ids_ref, bf16[256,2048]{1,0:T(8,128)(2,1)} %get-tuple-element.146.rest_0_.refs_0_, bf16[256,2048]{1,0:T(8,128)(2,1)} %copy-done.11, ...), custom_call_target="tpu_custom_call" | custom-call | flops 1 | bytes 1200000 | tf_op jit(solution)/shard_map/fold/pallas_call | solution.py:373
  275.2 8.2 %rows_of_own_core.5 = (bf16[256,2048]{1,0:T(8,128)(2,1)}, bf16[256,2048]{1,0:T(8,128)(2,1)}, bf16[256,2048]{1,0:T(8,128)(2,1)}, bf16[256,2048]{1,0:T(8,128)(2,1)}) custom-call(s32[3]{0:T(128)} %pad_add_fusion.ids_ref, bf16[512,1024]{1,0:T(8,128)(2,1)} %get-tuple-element.113.m_ref.refs_0_, bf16[512,1024]{1,0:T(8,128)(2,1)} %bitcast.29, ...), custom_call_target="tpu_custom_call" | custom-call | flops 1 | bytes 2699999 | tf_op jit(solution)/shard_map/rows_of_own_core/pallas_call | solution.py:373
  289.2 3.3 fold_z.1
  295.5 14.9 %collective-permute-done.43.refs_1_ = bf16[256,2048]{1,0:T(8,128)(2,1)S(1)} collective-permute-done((bf16[256,2048]{1,0:T(8,128)(2,1)}, bf16[256,2048]{1,0:T(8,128)(2,1)S(1)}, u32[]{:S(2)}, u32[]{:S(2)}) %collective-permute-start.43) | collective-permute-done | bytes 1048608 | tf_op jit(solution)/shard_map/ppermute | solution.py:195
  311.4 4.1 %fold.3 = (bf16[128,2048]{1,0:T(8,128)(2,1)}, bf16[128,2048]{1,0:T(8,128)(2,1)}, bf16[128,2048]{1,0:T(8,128)(2,1)}, bf16[128,2048]{1,0:T(8,128)(2,1)}) custom-call(s32[3]{0:T(128)} %pad_add_fusion.ids_ref, bf16[256,2048]{1,0:T(8,128)(2,1)} %get-tuple-element.158.refs_4_.refs_0_, bf16[256,2048]{1,0:T(8,128)(2,1)} %copy-done.18, ...), custom_call_target="tpu_custom_call" | custom-call | flops 1 | bytes 1200000 | tf_op jit(solution)/shard_map/fold/pallas_call | solution.py:373
  320.0 10.1 %inputs_back.1.refs_4_ = f32[512,1024]{1,0:T(8,128)} custom-call(s32[3]{0:T(128)} %pad_add_fusion.ids_ref, f32[512,1024]{1,0:T(8,128)} %get-tuple-element.142.base_ref, bf16[512,1024]{1,0:T(8,128)(2,1)} %get-tuple-element.149.refs_4_.refs_3_.q_ref, bf16[512,1024]{1,0:T(8,128)(2,1)} %get-tuple-element.150.refs_4_.k_ref, ...), custom_call_target="tpu_custom_call" | custom-call | flops 1 | bytes 3000000 | tf_op jit(solution)/shard_map/inputs_back/pallas_call | solution.py:373
  331.1 3.4 fold_direct.1
  344.8 4.6 %collective-permute-done.49 = bf16[32,4096]{1,0:T(8,128)(2,1)S(1)} collective-permute-done((bf16[32,4096]{1,0:T(8,128)(2,1)S(1)}, bf16[32,4096]{1,0:T(8,128)(2,1)S(1)}, u32[]{:S(2)}, u32[]{:S(2)}) %collective-permute-start.49) | collective-permute-done | bytes 262176 | tf_op jit(solution)/shard_map/ppermute | solution.py:195
  352.8 7.7 %collective-permute-done.50 = bf16[32,4096]{1,0:T(8,128)(2,1)S(1)} collective-permute-done((bf16[32,4096]{1,0:T(8,128)(2,1)S(1)}, bf16[32,4096]{1,0:T(8,128)(2,1)S(1)}, u32[]{:S(2)}, u32[]{:S(2)}) %collective-permute-start.50) | collective-permute-done | bytes 262176 | tf_op jit(solution)/shard_map/ppermute | solution.py:195
  (219 shorter events, 93.6 us)
Async XLA Ops:
  2.6 16.6 %collective-permute-start.1 = (bf16[32,4224]{1,0:T(8,128)(2,1)}, bf16[32,4224]{1,0:T(8,128)(2,1)S(1)}, u32[]{:S(2)}, u32[]{:S(2)}) collective-permute-start(bf16[32,4224]{1,0:T(8,128)(2,1)} %first_shard.1.refs_0_), channel_id=1, source_target_pairs={{0,2},{1,3},{2,0},{3,1},{4,6},{5,7},{6,4},{7,5},{8,10},{9,11},{10,... | collective-permute-start | bytes 811016 | tf_op jit(solution)/shard_map/ppermute | solution.py:195
  31.4 24.3 %collective-permute-start.4 = (bf16[128,4224]{1,0:T(8,128)(2,1)}, bf16[128,4224]{1,0:T(8,128)(2,1)S(1)}, u32[]{:S(2)}, u32[]{:S(2)}) collective-permute-start(bf16[128,4224]{1,0:T(8,128)(2,1)} %in_z_order.3.refs_0_), channel_id=1, source_target_pairs={{0,16},{1,17},{2,18},{3,19},{4,20},{5,21},{6,22},{7,23},{8,24},{9,... | collective-permute-start | bytes 3244040 | tf_op jit(solution)/shard_map/ppermute | solution.py:195
  32.7 24.4 %collective-permute-start.3 = (bf16[128,4224]{1,0:T(8,128)(2,1)}, bf16[128,4224]{1,0:T(8,128)(2,1)S(1)}, u32[]{:S(2)}, u32[]{:S(2)}) collective-permute-start(bf16[128,4224]{1,0:T(8,128)(2,1)} %in_z_order.3.refs_0_), channel_id=1, source_target_pairs={{0,8},{1,9},{2,10},{3,11},{4,12},{5,13},{6,14},{7,15},{8,0},{9,1},... | collective-permute-start | bytes 3244040 | tf_op jit(solution)/shard_map/ppermute | solution.py:195
  37.4 18.2 %collective-permute-start.5 = (bf16[32,4096]{1,0:T(8,128)(2,1)S(1)}, bf16[32,4096]{1,0:T(8,128)(2,1)S(1)}, u32[]{:S(2)}, u32[]{:S(2)}) collective-permute-start(bf16[32,4096]{1,0:T(8,128)(2,1)S(1)} %copy-done.25), channel_id=1, source_target_pairs={{0,1},{1,0},{2,3},{3,2},{4,5},{5,4},{6,7},{7,6},{8,9},{9,8},{10,11... | collective-permute-start | bytes 786440 | tf_op jit(solution)/shard_map/ppermute | solution.py:195
  49.2 27.2 %collective-permute-start.10 = (bf16[128,4224]{1,0:T(8,128)(2,1)}, bf16[128,4224]{1,0:T(8,128)(2,1)S(1)}, u32[]{:S(2)}, u32[]{:S(2)}) collective-permute-start(bf16[128,4224]{1,0:T(8,128)(2,1)} %in_z_order.3.refs_0_), channel_id=1, source_target_pairs={{0,4},{1,5},{2,6},{3,7},{4,0},{5,1},{6,2},{7,3},{8,12},{9,13},{10,... | collective-permute-start | bytes 3244040 | tf_op jit(solution)/shard_map/ppermute | solution.py:195
  55.7 20.7 %collective-permute-start.12 = (bf16[128,4224]{1,0:T(8,128)(2,1)S(1)}, bf16[128,4224]{1,0:T(8,128)(2,1)}, u32[]{:S(2)}, u32[]{:S(2)}) collective-permute-start(bf16[128,4224]{1,0:T(8,128)(2,1)S(1)} %collective-permute-done.4.refs_2_), channel_id=1, source_target_pairs={{0,4},{1,5},{2,6},{3,7},{4,0},{5,1},{6,2},{7,3},{8,12},{9,13},{10,... | collective-permute-start | bytes 3244040 | tf_op jit(solution)/shard_map/ppermute | solution.py:195
  57.2 14.8 %collective-permute-start.9 = (bf16[64,4224]{1,0:T(8,128)(2,1)S(1)}, bf16[64,4224]{1,0:T(8,128)(2,1)}, u32[]{:S(2)}, u32[]{:S(2)}) collective-permute-start(bf16[64,4224]{1,0:T(8,128)(2,1)S(1)} %slice.107), channel_id=1, source_target_pairs={{0,8},{1,9},{2,10},{3,11},{4,12},{5,13},{6,14},{7,15},{8,0},{9,1},... | collective-permute-start | bytes 1622024 | tf_op jit(solution)/shard_map/ppermute | solution.py:195
  58.7 17.7 %collective-permute-start.11 = (bf16[128,4224]{1,0:T(8,128)(2,1)S(1)}, bf16[128,4224]{1,0:T(8,128)(2,1)}, u32[]{:S(2)}, u32[]{:S(2)}) collective-permute-start(bf16[128,4224]{1,0:T(8,128)(2,1)S(1)} %collective-permute-done.3.refs_1_), channel_id=1, source_target_pairs={{0,4},{1,5},{2,6},{3,7},{4,0},{5,1},{6,2},{7,3},{8,12},{9,13},{10,... | collective-permute-start | bytes 3244040 | tf_op jit(solution)/shard_map/ppermute | solution.py:195
  76.4 28.9 %collective-permute-start.16 = (bf16[128,4096]{1,0:T(8,128)(2,1)}, bf16[128,4096]{1,0:T(8,128)(2,1)S(1)}, u32[]{:S(2)}, u32[]{:S(2)}) collective-permute-start(bf16[128,4096]{1,0:T(8,128)(2,1)} %in_z_order.4.refs_0_.refs_10_), channel_id=1, source_target_pairs={{0,16},{1,17},{2,18},{3,19},{4,20},{5,21},{6,22},{7,23},{8,24},{9,... | collective-permute-start | bytes 3145736 | tf_op jit(solution)/shard_map/ppermute | solution.py:195
  78.0 27.3 %collective-permute-start.15 = (bf16[128,4096]{1,0:T(8,128)(2,1)}, bf16[128,4096]{1,0:T(8,128)(2,1)S(1)}, u32[]{:S(2)}, u32[]{:S(2)}) collective-permute-start(bf16[128,4096]{1,0:T(8,128)(2,1)} %in_z_order.4.refs_0_.refs_10_), channel_id=1, source_target_pairs={{0,8},{1,9},{2,10},{3,11},{4,12},{5,13},{6,14},{7,15},{8,0},{9,1},... | collective-permute-start | bytes 3145736 | tf_op jit(solution)/shard_map/ppermute | solution.py:195
  78.5 47.6 %collective-permute-start.19 = (bf16[128,4096]{1,0:T(8,128)(2,1)}, bf16[128,4096]{1,0:T(8,128)(2,1)}, u32[]{:S(2)}, u32[]{:S(2)}) collective-permute-start(bf16[128,4096]{1,0:T(8,128)(2,1)} %in_z_order.4.refs_0_.refs_10_), channel_id=1, source_target_pairs={{0,4},{1,5},{2,6},{3,7},{4,0},{5,1},{6,2},{7,3},{8,12},{9,13},{10,... | collective-permute-start | bytes 3145736 | tf_op jit(solution)/shard_map/ppermute | solution.py:195
  88.1 20.8 %collective-permute-start.25 = (bf16[128,1024]{1,0:T(8,128)(2,1)S(1)}, bf16[128,1024]{1,0:T(8,128)(2,1)}, u32[]{:S(2)}, u32[]{:S(2)}) collective-permute-start(bf16[128,1024]{1,0:T(8,128)(2,1)S(1)} %copy-done.26), channel_id=1, source_target_pairs={{0,2},{1,3},{2,0},{3,1},{4,6},{5,7},{6,4},{7,5},{8,10},{9,11},{10,... | collective-permute-start | bytes 786440 | tf_op jit(solution)/shard_map/ppermute | solution.py:195
  105.4 19.1 %collective-permute-start.18 = (bf16[64,4096]{1,0:T(8,128)(2,1)S(1)}, bf16[64,4096]{1,0:T(8,128)(2,1)}, u32[]{:S(2)}, u32[]{:S(2)}) collective-permute-start(bf16[64,4096]{1,0:T(8,128)(2,1)S(1)} %slice.110), channel_id=1, source_target_pairs={{0,8},{1,9},{2,10},{3,11},{4,12},{5,13},{6,14},{7,15},{8,0},{9,1},... | collective-permute-start | bytes 1572872 | tf_op jit(solution)/shard_map/ppermute | solution.py:195
  107.0 17.6 %collective-permute-start.17 = (bf16[64,4096]{1,0:T(8,128)(2,1)S(1)}, bf16[64,4096]{1,0:T(8,128)(2,1)}, u32[]{:S(2)}, u32[]{:S(2)}) collective-permute-start(bf16[64,4096]{1,0:T(8,128)(2,1)S(1)} %slice.109), channel_id=1, source_target_pairs={{0,16},{1,17},{2,18},{3,19},{4,20},{5,21},{6,22},{7,23},{8,24},{9,... | collective-permute-start | bytes 1572872 | tf_op jit(solution)/shard_map/ppermute | solution.py:195
  124.6 25.7 %collective-permute-start.28 = (bf16[512,1024]{1,0:T(8,128)(2,1)}, bf16[512,1024]{1,0:T(8,128)(2,1)S(1)}, u32[]{:S(2)}, u32[]{:S(2)}) collective-permute-start(bf16[512,1024]{1,0:T(8,128)(2,1)} %in_z_order.5.refs_0_.refs_4_), channel_id=1, source_target_pairs={{0,16},{1,17},{2,18},{3,19},{4,20},{5,21},{6,22},{7,23},{8,24},{9,... | collective-permute-start | bytes 3145736 | tf_op jit(solution)/shard_map/ppermute | solution.py:195
  126.1 25.5 %collective-permute-start.27 = (bf16[512,1024]{1,0:T(8,128)(2,1)}, bf16[512,1024]{1,0:T(8,128)(2,1)}, u32[]{:S(2)}, u32[]{:S(2)}) collective-permute-start(bf16[512,1024]{1,0:T(8,128)(2,1)} %in_z_order.5.refs_0_.refs_4_), channel_id=1, source_target_pairs={{0,8},{1,9},{2,10},{3,11},{4,12},{5,13},{6,14},{7,15},{8,0},{9,1},... | collective-permute-start | bytes 3145736 | tf_op jit(solution)/shard_map/ppermute | solution.py:195
  130.7 35.6 %collective-permute-start.31 = (bf16[512,1024]{1,0:T(8,128)(2,1)}, bf16[512,1024]{1,0:T(8,128)(2,1)}, u32[]{:S(2)}, u32[]{:S(2)}) collective-permute-start(bf16[512,1024]{1,0:T(8,128)(2,1)} %in_z_order.5.refs_0_.refs_4_), channel_id=1, source_target_pairs={{0,4},{1,5},{2,6},{3,7},{4,0},{5,1},{6,2},{7,3},{8,12},{9,13},{10,... | collective-permute-start | bytes 3145736 | tf_op jit(solution)/shard_map/ppermute | solution.py:195
  199.4 27.3 %collective-permute-start.37 = (bf16[512,4096]{1,0:T(8,128)(2,1)}, bf16[512,4096]{1,0:T(8,128)(2,1)}, u32[]{:S(2)}, u32[]{:S(2)}) collective-permute-start(bf16[512,4096]{1,0:T(8,128)(2,1)} %get-tuple-element.140.refs_3_), channel_id=1, source_target_pairs={{0,4},{1,5},{2,6},{3,7},{4,0},{5,1},{6,2},{7,3},{8,12},{9,13},{10,... | collective-permute-start | bytes 12582920 | tf_op jit(solution)/shard_map/ppermute | solution.py:195
  207.8 27.9 %collective-permute-start.38 = (bf16[1024,512]{1,0:T(8,128)(2,1)}, bf16[1024,512]{1,0:T(8,128)(2,1)S(1)}, u32[]{:S(2)}, u32[]{:S(2)}) collective-permute-start(bf16[1024,512]{1,0:T(8,128)(2,1)} %get-tuple-element.147), channel_id=1, source_target_pairs={{0,8},{1,9},{2,10},{3,11},{4,12},{5,13},{6,14},{7,15},{8,0},{9,1},... | collective-permute-start | bytes 3145736 | tf_op jit(solution)/shard_map/ppermute | solution.py:195
  209.6 26.1 %collective-permute-start.39 = (bf16[1024,512]{1,0:T(8,128)(2,1)}, bf16[1024,512]{1,0:T(8,128)(2,1)S(1)}, u32[]{:S(2)}, u32[]{:S(2)}) collective-permute-start(bf16[1024,512]{1,0:T(8,128)(2,1)} %get-tuple-element.148), channel_id=1, source_target_pairs={{0,16},{1,17},{2,18},{3,19},{4,20},{5,21},{6,22},{7,23},{8,24},{9,... | collective-permute-start | bytes 3145736 | tf_op jit(solution)/shard_map/ppermute | solution.py:195
  234.6 24.9 %collective-permute-start.40 = (bf16[256,2048]{1,0:T(8,128)(2,1)}, bf16[256,2048]{1,0:T(8,128)(2,1)S(1)}, u32[]{:S(2)}, u32[]{:S(2)}) collective-permute-start(bf16[256,2048]{1,0:T(8,128)(2,1)} %get-tuple-element.154), channel_id=1, source_target_pairs={{0,8},{1,9},{2,10},{3,11},{4,12},{5,13},{6,14},{7,15},{8,0},{9,1},... | collective-permute-start | bytes 3145736 | tf_op jit(solution)/shard_map/ppermute | solution.py:195
  234.9 24.8 %collective-permute-start.41 = (bf16[256,2048]{1,0:T(8,128)(2,1)}, bf16[256,2048]{1,0:T(8,128)(2,1)}, u32[]{:S(2)}, u32[]{:S(2)}) collective-permute-start(bf16[256,2048]{1,0:T(8,128)(2,1)} %get-tuple-element.155), channel_id=1, source_target_pairs={{0,16},{1,17},{2,18},{3,19},{4,20},{5,21},{6,22},{7,23},{8,24},{9,... | collective-permute-start | bytes 3145736 | tf_op jit(solution)/shard_map/ppermute | solution.py:195
  267.7 25.8 %collective-permute-start.54 = (bf16[512,1024]{1,0:T(8,128)(2,1)}, bf16[512,1024]{1,0:T(8,128)(2,1)S(1)}, u32[]{:S(2)}, u32[]{:S(2)}) collective-permute-start(bf16[512,1024]{1,0:T(8,128)(2,1)} %get-tuple-element.184), channel_id=1, source_target_pairs={{0,1},{1,0},{2,3},{3,2},{4,5},{5,4},{6,7},{7,6},{8,9},{9,8},{10,11... | collective-permute-start | bytes 3145736 | tf_op jit(solution)/shard_map/ppermute | solution.py:195
  273.2 14.8 %collective-permute-start.45 = (bf16[128,2048]{1,0:T(8,128)(2,1)}, bf16[128,2048]{1,0:T(8,128)(2,1)}, u32[]{:S(2)}, u32[]{:S(2)}) collective-permute-start(bf16[128,2048]{1,0:T(8,128)(2,1)} %get-tuple-element.162), channel_id=1, source_target_pairs={{0,16},{1,17},{2,18},{3,19},{4,20},{5,21},{6,22},{7,23},{8,24},{9,... | collective-permute-start | bytes 1572872 | tf_op jit(solution)/shard_map/ppermute | solution.py:195
  274.1 15.1 %collective-permute-start.46 = (bf16[128,2048]{1,0:T(8,128)(2,1)}, bf16[128,2048]{1,0:T(8,128)(2,1)}, u32[]{:S(2)}, u32[]{:S(2)}) collective-permute-start(bf16[128,2048]{1,0:T(8,128)(2,1)} %get-tuple-element.164), channel_id=1, source_target_pairs={{0,8},{1,9},{2,10},{3,11},{4,12},{5,13},{6,14},{7,15},{8,0},{9,1},... | collective-permute-start | bytes 1572872 | tf_op jit(solution)/shard_map/ppermute | solution.py:195
  283.5 27.0 %collective-permute-start.43 = (bf16[256,2048]{1,0:T(8,128)(2,1)}, bf16[256,2048]{1,0:T(8,128)(2,1)S(1)}, u32[]{:S(2)}, u32[]{:S(2)}) collective-permute-start(bf16[256,2048]{1,0:T(8,128)(2,1)} %get-tuple-element.159), channel_id=1, source_target_pairs={{0,8},{1,9},{2,10},{3,11},{4,12},{5,13},{6,14},{7,15},{8,0},{9,1},... | collective-permute-start | bytes 3145736 | tf_op jit(solution)/shard_map/ppermute | solution.py:195
  284.4 26.1 %collective-permute-start.44 = (bf16[256,2048]{1,0:T(8,128)(2,1)}, bf16[256,2048]{1,0:T(8,128)(2,1)}, u32[]{:S(2)}, u32[]{:S(2)}) collective-permute-start(bf16[256,2048]{1,0:T(8,128)(2,1)} %get-tuple-element.161), channel_id=1, source_target_pairs={{0,16},{1,17},{2,18},{3,19},{4,20},{5,21},{6,22},{7,23},{8,24},{9,... | collective-permute-start | bytes 3145736 | tf_op jit(solution)/shard_map/ppermute | solution.py:195
  292.5 25.1 %collective-permute-start.52 = (bf16[64,4096]{1,0:T(8,128)(2,1)}, bf16[64,4096]{1,0:T(8,128)(2,1)}, u32[]{:S(2)}, u32[]{:S(2)}) collective-permute-start(bf16[64,4096]{1,0:T(8,128)(2,1)} %get-tuple-element.181), channel_id=1, source_target_pairs={{0,1},{1,0},{2,3},{3,2},{4,5},{5,4},{6,7},{7,6},{8,9},{9,8},{10,11... | collective-permute-start | bytes 1572872 | tf_op jit(solution)/shard_map/ppermute | solution.py:195
  294.8 39.8 %collective-permute-start.55 = (bf16[256,1024]{1,0:T(8,128)(2,1)}, bf16[256,1024]{1,0:T(8,128)(2,1)}, u32[]{:S(2)}, u32[]{:S(2)}) collective-permute-start(bf16[256,1024]{1,0:T(8,128)(2,1)} %get-tuple-element.188), channel_id=1, source_target_pairs={{0,2},{1,3},{2,0},{3,1},{4,6},{5,7},{6,4},{7,5},{8,10},{9,11},{10,... | collective-permute-start | bytes 1572872 | tf_op jit(solution)/shard_map/ppermute | solution.py:195
  318.8 22.2 %collective-permute-start.53 = (bf16[32,4096]{1,0:T(8,128)(2,1)S(1)}, bf16[32,4096]{1,0:T(8,128)(2,1)S(1)}, u32[]{:S(2)}, u32[]{:S(2)}) collective-permute-start(bf16[32,4096]{1,0:T(8,128)(2,1)S(1)} %slice.152), channel_id=1, source_target_pairs={{0,2},{1,3},{2,0},{3,1},{4,6},{5,7},{6,4},{7,5},{8,10},{9,11},{10,... | collective-permute-start | bytes 786440 | tf_op jit(solution)/shard_map/ppermute | solution.py:195
  339.2 21.4 %collective-permute-start.50 = (bf16[32,4096]{1,0:T(8,128)(2,1)S(1)}, bf16[32,4096]{1,0:T(8,128)(2,1)S(1)}, u32[]{:S(2)}, u32[]{:S(2)}) collective-permute-start(bf16[32,4096]{1,0:T(8,128)(2,1)S(1)} %copy-done.33), channel_id=1, source_target_pairs={{0,2},{1,3},{2,0},{3,1},{4,6},{5,7},{6,4},{7,5},{8,10},{9,11},{10,... | collective-permute-start | bytes 786440 | tf_op jit(solution)/shard_map/ppermute | solution.py:195
  341.0 19.5 %collective-permute-start.51 = (bf16[32,4096]{1,0:T(8,128)(2,1)S(1)}, bf16[32,4096]{1,0:T(8,128)(2,1)S(1)}, u32[]{:S(2)}, u32[]{:S(2)}) collective-permute-start(bf16[32,4096]{1,0:T(8,128)(2,1)S(1)} %copy-done.32), channel_id=1, source_target_pairs={{0,3},{1,2},{2,1},{3,0},{4,7},{5,6},{6,5},{7,4},{8,11},{9,10},{10,... | collective-permute-start | bytes 786440 | tf_op jit(solution)/shard_map/ppermute | solution.py:195
  (63 other events, 531.2 us)

commit v6 on v5

--- a/solution.py
+++ b/solution.py
@@ -239,7 +239,7 @@
     if rows % 16:
         stacked = jnp.stack(parts)
         return jnp.take(stacked, jnp.arange(net.inner) ^ ids[2], axis=0).reshape(-1, columns)
-    tile = next(columns // n for n in (2, 3, 1) if columns % (n * 128) == 0)
+    tile = columns
 
     def body(ids_ref, *refs):
         for s, part in enumerate(refs[:-1]):

time: 367 us -> 366 us (level)
  no operation moved by 1% of the time
where the time goes in v6:
time: 366 us; the launch traced here: 365 us
  Pallas kernels  177 us (48%)
  waiting for transfers between devices  107 us (29%)
  starting transfers between devices  57.8 us (16%)
  local copies, waits for them, and re-layouts  16.2 us (4%)
  other arithmetic  5.41 us (1%)
    pallas_call x16, Pallas kernels, kernel(): pl.pallas_call(body, out_shape=[o for o, _ in outs], grid_spec=pltpu.Pref...  136 us
    ppermute x58, waiting for transfers between devices, swap(): return lax.ppermute(value, AXES, pairs)  105 us
    ppermute x58, starting transfers between devices, swap(): return lax.ppermute(value, AXES, pairs)  55 us
    pallas_call x1, Pallas kernels, attend_backward(): pl.pallas_call(attend_backward_body, out_shape=[jax.ShapeDtypeStruct((tok...  17 us
    pallas_call x1, Pallas kernels, attend_forward(): pl.pallas_call(attend_forward_body, out_shape=[jax.ShapeDtypeStruct((toke...  12.8 us
    pallas_call x3, Pallas kernels, in_z_order(): pl.pallas_call(body, out_shape=struct((net.inner * rows, columns), BF), g...  8.77 us
    unnamed x70, local copies, waits for them, and re-layouts  7.62 us
  transfers between devices with their start and end apart: 59, of which 25 were waited for; matrix products, arithmetic and copies ran while one was open for 4% of the time, Pallas kernels for 41%

profile of v6, /device:TPU:0, one launch (start us, length us, event | category | flops | bytes accessed | tf_op | source)
XLA Modules:
  0.0 364.5 jit_solution(7528096856554774678)
XLA Ops:
  2.6 4.0 %collective-permute-start.1 = (bf16[32,4224]{1,0:T(8,128)(2,1)}, bf16[32,4224]{1,0:T(8,128)(2,1)S(1)}, u32[]{:S(2)}, u32[]{:S(2)}) collective-permute-start(bf16[32,4224]{1,0:T(8,128)(2,1)} %first_shard.1.refs_0_), channel_id=1, source_target_pairs={{0,2},{1,3},{2,0},{3,1},{4,6},{5,7},{6,4},{7,5},{8,10},{9,11},{10,... | collective-permute-start | bytes 811016 | tf_op jit(solution)/shard_map/ppermute | solution.py:195
  8.2 11.0 %collective-permute-done.1.refs_2_ = bf16[32,4224]{1,0:T(8,128)(2,1)S(1)} collective-permute-done((bf16[32,4224]{1,0:T(8,128)(2,1)}, bf16[32,4224]{1,0:T(8,128)(2,1)S(1)}, u32[]{:S(2)}, u32[]{:S(2)}) %collective-permute-start.1) | collective-permute-done | bytes 270368 | tf_op jit(solution)/shard_map/ppermute | solution.py:195
  20.5 6.3 %collective-permute-done.2.refs_3_ = bf16[32,4224]{1,0:T(8,128)(2,1)S(1)} collective-permute-done((bf16[32,4224]{1,0:T(8,128)(2,1)S(1)}, bf16[32,4224]{1,0:T(8,128)(2,1)S(1)}, u32[]{:S(2)}, u32[]{:S(2)}) %collective-permute-start.2) | collective-permute-done | bytes 270368 | tf_op jit(solution)/shard_map/ppermute | solution.py:195
  33.3 3.3 collective-permute-start.6
  38.3 9.4 %collective-permute-done.6.refs_2_ = bf16[32,4096]{1,0:T(8,128)(2,1)S(1)} collective-permute-done((bf16[32,4096]{1,0:T(8,128)(2,1)S(1)}, bf16[32,4096]{1,0:T(8,128)(2,1)S(1)}, u32[]{:S(2)}, u32[]{:S(2)}) %collective-permute-start.6) | collective-permute-done | bytes 262176 | tf_op jit(solution)/shard_map/ppermute | solution.py:195
  48.3 6.5 %collective-permute-done.4.refs_2_ = bf16[128,4224]{1,0:T(8,128)(2,1)S(1)} collective-permute-done((bf16[128,4224]{1,0:T(8,128)(2,1)}, bf16[128,4224]{1,0:T(8,128)(2,1)S(1)}, u32[]{:S(2)}, u32[]{:S(2)}) %collective-permute-start.4) | collective-permute-done | bytes 1081376 | tf_op jit(solution)/shard_map/ppermute | solution.py:195
  59.5 11.6 %collective-permute-done.9.refs_4_ = bf16[64,4224]{1,0:T(8,128)(2,1)} collective-permute-done((bf16[64,4224]{1,0:T(8,128)(2,1)S(1)}, bf16[64,4224]{1,0:T(8,128)(2,1)}, u32[]{:S(2)}, u32[]{:S(2)}) %collective-permute-start.9) | collective-permute-done | bytes 540704 | tf_op jit(solution)/shard_map/ppermute | solution.py:195
  77.7 9.6 %project.1 = (bf16[512,1024]{1,0:T(8,128)(2,1)}, bf16[512,1024]{1,0:T(8,128)(2,1)}, bf16[512,1024]{1,0:T(8,128)(2,1)}, f32[16,1024]{1,0:T(8,128)}) custom-call(s32[3]{0:T(128)} %pad_add_fusion.ids_ref, bf16[512,1024]{1,0:T(8,128)(2,1)} %bitcast.26, bf16[128,4224]{1,0:T(8,128)(2,1)} %in_z_order.3.refs_0_, bf16[128,4224]{1,0:T(8,128)(2,1)} %copy-done.1, ...), custom_call_target="tpu_custom_call" | custom-call | flops 1 | bytes 3000000 | tf_op jit(solution)/shard_map/project/pallas_call | solution.py:373
  87.3 4.4 %collective-permute-start.25 = (bf16[128,1024]{1,0:T(8,128)(2,1)S(1)}, bf16[128,1024]{1,0:T(8,128)(2,1)}, u32[]{:S(2)}, u32[]{:S(2)}) collective-permute-start(bf16[128,1024]{1,0:T(8,128)(2,1)S(1)} %copy-done.26), channel_id=1, source_target_pairs={{0,2},{1,3},{2,0},{3,1},{4,6},{5,7},{6,4},{7,5},{8,10},{9,11},{10,... | collective-permute-start | bytes 786440 | tf_op jit(solution)/shard_map/ppermute | solution.py:195
  91.7 12.8 %attend_forward.1 = (bf16[512,1024]{1,0:T(8,128)(2,1)}, f32[1,8,8,512]{3,2,1,0:T(8,128)}) custom-call(s32[1,1,512]{2,1,0:T(1,128)} %bitcast.37, bf16[512,1024]{1,0:T(8,128)(2,1)} %get-tuple-element.110.q_ref, bf16[512,1024]{1,0:T(8,128)(2,1)} %get-tuple-element.111.k_ref, bf16[512,1024]{1,0:T(8,128)(2,1)} %get-tuple-element.112.v_ref), custom_call_target="tpu_custom_call" | custom-call | flops 1 | bytes 3900000 | tf_op jit(solution)/shard_map/attend_forward/pallas_call | solution.py:154
  108.8 6.8 %close_attention.1 = (f32[512,1024]{1,0:T(8,128)}, f32[512,128]{1,0:T(8,128)}, bf16[512,1024]{1,0:T(8,128)(2,1)}) custom-call(s32[3]{0:T(128)} %pad_add_fusion.ids_ref, bf16[512,1024]{1,0:T(8,128)(2,1)} %get-tuple-element.113.m_ref.refs_0_, bf16[512,1024]{1,0:T(8,128)(2,1)} %bitcast.27, f32[16,1024]{1,0:T(8,128)} %get-tuple-element.109.vec_ref, ...), custom_call_target="tpu_custom_call" | custom-call | flops 1 | bytes 2100000 | tf_op jit(solution)/shard_map/close_attention/pallas_call | solution.py:373
  116.0 4.3 %collective-permute-done.26.refs_3_ = bf16[128,1024]{1,0:T(8,128)(2,1)} collective-permute-done((bf16[128,1024]{1,0:T(8,128)(2,1)}, bf16[128,1024]{1,0:T(8,128)(2,1)}, u32[]{:S(2)}, u32[]{:S(2)}) %collective-permute-start.26) | collective-permute-done | bytes 262176 | tf_op jit(solution)/shard_map/ppermute | solution.py:195
  130.1 13.9 %ffn_in.1 = (bf16[512,4096]{1,0:T(8,128)(2,1)}, f32[512,4096]{1,0:T(8,128)}) custom-call(s32[3]{0:T(128)} %pad_add_fusion.ids_ref, bf16[512,1024]{1,0:T(8,128)(2,1)} %get-tuple-element.114.x_ref.refs_0_.refs_1_.refs_2_.refs_3_, f32[1,4096]{1,0:T(1,128)} %reshape.116.bias_ref, bf16[128,4096]{1,0:T(8,128)(2,1)} %in_z_order.4.refs_0_.refs_10_, ...), custom_call_target="tpu_custom_call" | custom-call | flops 1 | bytes 3900000 | tf_op jit(solution)/shard_map/ffn_in/pallas_call | solution.py:373
  144.0 5.5 %collective-permute-done.28.refs_2_.refs_6_ = bf16[512,1024]{1,0:T(8,128)(2,1)S(1)} collective-permute-done((bf16[512,1024]{1,0:T(8,128)(2,1)}, bf16[512,1024]{1,0:T(8,128)(2,1)S(1)}, u32[]{:S(2)}, u32[]{:S(2)}) %collective-permute-start.28) | collective-permute-done | bytes 1048608 | tf_op jit(solution)/shard_map/ppermute | solution.py:195
  153.7 10.5 %collective-permute-done.30.refs_4_.refs_8_ = bf16[256,1024]{1,0:T(8,128)(2,1)S(1)} collective-permute-done((bf16[256,1024]{1,0:T(8,128)(2,1)S(1)}, bf16[256,1024]{1,0:T(8,128)(2,1)S(1)}, u32[]{:S(2)}, u32[]{:S(2)}) %collective-permute-start.30) | collective-permute-done | bytes 524320 | tf_op jit(solution)/shard_map/ppermute | solution.py:195
  168.9 15.8 %ffn_out.1 = (bf16[512,1024]{1,0:T(8,128)(2,1)}, f32[512,1024]{1,0:T(8,128)}, bf16[512,1024]{1,0:T(8,128)(2,1)}, f32[8,1024]{1,0:T(8,128)}, bf16[2048,1024]{1,0:T(8,128)(2,1)}) custom-call(s32[3]{0:T(128)} %pad_add_fusion.ids_ref, f32[16,1024]{1,0:T(8,128)} %get-tuple-element.109.vec_ref, bf16[512,4096]{1,0:T(8,128)(2,1)} %get-tuple-element.122.act_hbm.refs_0_, ...), custom_call_target="tpu_custom_call" | custom-call | flops 1 | bytes 5399999 | tf_op jit(solution)/shard_map/ffn_out/pallas_call | solution.py:373
  184.9 14.0 %ffn_back.1 = (bf16[512,4096]{1,0:T(8,128)(2,1)}, f32[8,4096]{1,0:T(8,128)}, bf16[512,4096]{1,0:T(8,128)(2,1)}) custom-call(s32[3]{0:T(128)} %pad_add_fusion.ids_ref, bf16[512,1024]{1,0:T(8,128)(2,1)} %get-tuple-element.135.grad_ref.refs_1_, f32[512,4096]{1,0:T(8,128)} %get-tuple-element.136.slope_ref, ...), custom_call_target="tpu_custom_call" | custom-call | flops 1 | bytes 3599999 | tf_op jit(solution)/shard_map/ffn_back/pallas_call | solution.py:373
  199.3 7.9 %rows_of_own_core.3 = (bf16[1024,512]{1,0:T(8,128)(2,1)}, bf16[1024,512]{1,0:T(8,128)(2,1)}, bf16[1024,512]{1,0:T(8,128)(2,1)}, bf16[1024,512]{1,0:T(8,128)(2,1)}) custom-call(s32[3]{0:T(128)} %pad_add_fusion.ids_ref, bf16[512,4096]{1,0:T(8,128)(2,1)} %get-tuple-element.122.act_hbm.refs_0_, bf16[512,1024]{1,0:T(8,128)(2,1)} %get-tuple-element.135.grad_ref.refs_1_, ...), custom_call_target="tpu_custom_call" | custom-call | flops 1 | bytes 2699999 | tf_op jit(solution)/shard_map/rows_of_own_core/pallas_call | solution.py:373
  210.2 15.7 %attention_norm_back.1 = (bf16[512,1024]{1,0:T(8,128)(2,1)}, f32[512,1024]{1,0:T(8,128)}, bf16[512,1024]{1,0:T(8,128)(2,1)}, f32[8,1024]{1,0:T(8,128)}) custom-call(s32[3]{0:T(128)} %pad_add_fusion.ids_ref, f32[512,128]{1,0:T(8,128)} %get-tuple-element.134.inverse_ref, f32[16,1024]{1,0:T(8,128)} %get-tuple-element.109.vec_ref, ...), custom_call_target="tpu_custom_call" | custom-call | flops 1 | bytes 4800000 | tf_op jit(solution)/shard_map/attention_norm_back/pallas_call | solution.py:373
  225.9 7.8 %rows_of_own_core.4 = (bf16[256,2048]{1,0:T(8,128)(2,1)}, bf16[256,2048]{1,0:T(8,128)(2,1)}, bf16[256,2048]{1,0:T(8,128)(2,1)}, bf16[256,2048]{1,0:T(8,128)(2,1)}) custom-call(s32[3]{0:T(128)} %pad_add_fusion.ids_ref, bf16[512,1024]{1,0:T(8,128)(2,1)} %get-tuple-element.114.x_ref.refs_0_.refs_1_.refs_2_.refs_3_, ...), custom_call_target="tpu_custom_call" | custom-call | flops 1 | bytes 2699999 | tf_op jit(solution)/shard_map/rows_of_own_core/pallas_call | solution.py:373
  236.2 17.0 %attend_backward.1 = (bf16[512,1024]{1,0:T(8,128)(2,1)}, bf16[512,1024]{1,0:T(8,128)(2,1)}, bf16[512,1024]{1,0:T(8,128)(2,1)}, f32[1,8,1024]{2,1,0:T(8,128)}, f32[1,8,1024]{2,1,0:T(8,128)}) custom-call(s32[1,1,512]{2,1,0:T(1,128)} %bitcast.38, bf16[512,1024]{1,0:T(8,128)(2,1)} %get-tuple-element.110.q_ref, bf16[512,1024]{1,0:T(8,128)(2,1)} %get-tuple-element.111.k_ref, ...), custom_call_target="tpu_custom_call" | custom-call | flops 1 | bytes 5100000 | tf_op jit(solution)/shard_map/attend_backward/pallas_call | solution.py:174
  253.2 4.5 %cross_near.1 = (bf16[512,1024]{1,0:T(8,128)(2,1)}, bf16[512,1024]{1,0:T(8,128)(2,1)}) custom-call(s32[3]{0:T(128)} %pad_add_fusion.ids_ref, bf16[1024,512]{1,0:T(8,128)(2,1)} %get-tuple-element.141.refs_20_.refs_0_, bf16[1024,512]{1,0:T(8,128)(2,1)} %copy-done.9, bf16[1024,512]{1,0:T(8,128)(2,1)} %get-tuple-element.152.refs_2_, ...), custom_call_target="tpu_custom_call" | custom-call | flops 1 | bytes 1799999 | tf_op jit(solution)/shard_map/cross_near/pallas_call | solution.py:373
  259.7 7.2 %rows_of_other_core.1.refs_4_ = bf16[512,4096]{1,0:T(8,128)(2,1)} custom-call(s32[3]{0:T(128)} %pad_add_fusion.ids_ref, bf16[512,1024]{1,0:T(8,128)(2,1)} %get-tuple-element.113.m_ref.refs_0_, bf16[512,1024]{1,0:T(8,128)(2,1)} %bitcast.28, bf16[512,1024]{1,0:T(8,128)(2,1)} %get-tuple-element.145.refs_3_.refs_2_, ...), custom_call_target="tpu_custom_call" | custom-call | flops 1 | bytes 2100000 | tf_op jit(solution)/shard_map/rows_of_other_core/pallas_call | solution.py:373
  268.4 4.0 %fold.2 = (bf16[128,2048]{1,0:T(8,128)(2,1)}, bf16[128,2048]{1,0:T(8,128)(2,1)}, bf16[128,2048]{1,0:T(8,128)(2,1)}, bf16[128,2048]{1,0:T(8,128)(2,1)}) custom-call(s32[3]{0:T(128)} %pad_add_fusion.ids_ref, bf16[256,2048]{1,0:T(8,128)(2,1)} %get-tuple-element.146.rest_0_.refs_0_, bf16[256,2048]{1,0:T(8,128)(2,1)} %copy-done.11, ...), custom_call_target="tpu_custom_call" | custom-call | flops 1 | bytes 1200000 | tf_op jit(solution)/shard_map/fold/pallas_call | solution.py:373
  274.4 8.2 %rows_of_own_core.5 = (bf16[256,2048]{1,0:T(8,128)(2,1)}, bf16[256,2048]{1,0:T(8,128)(2,1)}, bf16[256,2048]{1,0:T(8,128)(2,1)}, bf16[256,2048]{1,0:T(8,128)(2,1)}) custom-call(s32[3]{0:T(128)} %pad_add_fusion.ids_ref, bf16[512,1024]{1,0:T(8,128)(2,1)} %get-tuple-element.113.m_ref.refs_0_, bf16[512,1024]{1,0:T(8,128)(2,1)} %bitcast.29, ...), custom_call_target="tpu_custom_call" | custom-call | flops 1 | bytes 2699999 | tf_op jit(solution)/shard_map/rows_of_own_core/pallas_call | solution.py:373
  288.4 3.3 fold_z.1
  294.7 14.9 %collective-permute-done.43.refs_1_ = bf16[256,2048]{1,0:T(8,128)(2,1)S(1)} collective-permute-done((bf16[256,2048]{1,0:T(8,128)(2,1)}, bf16[256,2048]{1,0:T(8,128)(2,1)S(1)}, u32[]{:S(2)}, u32[]{:S(2)}) %collective-permute-start.43) | collective-permute-done | bytes 1048608 | tf_op jit(solution)/shard_map/ppermute | solution.py:195
  310.6 4.1 %fold.3 = (bf16[128,2048]{1,0:T(8,128)(2,1)}, bf16[128,2048]{1,0:T(8,128)(2,1)}, bf16[128,2048]{1,0:T(8,128)(2,1)}, bf16[128,2048]{1,0:T(8,128)(2,1)}) custom-call(s32[3]{0:T(128)} %pad_add_fusion.ids_ref, bf16[256,2048]{1,0:T(8,128)(2,1)} %get-tuple-element.158.refs_4_.refs_0_, bf16[256,2048]{1,0:T(8,128)(2,1)} %copy-done.18, ...), custom_call_target="tpu_custom_call" | custom-call | flops 1 | bytes 1200000 | tf_op jit(solution)/shard_map/fold/pallas_call | solution.py:373
  319.2 10.1 %inputs_back.1.refs_4_ = f32[512,1024]{1,0:T(8,128)} custom-call(s32[3]{0:T(128)} %pad_add_fusion.ids_ref, f32[512,1024]{1,0:T(8,128)} %get-tuple-element.142.base_ref, bf16[512,1024]{1,0:T(8,128)(2,1)} %get-tuple-element.149.refs_4_.refs_3_.q_ref, bf16[512,1024]{1,0:T(8,128)(2,1)} %get-tuple-element.150.refs_4_.k_ref, ...), custom_call_target="tpu_custom_call" | custom-call | flops 1 | bytes 3000000 | tf_op jit(solution)/shard_map/inputs_back/pallas_call | solution.py:373
  330.3 3.4 fold_direct.1
  344.0 4.6 %collective-permute-done.49 = bf16[32,4096]{1,0:T(8,128)(2,1)S(1)} collective-permute-done((bf16[32,4096]{1,0:T(8,128)(2,1)S(1)}, bf16[32,4096]{1,0:T(8,128)(2,1)S(1)}, u32[]{:S(2)}, u32[]{:S(2)}) %collective-permute-start.49) | collective-permute-done | bytes 262176 | tf_op jit(solution)/shard_map/ppermute | solution.py:195
  352.0 7.7 %collective-permute-done.50 = bf16[32,4096]{1,0:T(8,128)(2,1)S(1)} collective-permute-done((bf16[32,4096]{1,0:T(8,128)(2,1)S(1)}, bf16[32,4096]{1,0:T(8,128)(2,1)S(1)}, u32[]{:S(2)}, u32[]{:S(2)}) %collective-permute-start.50) | collective-permute-done | bytes 262176 | tf_op jit(solution)/shard_map/ppermute | solution.py:195
  (219 shorter events, 93.4 us)
Async XLA Ops:
  2.6 16.6 %collective-permute-start.1 = (bf16[32,4224]{1,0:T(8,128)(2,1)}, bf16[32,4224]{1,0:T(8,128)(2,1)S(1)}, u32[]{:S(2)}, u32[]{:S(2)}) collective-permute-start(bf16[32,4224]{1,0:T(8,128)(2,1)} %first_shard.1.refs_0_), channel_id=1, source_target_pairs={{0,2},{1,3},{2,0},{3,1},{4,6},{5,7},{6,4},{7,5},{8,10},{9,11},{10,... | collective-permute-start | bytes 811016 | tf_op jit(solution)/shard_map/ppermute | solution.py:195
  30.5 24.3 %collective-permute-start.4 = (bf16[128,4224]{1,0:T(8,128)(2,1)}, bf16[128,4224]{1,0:T(8,128)(2,1)S(1)}, u32[]{:S(2)}, u32[]{:S(2)}) collective-permute-start(bf16[128,4224]{1,0:T(8,128)(2,1)} %in_z_order.3.refs_0_), channel_id=1, source_target_pairs={{0,16},{1,17},{2,18},{3,19},{4,20},{5,21},{6,22},{7,23},{8,24},{9,... | collective-permute-start | bytes 3244040 | tf_op jit(solution)/shard_map/ppermute | solution.py:195
  31.8 24.4 %collective-permute-start.3 = (bf16[128,4224]{1,0:T(8,128)(2,1)}, bf16[128,4224]{1,0:T(8,128)(2,1)S(1)}, u32[]{:S(2)}, u32[]{:S(2)}) collective-permute-start(bf16[128,4224]{1,0:T(8,128)(2,1)} %in_z_order.3.refs_0_), channel_id=1, source_target_pairs={{0,8},{1,9},{2,10},{3,11},{4,12},{5,13},{6,14},{7,15},{8,0},{9,1},... | collective-permute-start | bytes 3244040 | tf_op jit(solution)/shard_map/ppermute | solution.py:195
  36.6 18.2 %collective-permute-start.5 = (bf16[32,4096]{1,0:T(8,128)(2,1)S(1)}, bf16[32,4096]{1,0:T(8,128)(2,1)S(1)}, u32[]{:S(2)}, u32[]{:S(2)}) collective-permute-start(bf16[32,4096]{1,0:T(8,128)(2,1)S(1)} %copy-done.25), channel_id=1, source_target_pairs={{0,1},{1,0},{2,3},{3,2},{4,5},{5,4},{6,7},{7,6},{8,9},{9,8},{10,11... | collective-permute-start | bytes 786440 | tf_op jit(solution)/shard_map/ppermute | solution.py:195
  48.3 27.2 %collective-permute-start.10 = (bf16[128,4224]{1,0:T(8,128)(2,1)}, bf16[128,4224]{1,0:T(8,128)(2,1)S(1)}, u32[]{:S(2)}, u32[]{:S(2)}) collective-permute-start(bf16[128,4224]{1,0:T(8,128)(2,1)} %in_z_order.3.refs_0_), channel_id=1, source_target_pairs={{0,4},{1,5},{2,6},{3,7},{4,0},{5,1},{6,2},{7,3},{8,12},{9,13},{10,... | collective-permute-start | bytes 3244040 | tf_op jit(solution)/shard_map/ppermute | solution.py:195
  54.8 20.8 %collective-permute-start.12 = (bf16[128,4224]{1,0:T(8,128)(2,1)S(1)}, bf16[128,4224]{1,0:T(8,128)(2,1)}, u32[]{:S(2)}, u32[]{:S(2)}) collective-permute-start(bf16[128,4224]{1,0:T(8,128)(2,1)S(1)} %collective-permute-done.4.refs_2_), channel_id=1, source_target_pairs={{0,4},{1,5},{2,6},{3,7},{4,0},{5,1},{6,2},{7,3},{8,12},{9,13},{10,... | collective-permute-start | bytes 3244040 | tf_op jit(solution)/shard_map/ppermute | solution.py:195
  56.3 14.8 %collective-permute-start.9 = (bf16[64,4224]{1,0:T(8,128)(2,1)S(1)}, bf16[64,4224]{1,0:T(8,128)(2,1)}, u32[]{:S(2)}, u32[]{:S(2)}) collective-permute-start(bf16[64,4224]{1,0:T(8,128)(2,1)S(1)} %slice.107), channel_id=1, source_target_pairs={{0,8},{1,9},{2,10},{3,11},{4,12},{5,13},{6,14},{7,15},{8,0},{9,1},... | collective-permute-start | bytes 1622024 | tf_op jit(solution)/shard_map/ppermute | solution.py:195
  57.8 17.7 %collective-permute-start.11 = (bf16[128,4224]{1,0:T(8,128)(2,1)S(1)}, bf16[128,4224]{1,0:T(8,128)(2,1)}, u32[]{:S(2)}, u32[]{:S(2)}) collective-permute-start(bf16[128,4224]{1,0:T(8,128)(2,1)S(1)} %collective-permute-done.3.refs_1_), channel_id=1, source_target_pairs={{0,4},{1,5},{2,6},{3,7},{4,0},{5,1},{6,2},{7,3},{8,12},{9,13},{10,... | collective-permute-start | bytes 3244040 | tf_op jit(solution)/shard_map/ppermute | solution.py:195
  75.6 28.9 %collective-permute-start.16 = (bf16[128,4096]{1,0:T(8,128)(2,1)}, bf16[128,4096]{1,0:T(8,128)(2,1)S(1)}, u32[]{:S(2)}, u32[]{:S(2)}) collective-permute-start(bf16[128,4096]{1,0:T(8,128)(2,1)} %in_z_order.4.refs_0_.refs_10_), channel_id=1, source_target_pairs={{0,16},{1,17},{2,18},{3,19},{4,20},{5,21},{6,22},{7,23},{8,24},{9,... | collective-permute-start | bytes 3145736 | tf_op jit(solution)/shard_map/ppermute | solution.py:195
  77.1 27.3 %collective-permute-start.15 = (bf16[128,4096]{1,0:T(8,128)(2,1)}, bf16[128,4096]{1,0:T(8,128)(2,1)S(1)}, u32[]{:S(2)}, u32[]{:S(2)}) collective-permute-start(bf16[128,4096]{1,0:T(8,128)(2,1)} %in_z_order.4.refs_0_.refs_10_), channel_id=1, source_target_pairs={{0,8},{1,9},{2,10},{3,11},{4,12},{5,13},{6,14},{7,15},{8,0},{9,1},... | collective-permute-start | bytes 3145736 | tf_op jit(solution)/shard_map/ppermute | solution.py:195
  77.7 47.7 %collective-permute-start.19 = (bf16[128,4096]{1,0:T(8,128)(2,1)}, bf16[128,4096]{1,0:T(8,128)(2,1)}, u32[]{:S(2)}, u32[]{:S(2)}) collective-permute-start(bf16[128,4096]{1,0:T(8,128)(2,1)} %in_z_order.4.refs_0_.refs_10_), channel_id=1, source_target_pairs={{0,4},{1,5},{2,6},{3,7},{4,0},{5,1},{6,2},{7,3},{8,12},{9,13},{10,... | collective-permute-start | bytes 3145736 | tf_op jit(solution)/shard_map/ppermute | solution.py:195
  87.3 20.8 %collective-permute-start.25 = (bf16[128,1024]{1,0:T(8,128)(2,1)S(1)}, bf16[128,1024]{1,0:T(8,128)(2,1)}, u32[]{:S(2)}, u32[]{:S(2)}) collective-permute-start(bf16[128,1024]{1,0:T(8,128)(2,1)S(1)} %copy-done.26), channel_id=1, source_target_pairs={{0,2},{1,3},{2,0},{3,1},{4,6},{5,7},{6,4},{7,5},{8,10},{9,11},{10,... | collective-permute-start | bytes 786440 | tf_op jit(solution)/shard_map/ppermute | solution.py:195
  104.5 19.2 %collective-permute-start.18 = (bf16[64,4096]{1,0:T(8,128)(2,1)S(1)}, bf16[64,4096]{1,0:T(8,128)(2,1)}, u32[]{:S(2)}, u32[]{:S(2)}) collective-permute-start(bf16[64,4096]{1,0:T(8,128)(2,1)S(1)} %slice.110), channel_id=1, source_target_pairs={{0,8},{1,9},{2,10},{3,11},{4,12},{5,13},{6,14},{7,15},{8,0},{9,1},... | collective-permute-start | bytes 1572872 | tf_op jit(solution)/shard_map/ppermute | solution.py:195
  106.1 17.7 %collective-permute-start.17 = (bf16[64,4096]{1,0:T(8,128)(2,1)S(1)}, bf16[64,4096]{1,0:T(8,128)(2,1)}, u32[]{:S(2)}, u32[]{:S(2)}) collective-permute-start(bf16[64,4096]{1,0:T(8,128)(2,1)S(1)} %slice.109), channel_id=1, source_target_pairs={{0,16},{1,17},{2,18},{3,19},{4,20},{5,21},{6,22},{7,23},{8,24},{9,... | collective-permute-start | bytes 1572872 | tf_op jit(solution)/shard_map/ppermute | solution.py:195
  123.8 25.7 %collective-permute-start.28 = (bf16[512,1024]{1,0:T(8,128)(2,1)}, bf16[512,1024]{1,0:T(8,128)(2,1)S(1)}, u32[]{:S(2)}, u32[]{:S(2)}) collective-permute-start(bf16[512,1024]{1,0:T(8,128)(2,1)} %in_z_order.5.refs_0_.refs_4_), channel_id=1, source_target_pairs={{0,16},{1,17},{2,18},{3,19},{4,20},{5,21},{6,22},{7,23},{8,24},{9,... | collective-permute-start | bytes 3145736 | tf_op jit(solution)/shard_map/ppermute | solution.py:195
  125.3 25.5 %collective-permute-start.27 = (bf16[512,1024]{1,0:T(8,128)(2,1)}, bf16[512,1024]{1,0:T(8,128)(2,1)}, u32[]{:S(2)}, u32[]{:S(2)}) collective-permute-start(bf16[512,1024]{1,0:T(8,128)(2,1)} %in_z_order.5.refs_0_.refs_4_), channel_id=1, source_target_pairs={{0,8},{1,9},{2,10},{3,11},{4,12},{5,13},{6,14},{7,15},{8,0},{9,1},... | collective-permute-start | bytes 3145736 | tf_op jit(solution)/shard_map/ppermute | solution.py:195
  130.0 35.6 %collective-permute-start.31 = (bf16[512,1024]{1,0:T(8,128)(2,1)}, bf16[512,1024]{1,0:T(8,128)(2,1)}, u32[]{:S(2)}, u32[]{:S(2)}) collective-permute-start(bf16[512,1024]{1,0:T(8,128)(2,1)} %in_z_order.5.refs_0_.refs_4_), channel_id=1, source_target_pairs={{0,4},{1,5},{2,6},{3,7},{4,0},{5,1},{6,2},{7,3},{8,12},{9,13},{10,... | collective-permute-start | bytes 3145736 | tf_op jit(solution)/shard_map/ppermute | solution.py:195
  198.9 27.0 %collective-permute-start.37 = (bf16[512,4096]{1,0:T(8,128)(2,1)}, bf16[512,4096]{1,0:T(8,128)(2,1)}, u32[]{:S(2)}, u32[]{:S(2)}) collective-permute-start(bf16[512,4096]{1,0:T(8,128)(2,1)} %get-tuple-element.140.refs_3_), channel_id=1, source_target_pairs={{0,4},{1,5},{2,6},{3,7},{4,0},{5,1},{6,2},{7,3},{8,12},{9,13},{10,... | collective-permute-start | bytes 12582920 | tf_op jit(solution)/shard_map/ppermute | solution.py:195
  207.2 27.7 %collective-permute-start.38 = (bf16[1024,512]{1,0:T(8,128)(2,1)}, bf16[1024,512]{1,0:T(8,128)(2,1)S(1)}, u32[]{:S(2)}, u32[]{:S(2)}) collective-permute-start(bf16[1024,512]{1,0:T(8,128)(2,1)} %get-tuple-element.147), channel_id=1, source_target_pairs={{0,8},{1,9},{2,10},{3,11},{4,12},{5,13},{6,14},{7,15},{8,0},{9,1},... | collective-permute-start | bytes 3145736 | tf_op jit(solution)/shard_map/ppermute | solution.py:195
  209.1 25.9 %collective-permute-start.39 = (bf16[1024,512]{1,0:T(8,128)(2,1)}, bf16[1024,512]{1,0:T(8,128)(2,1)S(1)}, u32[]{:S(2)}, u32[]{:S(2)}) collective-permute-start(bf16[1024,512]{1,0:T(8,128)(2,1)} %get-tuple-element.148), channel_id=1, source_target_pairs={{0,16},{1,17},{2,18},{3,19},{4,20},{5,21},{6,22},{7,23},{8,24},{9,... | collective-permute-start | bytes 3145736 | tf_op jit(solution)/shard_map/ppermute | solution.py:195
  233.7 24.9 %collective-permute-start.40 = (bf16[256,2048]{1,0:T(8,128)(2,1)}, bf16[256,2048]{1,0:T(8,128)(2,1)S(1)}, u32[]{:S(2)}, u32[]{:S(2)}) collective-permute-start(bf16[256,2048]{1,0:T(8,128)(2,1)} %get-tuple-element.154), channel_id=1, source_target_pairs={{0,8},{1,9},{2,10},{3,11},{4,12},{5,13},{6,14},{7,15},{8,0},{9,1},... | collective-permute-start | bytes 3145736 | tf_op jit(solution)/shard_map/ppermute | solution.py:195
  234.1 24.8 %collective-permute-start.41 = (bf16[256,2048]{1,0:T(8,128)(2,1)}, bf16[256,2048]{1,0:T(8,128)(2,1)}, u32[]{:S(2)}, u32[]{:S(2)}) collective-permute-start(bf16[256,2048]{1,0:T(8,128)(2,1)} %get-tuple-element.155), channel_id=1, source_target_pairs={{0,16},{1,17},{2,18},{3,19},{4,20},{5,21},{6,22},{7,23},{8,24},{9,... | collective-permute-start | bytes 3145736 | tf_op jit(solution)/shard_map/ppermute | solution.py:195
  266.9 25.8 %collective-permute-start.54 = (bf16[512,1024]{1,0:T(8,128)(2,1)}, bf16[512,1024]{1,0:T(8,128)(2,1)S(1)}, u32[]{:S(2)}, u32[]{:S(2)}) collective-permute-start(bf16[512,1024]{1,0:T(8,128)(2,1)} %get-tuple-element.184), channel_id=1, source_target_pairs={{0,1},{1,0},{2,3},{3,2},{4,5},{5,4},{6,7},{7,6},{8,9},{9,8},{10,11... | collective-permute-start | bytes 3145736 | tf_op jit(solution)/shard_map/ppermute | solution.py:195
  272.4 14.8 %collective-permute-start.45 = (bf16[128,2048]{1,0:T(8,128)(2,1)}, bf16[128,2048]{1,0:T(8,128)(2,1)}, u32[]{:S(2)}, u32[]{:S(2)}) collective-permute-start(bf16[128,2048]{1,0:T(8,128)(2,1)} %get-tuple-element.162), channel_id=1, source_target_pairs={{0,16},{1,17},{2,18},{3,19},{4,20},{5,21},{6,22},{7,23},{8,24},{9,... | collective-permute-start | bytes 1572872 | tf_op jit(solution)/shard_map/ppermute | solution.py:195
  273.3 15.1 %collective-permute-start.46 = (bf16[128,2048]{1,0:T(8,128)(2,1)}, bf16[128,2048]{1,0:T(8,128)(2,1)}, u32[]{:S(2)}, u32[]{:S(2)}) collective-permute-start(bf16[128,2048]{1,0:T(8,128)(2,1)} %get-tuple-element.164), channel_id=1, source_target_pairs={{0,8},{1,9},{2,10},{3,11},{4,12},{5,13},{6,14},{7,15},{8,0},{9,1},... | collective-permute-start | bytes 1572872 | tf_op jit(solution)/shard_map/ppermute | solution.py:195
  282.7 27.0 %collective-permute-start.43 = (bf16[256,2048]{1,0:T(8,128)(2,1)}, bf16[256,2048]{1,0:T(8,128)(2,1)S(1)}, u32[]{:S(2)}, u32[]{:S(2)}) collective-permute-start(bf16[256,2048]{1,0:T(8,128)(2,1)} %get-tuple-element.159), channel_id=1, source_target_pairs={{0,8},{1,9},{2,10},{3,11},{4,12},{5,13},{6,14},{7,15},{8,0},{9,1},... | collective-permute-start | bytes 3145736 | tf_op jit(solution)/shard_map/ppermute | solution.py:195
  283.6 26.1 %collective-permute-start.44 = (bf16[256,2048]{1,0:T(8,128)(2,1)}, bf16[256,2048]{1,0:T(8,128)(2,1)}, u32[]{:S(2)}, u32[]{:S(2)}) collective-permute-start(bf16[256,2048]{1,0:T(8,128)(2,1)} %get-tuple-element.161), channel_id=1, source_target_pairs={{0,16},{1,17},{2,18},{3,19},{4,20},{5,21},{6,22},{7,23},{8,24},{9,... | collective-permute-start | bytes 3145736 | tf_op jit(solution)/shard_map/ppermute | solution.py:195
  291.7 25.1 %collective-permute-start.52 = (bf16[64,4096]{1,0:T(8,128)(2,1)}, bf16[64,4096]{1,0:T(8,128)(2,1)}, u32[]{:S(2)}, u32[]{:S(2)}) collective-permute-start(bf16[64,4096]{1,0:T(8,128)(2,1)} %get-tuple-element.181), channel_id=1, source_target_pairs={{0,1},{1,0},{2,3},{3,2},{4,5},{5,4},{6,7},{7,6},{8,9},{9,8},{10,11... | collective-permute-start | bytes 1572872 | tf_op jit(solution)/shard_map/ppermute | solution.py:195
  294.0 39.7 %collective-permute-start.55 = (bf16[256,1024]{1,0:T(8,128)(2,1)}, bf16[256,1024]{1,0:T(8,128)(2,1)}, u32[]{:S(2)}, u32[]{:S(2)}) collective-permute-start(bf16[256,1024]{1,0:T(8,128)(2,1)} %get-tuple-element.188), channel_id=1, source_target_pairs={{0,2},{1,3},{2,0},{3,1},{4,6},{5,7},{6,4},{7,5},{8,10},{9,11},{10,... | collective-permute-start | bytes 1572872 | tf_op jit(solution)/shard_map/ppermute | solution.py:195
  318.0 22.3 %collective-permute-start.53 = (bf16[32,4096]{1,0:T(8,128)(2,1)S(1)}, bf16[32,4096]{1,0:T(8,128)(2,1)S(1)}, u32[]{:S(2)}, u32[]{:S(2)}) collective-permute-start(bf16[32,4096]{1,0:T(8,128)(2,1)S(1)} %slice.152), channel_id=1, source_target_pairs={{0,2},{1,3},{2,0},{3,1},{4,6},{5,7},{6,4},{7,5},{8,10},{9,11},{10,... | collective-permute-start | bytes 786440 | tf_op jit(solution)/shard_map/ppermute | solution.py:195
  338.4 21.4 %collective-permute-start.50 = (bf16[32,4096]{1,0:T(8,128)(2,1)S(1)}, bf16[32,4096]{1,0:T(8,128)(2,1)S(1)}, u32[]{:S(2)}, u32[]{:S(2)}) collective-permute-start(bf16[32,4096]{1,0:T(8,128)(2,1)S(1)} %copy-done.33), channel_id=1, source_target_pairs={{0,2},{1,3},{2,0},{3,1},{4,6},{5,7},{6,4},{7,5},{8,10},{9,11},{10,... | collective-permute-start | bytes 786440 | tf_op jit(solution)/shard_map/ppermute | solution.py:195
  340.2 19.5 %collective-permute-start.51 = (bf16[32,4096]{1,0:T(8,128)(2,1)S(1)}, bf16[32,4096]{1,0:T(8,128)(2,1)S(1)}, u32[]{:S(2)}, u32[]{:S(2)}) collective-permute-start(bf16[32,4096]{1,0:T(8,128)(2,1)S(1)} %copy-done.32), channel_id=1, source_target_pairs={{0,3},{1,2},{2,1},{3,0},{4,7},{5,6},{6,5},{7,4},{8,11},{9,10},{10,... | collective-permute-start | bytes 786440 | tf_op jit(solution)/shard_map/ppermute | solution.py:195
  (63 other events, 530.8 us)
